TPU v7x, 128 devices: a whole 4x4x4 slice. The times are simulated.
128 devices in a mesh: row: 8 (over z, y_lo), col: 16 (over y_hi, x, core).
Axes of the slice: x: 4, y: 4 (y_hi: 2, y_lo: 2; y = y_hi * 2 + y_lo), z: 4, core: 2. Of those that a mesh axis runs over, the one named last changes fastest.
Arguments:
- spectra: bfloat16 [2048, 256, 512], P(('row', 'col')), may hold values from 0.05 to 20000
- sensor_ids: int32 [2048, 1], P(('row', 'col')), may hold values from 0 to 255, as said below
- permutation: int32 [2048], P(('row', 'col')), may hold values from 0 to 2047, as said below
- w_enc1: bfloat16 [2048, 256], replicated, may hold values from -0.125 to 0.125
- w_enc2: bfloat16 [1024, 256], replicated, may hold values from -0.1875 to 0.1875
- w_dec1: bfloat16 [256, 1024], replicated, may hold values from -0.25 to 0.25
- w_dec2: bfloat16 [256, 2048], replicated, may hold values from -0.25 to 0.25
Outputs:
- grad_enc1: float32 [2048, 256], replicated
- grad_enc2: float32 [1024, 256], replicated
- grad_dec1: float32 [256, 1024], replicated
- grad_dec2: float32 [256, 2048], replicated
Inputs may be any that keep to these rules, and one draw needn't show every extreme that they name: `sensor_ids`: every sensor from 0 to 255 recorded exactly 8 windows. A permutation of all slots; the 16 windows of the ingest device with indices (a, b) go to 16 different trainers, one to each trainer whose col index c has c // 2 = a; each trainer thus receives one window from each ingest device of one row index.
All inputs are finite; a program needn't handle non-finite values.
Results may differ from a plain program's by a relative error of at most 0.004.
Values may be sent and summed in bfloat16 or wider, within the bound.
No kernel may reach another device: no remote copies, remote signals or barrier semaphores. Data moves between devices by JAX's collectives and lax.ppermute only.
A program may use at most 192 MiB of HBM per device.

v0:
```python
import jax
import jax.numpy as jnp
from jax import lax
from jax.sharding import PartitionSpec as P

WIN_SENSOR = 8


EPS = 1e-05


def frame_taps(values):
    windows, length, channels = values.shape
    padded = jnp.pad(values, ((0, 0), (1, 1), (0, 0)))
    paired = padded.reshape(windows, length // 2 + 1, 2 * channels)
    return jnp.concatenate([paired[:, :-1], paired[:, 1:]], axis=2)


def fold_taps(stacked):
    windows, length, columns = stacked.shape
    channels = columns // 4
    pieces = stacked.reshape(windows, length, 4, channels)
    blank = jnp.zeros((windows, 1, channels), stacked.dtype)
    even_rows = pieces[:, :, 1] + jnp.concatenate([blank, pieces[:, :-1, 3]], axis=1)
    odd_rows = pieces[:, :, 2] + jnp.concatenate([pieces[:, 1:, 0], blank], axis=1)
    return jnp.stack([even_rows, odd_rows], axis=2).reshape(windows, 2 * length, channels)


def silu_slope(values):
    logistic = jax.nn.sigmoid(values)
    return logistic * (1.0 + values * (1.0 - logistic))


def forward_dot(values, weight):
    flat = values.reshape(-1, values.shape[-1])
    result = jnp.dot(flat, weight, preferred_element_type=jnp.float32)
    return result.reshape(values.shape[:-1] + (weight.shape[1],))


def backward_dot(values, weight):
    flat = values.reshape(-1, values.shape[-1])
    result = lax.dot_general(
        flat, weight, (((1,), (1,)), ((), ())), preferred_element_type=jnp.float32
    )
    return result.reshape(values.shape[:-1] + (weight.shape[0],))


def sensor_table(sensor_col, sensor_total):
    return (sensor_col[:, None] == jnp.arange(sensor_total, dtype=jnp.int32)[None, :]).astype(
        jnp.float32
    )


def standardize(log_power, table, center, factor):
    shift = jnp.dot(table, center, precision=lax.Precision.HIGHEST)
    stretch = jnp.dot(table, factor, precision=lax.Precision.HIGHEST)
    return ((log_power - shift[:, None, :]) * stretch[:, None, :]).astype(jnp.bfloat16)


def layer_sum(left, right):
    left_flat = left.reshape(-1, left.shape[-1])
    right_flat = right.reshape(-1, right.shape[-1])
    gradient = jnp.einsum("rk,ro->ko", left_flat, right_flat, preferred_element_type=jnp.float32)
    return gradient


def local(spectra, sensor_ids, permutation, w_enc1, w_enc2, w_dec1, w_dec2):
    window_count = spectra.shape[0]
    frame_count = spectra.shape[1]
    row_count = lax.axis_size("row")
    col_count = lax.axis_size("col")
    total_windows = window_count * row_count * col_count
    sensor_total = total_windows // WIN_SENSOR
    sensor_col = sensor_ids[:, 0]
    table = sensor_table(sensor_col, sensor_total)
    log_power = jnp.log1p(spectra.astype(jnp.float32))
    win_sums = jnp.sum(log_power, axis=1)
    win_squares = jnp.sum(log_power * log_power, axis=1)
    totals = jnp.einsum("ws,wb->sb", table, win_sums, precision=lax.Precision.HIGHEST)
    squares = jnp.einsum("ws,wb->sb", table, win_squares, precision=lax.Precision.HIGHEST)
    counts = jnp.sum(table, axis=0) * frame_count
    totals, squares, counts = lax.psum((totals, squares, counts), ("row", "col"))
    center = totals / counts[:, None]
    factor = lax.rsqrt(squares / counts[:, None] - center * center + EPS)
    payload = standardize(log_power, table, center, factor)
    labels = jnp.stack([permutation, sensor_col], axis=1)
    positions = jnp.arange(window_count, dtype=jnp.int32)
    ranking = jnp.argsort(labels[:, 0] // col_count // col_count * col_count + positions)
    payload, labels = (
        lax.all_to_all(payload[ranking], "row", split_axis=0, concat_axis=0, tiled=True),
        lax.all_to_all(labels[ranking], "row", split_axis=0, concat_axis=0, tiled=True),
    )
    ranking = jnp.argsort(labels[:, 0] // col_count % col_count)
    payload, labels = (
        lax.all_to_all(payload[ranking], "col", split_axis=0, concat_axis=0, tiled=True),
        lax.all_to_all(labels[ranking], "col", split_axis=0, concat_axis=0, tiled=True),
    )
    stem_taps = frame_taps(payload)
    enc1_pre = forward_dot(stem_taps, w_enc1)
    middle = jnp.mean(enc1_pre, axis=(0, 1))
    variance = jnp.mean(jnp.square(enc1_pre - middle), axis=(0, 1))
    inverse = lax.rsqrt(variance + EPS)
    enc1_hat = (enc1_pre - middle) * inverse
    enc1_out = jax.nn.silu(enc1_hat).astype(jnp.bfloat16)
    mid_taps = frame_taps(enc1_out)
    enc2_pre = forward_dot(mid_taps, w_enc2)
    enc2_out = jax.nn.silu(enc2_pre).astype(jnp.bfloat16)
    dec1_pre = fold_taps(forward_dot(enc2_out, w_dec1))
    dec1_out = jax.nn.silu(dec1_pre).astype(jnp.bfloat16)
    rebuilt = fold_taps(forward_dot(dec1_out, w_dec2))
    delta_out = ((rebuilt - payload.astype(jnp.float32)) / total_windows).astype(jnp.bfloat16)
    out_taps = frame_taps(delta_out)
    grad_dec2 = layer_sum(dec1_out, out_taps)
    delta_dec1 = (backward_dot(out_taps, w_dec2) * silu_slope(dec1_pre)).astype(jnp.bfloat16)
    dec_taps = frame_taps(delta_dec1)
    grad_dec1 = layer_sum(enc2_out, dec_taps)
    delta_enc2 = (backward_dot(dec_taps, w_dec1) * silu_slope(enc2_pre)).astype(jnp.bfloat16)
    grad_enc2 = layer_sum(mid_taps, delta_enc2)
    back_enc1 = fold_taps(backward_dot(delta_enc2, w_enc2)) * silu_slope(enc1_hat)
    first_mean = jnp.mean(back_enc1, axis=(0, 1))
    second_mean = jnp.mean(back_enc1 * enc1_hat, axis=(0, 1))
    delta_enc1 = ((back_enc1 - first_mean - enc1_hat * second_mean) * inverse).astype(jnp.bfloat16)
    grad_enc1 = layer_sum(stem_taps, delta_enc1)
    grad_enc1, grad_enc2, grad_dec1, grad_dec2 = lax.psum(
        (grad_enc1, grad_enc2, grad_dec1, grad_dec2), ("row", "col")
    )
    return (grad_enc1, grad_enc2, grad_dec1, grad_dec2)


def solution(mesh):
    return jax.shard_map(
        local,
        mesh=mesh,
        in_specs=(
            P(("row", "col"), None, None),
            P(("row", "col"), None),
            P(("row", "col")),
            P(),
            P(),
            P(),
            P(),
        ),
        out_specs=(P(), P(), P(), P()),
        check_vma=False,
    )
```

profile of v0, /device:TPU:1, one launch (start us, length us, event | category | flops | bytes accessed | tf_op | source)
XLA Modules:
  0.0 608.6 jit_solution(8705638095930346824)
XLA Ops:
  7.2 5.9 fusion.2
  18.4 6.9 %all-to-all-start.1 = ((s32[8,2,2]{1,2,0:T(2,128)}), s32[8,2,2]{1,2,0:T(2,128)S(1)}, u32[]{:S(2)}, u32[]{:S(2)}) async-start(s32[8,2,2]{1,2,0:T(2,128)} %copy.99), calls=%async_computation.1 | async-start | bytes 16384 | tf_op jit(solution)/shard_map/all_to_all | solution.py:91
  25.4 67.2 %psum.50 = f32[256]{0:T(256)S(1)} all-reduce(f32[256]{0:T(256)S(1)} %broadcast_multiply_fusion.3), channel_id=1, replica_groups=mesh['row'=8,'col'=16] {'row','col'}, use_global_device_ids=true, to_apply=%region_3.0 | all-reduce | flops 256 | bytes 2048 | tf_op jit(solution)/shard_map/psum | solution.py:82
  92.6 74.5 %all-reduce.17.cloned.1.call-done = (f32[256,512]{1,0:T(8,128)}, f32[256,512]{1,0:T(8,128)}) async-done(((f32[256,512]{1,0:T(8,128)}, f32[256,512]{1,0:T(8,128)}), (f32[256,512]{1,0:T(8,128)}, f32[256,512]{1,0:T(8,128)})) %all-reduce.17.cloned.1.call-update) | async-done | bytes 1048592 | tf_op jit(solution)/shard_map/psum | solution.py:82
  170.4 5.4 multiply_convert_fusion
  175.8 4.9 gather_fusion
  180.7 4.6 all-to-all-start
  186.7 48.3 %all-to-all-done = bf16[16,256,512]{2,1,0:T(8,128)(2,1)} async-done(((bf16[16,256,512]{2,1,0:T(8,128)(2,1)}), bf16[16,256,512]{2,1,0:T(8,128)(2,1)}, u32[]{:S(2)}, u32[]{:S(2)}) %all-to-all-start) | async-done | bytes 4194336 | tf_op jit(solution)/shard_map/all_to_all | solution.py:90
  234.9 5.0 gather_fusion.2
  239.9 6.1 %all-to-all-start.2 = ((bf16[16,256,512]{2,1,0:T(8,128)(2,1)}), bf16[16,256,512]{2,1,0:T(8,128)(2,1)}, u32[]{:S(2)}, u32[]{:S(2)}) async-start(bf16[16,256,512]{2,1,0:T(8,128)(2,1)} %gather_fusion.2), calls=%async_computation.2 | async-start | bytes 8388608 | tf_op jit(solution)/shard_map/all_to_all | solution.py:95
  248.6 53.3 %all-to-all-done.2 = bf16[16,256,512]{2,1,0:T(8,128)(2,1)} async-done(((bf16[16,256,512]{2,1,0:T(8,128)(2,1)}), bf16[16,256,512]{2,1,0:T(8,128)(2,1)}, u32[]{:S(2)}, u32[]{:S(2)}) %all-to-all-start.2) | async-done | bytes 4194336 | tf_op jit(solution)/shard_map/all_to_all | solution.py:95
  301.9 5.9 pad.20
  307.9 7.2 %reshape.92 = bf16[16,129,1024]{2,1,0:T(8,128)(2,1)} reshape(bf16[16,258,512]{2,1,0:T(8,128)(2,1)} %pad.20) | data formatting | bytes 8454144 | tf_op jit(solution)/shard_map/reshape | solution.py:15
  315.1 4.4 fusion.66
  334.3 3.0 copy.113
  337.2 3.8 reshape.96
  341.1 3.6 fusion.24
  344.7 4.8 slice_bitcast_fusion.2
  349.5 3.4 copy-done.2
  352.9 11.7 %fusion.10 = (f32[16,128,1,512]{3,1,0,2:T(8,128)}, f32[16,128,1,512]{3,1,0,2:T(8,128)}) fusion(f32[16,128,4,512]{3,1,2,0:T(8,128)} %copy-done.2, f32[16,127,512]{2,1,0:T(8,128)} %get-tuple-element.20, f32[16,127,512]{2,1,0:T(8,128)} %get-tuple-element.21), kind=kLoop, calls=%fused_computation.24 | loop fusion | flops 2097152 | bytes 25100288 | tf_op jit(solution)/shard_map/stack | solution.py:26
  364.6 4.5 pad_maximum_fusion.1
  369.1 4.9 copy.111
  374.0 10.0 %fusion.1 = bf16[16,256,512]{2,1,0:T(8,128)(2,1)} fusion(f32[16,256,512]{2,0,1:T(8,128)S(1)} %bitcast.146, bf16[16,256,512]{2,1,0:T(8,128)(2,1)} %all-to-all-done.2), kind=kLoop, calls=%fused_computation.8 | loop fusion | flops 8388608 | bytes 16777216 | tf_op jit(solution)/shard_map/convert_element_type | solution.py:111
  384.0 5.9 pad.22
  389.9 7.2 %reshape.95 = bf16[16,129,1024]{2,1,0:T(8,128)(2,1)} reshape(bf16[16,258,512]{2,1,0:T(8,128)(2,1)} %pad.22) | data formatting | bytes 8454144 | tf_op jit(solution)/shard_map/reshape | solution.py:15
  397.1 4.7 fusion.65
  404.6 3.7 fusion.12
  420.2 3.0 copy.117
  423.1 3.6 reshape.98
  429.5 7.7 %fusion.11 = f32[2048,256]{1,0:T(8,128)} fusion(bf16[16,128,1024]{2,1,0:T(8,128)(2,1)} %copy-done.6, bf16[16,128,1024]{2,1,0:T(8,128)(2,1)} %copy-done.5, f32[16,128,256]{2,1,0:T(8,128)S(1)} %get-tuple-element.41, f32[256]{0:T(256)S(1)} %get-tuple-element.42, f32[256]{0:T(256)S(1)} %get-tuple-element.43, f32[256]{0:T(256)S(1)} %add_rsqrt_fusion, ...), kind=kOutput, calls=%fused_computation.25 | convolution fusion | flops 2172125184 | bytes 14684160 | tf_op jit(solution)/shard_map/rk,ro->ko/dot_general | solution.py:63
  437.2 157.9 %all-reduce.15.cloned.1.call-done = (f32[2048,256]{1,0:T(8,128)}, f32[1024,256]{1,0:T(8,128)}, f32[256,1024]{1,0:T(8,128)}, f32[256,2048]{1,0:T(8,128)}) async-done(((f32[2048,256]{1,0:T(8,128)}, f32[1024,256]{1,0:T(8,128)}, f32[256,1024]{1,0:T(8,128)}, f32[256,2048]{1,0:T(8,128)}), (f32[2048,256]{1,0:T(8,128)}, f32[1024,256]{1,0:T(8,128)}, f32[256,1024]{1,0:T(8,128)}, ...) | async-done | bytes 6291472 | tf_op jit(solution)/shard_map/psum | solution.py:124
  595.1 3.2 copy.153
  (108 shorter events, 47.8 us)
Async XLA Ops:
  7.2 312.4 %copy-start = (bf16[2048,256]{1,0:T(8,128)(2,1)S(1)}, bf16[2048,256]{1,0:T(8,128)(2,1)}, u32[]{:S(2)}) copy-start(bf16[2048,256]{1,0:T(8,128)(2,1)} %param.10) | copy-start | bytes 3145732
  7.2 5.9 copy-start.21
  7.2 8.5 %copy-start.22 = (s32[16]{0:T(128)S(1)}, s32[16]{0:T(128)}, u32[]{:S(2)}) copy-start(s32[16]{0:T(128)} %param.9) | copy-start | bytes 196
  7.2 159.9 %all-reduce.17.cloned.1.call-start = ((), (), s32[]{:S(2)}) async-start(), calls=%async_computation.4 | async-start | bytes 2097152 | tf_op jit(solution)/shard_map/psum | solution.py:82
  18.4 162.3 %all-to-all-start.1 = ((s32[8,2,2]{1,2,0:T(2,128)}), s32[8,2,2]{1,2,0:T(2,128)S(1)}, u32[]{:S(2)}, u32[]{:S(2)}) async-start(s32[8,2,2]{1,2,0:T(2,128)} %copy.99), calls=%async_computation.1 | async-start | bytes 16384 | tf_op jit(solution)/shard_map/all_to_all | solution.py:91
  167.1 3.2 copy-start.3
  180.7 54.2 %all-to-all-start = ((bf16[16,256,512]{2,1,0:T(8,128)(2,1)}), bf16[16,256,512]{2,1,0:T(8,128)(2,1)}, u32[]{:S(2)}, u32[]{:S(2)}) async-start(bf16[16,256,512]{2,1,0:T(8,128)(2,1)} %gather_fusion), calls=%async_computation | async-start | bytes 8388608 | tf_op jit(solution)/shard_map/all_to_all | solution.py:90
  239.9 6.4 %copy-start.18 = (bf16[256,1024]{1,0:T(8,128)(2,1)S(1)}, bf16[256,1024]{1,0:T(8,128)(2,1)}, u32[]{:S(2)}) copy-start(bf16[256,1024]{1,0:T(8,128)(2,1)} %param.12) | copy-start | bytes 1572868
  239.9 7.4 %copy-start.9 = (bf16[256,2048]{1,0:T(8,128)(2,1)S(1)}, bf16[256,2048]{1,0:T(8,128)(2,1)}, u32[]{:S(2)}) copy-start(bf16[256,2048]{1,0:T(8,128)(2,1)} %param.13) | copy-start | bytes 3145732
  239.9 62.0 %all-to-all-start.2 = ((bf16[16,256,512]{2,1,0:T(8,128)(2,1)}), bf16[16,256,512]{2,1,0:T(8,128)(2,1)}, u32[]{:S(2)}, u32[]{:S(2)}) async-start(bf16[16,256,512]{2,1,0:T(8,128)(2,1)} %gather_fusion.2), calls=%async_computation.2 | async-start | bytes 8388608 | tf_op jit(solution)/shard_map/all_to_all | solution.py:95
  246.0 349.1 %all-reduce.15.cloned.1.call-start = ((), (), s32[]{:S(2)}) async-start(), calls=%async_computation.3 | async-start | bytes 12582912 | tf_op jit(solution)/shard_map/psum | solution.py:124
  319.5 2.6 copy-start.5
  319.5 3.2 copy-start.6
  327.4 4.3 copy-start.20
  329.5 3.0 copy-start.13
  329.5 3.0 copy-start.15
  331.7 1.0 copy-start.23
  344.7 8.2 %copy-start.2 = (f32[16,128,4,512]{3,1,2,0:T(8,128)}, f32[16,128,4,512]{3,1,2,0:T(8,128)S(1)}, u32[]{:S(2)}) copy-start(f32[16,128,4,512]{3,1,2,0:T(8,128)S(1)} %fusion.24) | copy-start | bytes 50331652
  397.1 4.7 copy-start.7
  397.1 4.7 copy-start.10
  409.7 4.6 copy-start.19
  412.2 2.2 copy-start.24
  415.2 1.8 copy-start.14
  415.2 1.8 copy-start.16
  416.9 1.7 copy-start.17
  426.8 2.7 copy-start.4
  595.1 3.2 copy-start.12
  595.1 4.2 copy-start.11
  595.1 5.2 copy-start.8
  595.1 6.5 %copy-start.1 = (bf16[2048,256]{1,0:T(8,128)(2,1)S(1)}, bf16[2048,256]{1,0:T(8,128)(2,1)}, u32[]{:S(2)}) copy-start(bf16[2048,256]{1,0:T(8,128)(2,1)} %param.10) | copy-start | bytes 3145732
Sparse Core Ops, SparseCore 0:
  15.9 151.2 all-reduce.16
  437.3 157.7 all-reduce.14
where the time goes:
time: 618 us; the launch traced here: 609 us
  waiting for transfers between devices  334 us (54%)
  local copies, waits for them, and re-layouts  95.4 us (15%)
  blocking collectives  67.2 us (11%)
  other arithmetic  45.3 us (7%)
  matrix products  34.1 us (6%)
  starting transfers between devices  17.8 us (3%)
  between operations  14.7 us (2%)
    psum x1, waiting for transfers between devices, local(): lax.psum((grad_enc1, grad_enc2, grad_dec1, grad_dec2), ('row', 'col'))  158 us
    psum x1, waiting for transfers between devices, local(): lax.psum((totals, squares, counts), ('row', 'col'))  74.5 us
    psum x1, blocking collectives, local(): lax.psum((totals, squares, counts), ('row', 'col'))  67.2 us
    all_to_all x1, waiting for transfers between devices, local(): lax.all_to_all(payload[ranking], 'col', split_axis=0, concat_axis=0, tile...  53.3 us
    all_to_all x1, waiting for transfers between devices, local(): lax.all_to_all(payload[ranking], 'row', split_axis=0, concat_axis=0, tile...  48.3 us
    reshape x4, local copies, waits for them, and re-layouts, frame_taps(): paired = padded.reshape(windows, length // 2 + 1, 2 * channels)  19.1 us
    another operation x5, other arithmetic, fold_taps(): jnp.stack([even_rows, odd_rows], axis=2)  17 us
    dot_general x4, matrix products, layer_sum(): jnp.einsum('rk,ro->ko', left_flat, right_flat, preferred_element_type=jnp...  14.9 us
  transfers between devices with their start and end apart: 5, of which 4 were waited for; matrix products, arithmetic and copies ran while one was open for 3% of the time, Pallas kernels for 0%

commit v1 on v0

v1 whole, which is shorter than its diff:
```python
import functools

import jax
import jax.numpy as jnp
from jax import lax
from jax.experimental import pallas as pl
from jax.experimental.pallas import tpu as pltpu
from jax.sharding import PartitionSpec as P

WIN_SENSOR = 8
EPS = 1e-05
F32 = jnp.float32
BF16 = jnp.bfloat16
LANES = 128
STEP_WINDOWS = 4
VMEM_LIMIT = 56 * 1024 * 1024


def dot(left, right):
    return jnp.dot(left, right, preferred_element_type=F32)


def dot_nt(left, right):
    return lax.dot_general(left, right, (((1,), (1,)), ((), ())), preferred_element_type=F32)


def dot_tn(left, right):
    return lax.dot_general(left, right, (((0,), (0,)), ((), ())), preferred_element_type=F32)


def split3(values):
    first = values.astype(BF16)
    rest = values - first.astype(F32)
    second = rest.astype(BF16)
    third = (rest - second.astype(F32)).astype(BF16)
    return first, second, third


def sigmoid(values):
    return 1.0 / (1.0 + jnp.exp(-values))


def shift_down(values, period):
    rows = lax.broadcasted_iota(jnp.int32, values.shape, 0) % period
    return jnp.where(rows == 0, 0.0, pltpu.roll(values, 1, 0))


def shift_up(values, period):
    total = values.shape[0]
    rows = lax.broadcasted_iota(jnp.int32, values.shape, 0) % period
    return jnp.where(rows == period - 1, 0.0, pltpu.roll(values, total - 1, 0))


def group_rank(perm_ref, window, window_dev, col_count):
    trainer = perm_ref[window] // window_dev
    per_row = 2
    return (trainer // col_count) * per_row + trainer % per_row


def sums_kernel(spec_ref, ids_ref, out_ref, acc, *, chunks):
    step = pl.program_id(0)
    windows, frames, bins = spec_ref.shape
    rows = 16

    for w in range(windows):
        def body(i, carry):
            total, square = carry
            start = pl.multiple_of(i * rows, rows)
            value = jnp.log(1.0 + spec_ref[w, pl.ds(start, rows), :].astype(F32))
            value_sq = value * value
            return (total + value[0:8] + value[8:16], square + value_sq[0:8] + value_sq[8:16])

        zero = jnp.zeros((8, bins), F32)
        total, square = lax.fori_loop(0, frames // rows, body, (zero, zero), unroll=4)
        total = jnp.sum(total, axis=0, keepdims=True)
        square = jnp.sum(square, axis=0, keepdims=True)
        pieces = [total[:, k * LANES:(k + 1) * LANES] for k in range(chunks)]
        pieces += [square[:, k * LANES:(k + 1) * LANES] for k in range(chunks)]
        start = pl.multiple_of((step * windows + w) * 2 * chunks, 2 * chunks)
        acc[pl.ds(start, 2 * chunks), :] = jnp.concatenate(pieces, axis=0)

    @pl.when(step == pl.num_programs(0) - 1)
    def _():
        count = ids_ref.shape[0]
        acc[LANES:2 * LANES, :] = jnp.zeros((LANES, LANES), F32)
        acc[LANES:LANES + count, :] = jnp.broadcast_to(ids_ref[...].astype(F32), (count, LANES))
        out_ref[:, 0:LANES] = acc[0:LANES, :].T
        out_ref[:, LANES:2 * LANES] = acc[LANES:2 * LANES, :].T


def sums_call(spectra, sensor_ids):
    windows, frames, bins = spectra.shape
    chunks = bins // LANES
    return pl.pallas_call(
        functools.partial(sums_kernel, chunks=chunks),
        grid=(windows // STEP_WINDOWS,),
        in_specs=[
            pl.BlockSpec((STEP_WINDOWS, frames, bins), lambda i: (i, 0, 0)),
            pl.BlockSpec(sensor_ids.shape, lambda i: (0, 0)),
        ],
        out_specs=pl.BlockSpec((LANES, 2 * LANES), lambda i: (0, 0)),
        out_shape=jax.ShapeDtypeStruct((LANES, 2 * LANES), F32),
        scratch_shapes=[pltpu.VMEM((2 * LANES, LANES), F32)],
        compiler_params=pltpu.CompilerParams(vmem_limit_bytes=VMEM_LIMIT),
        name="window_sums",
    )(spectra, sensor_ids)


def stats_kernel(in_ref, out_ref, *, windows, chunks, sensors, per_sensor):
    width = 2 * chunks
    data = in_ref[:, 0:LANES].T
    labels = in_ref[:, LANES:2 * LANES].T
    sensor_rows = lax.broadcasted_iota(jnp.int32, (sensors, LANES), 0).astype(F32)
    tables = [(sensor_rows == labels[w:w + 1, :]).astype(F32).astype(BF16) for w in range(windows)]
    table = jnp.concatenate(tables, axis=1)
    values = jnp.concatenate([data[w * width:(w + 1) * width, :] for w in range(windows)], axis=1)
    parts = dot_nt(jnp.concatenate(split3(values), axis=0), table)
    sums = parts[0:width] + parts[width:2 * width] + parts[2 * width:3 * width]
    center = sums[0:chunks] / per_sensor
    factor = lax.rsqrt(sums[chunks:width] / per_sensor - center * center + EPS)
    both = jnp.concatenate([center, factor], axis=0)
    back = dot(jnp.concatenate(split3(both), axis=0), table)
    back = back[0:width] + back[width:2 * width] + back[2 * width:3 * width]
    rows = jnp.concatenate([back[:, w * LANES:(w + 1) * LANES] for w in range(windows)], axis=0)
    out_ref[...] = rows.T


def stats_call(received, windows, chunks, sensors, per_sensor):
    return pl.pallas_call(
        functools.partial(stats_kernel, windows=windows, chunks=chunks, sensors=sensors, per_sensor=float(per_sensor)),
        out_shape=jax.ShapeDtypeStruct((LANES, LANES), F32),
        compiler_params=pltpu.CompilerParams(vmem_limit_bytes=VMEM_LIMIT),
        name="sensor_stats",
    )(received)


def enc1_kernel(perm_ref, spec_ref, coef_ref, w_ref, normed_ref, pre_ref, stat_ref, coef, lane, stat, *, chunks, cols, copies):
    step = pl.program_id(0)
    windows, frames, bins = spec_ref.shape
    quarter = frames // 4
    channels = w_ref.shape[1]
    all_windows = windows * pl.num_programs(0)
    width = 2 * chunks

    @pl.when(step == 0)
    def _():
        coef[...] = coef_ref[...].T

    rows = 32
    for w in range(windows):
        start = pl.multiple_of((step * windows + w) * width, width)
        both = coef[pl.ds(start, width), :]

        def body(i, carry):
            at = pl.multiple_of(i * rows, rows)
            value = jnp.log(1.0 + spec_ref[w, pl.ds(at, rows), :].astype(F32))
            for k in range(chunks):
                part = value[:, k * LANES:(k + 1) * LANES]
                lane[w % 2, k, pl.ds(at, rows), :] = (part - both[k:k + 1, :]) * both[chunks + k:chunks + k + 1, :]
            return carry

        lax.fori_loop(0, frames // rows, body, 0, unroll=2)
        for i in range(4):
            for k in range(chunks):
                picked = lane[w % 2, k, pl.ds(i, quarter, stride=4), :]
                normed_ref[i, w * quarter:(w + 1) * quarter, k * LANES:(k + 1) * LANES] = picked.astype(BF16)

    w0, w1, w2, w3 = (w_ref[k * bins:(k + 1) * bins, :] for k in range(4))
    f0, f1, f2, f3 = (normed_ref[i] for i in range(4))
    even = shift_down(dot(f3, w0), quarter) + dot(f0, w1) + dot(f1, w2) + dot(f2, w3)
    odd = dot(f1, w0) + dot(f2, w1) + dot(f3, w2) + shift_up(dot(f0, w3), quarter)
    pre_ref[0] = even
    pre_ref[1] = odd
    for w in range(windows):
        part_e = even[w * quarter:(w + 1) * quarter]
        part_o = odd[w * quarter:(w + 1) * quarter]
        mean = (jnp.sum(part_e, axis=0, keepdims=True) + jnp.sum(part_o, axis=0, keepdims=True)) / (2 * quarter)
        diff_e = part_e - mean
        diff_o = part_o - mean
        spread = (jnp.sum(diff_e * diff_e, axis=0, keepdims=True) + jnp.sum(diff_o * diff_o, axis=0, keepdims=True)) / (2 * quarter)
        place = group_rank(perm_ref, step * windows + w, all_windows, cols)
        stat[pl.ds(place, 1), 0:channels] = mean
        stat[pl.ds(place, 1), channels:2 * channels] = spread

    @pl.when(step == pl.num_programs(0) - 1)
    def _():
        for d in range(copies):
            stat_ref[d] = stat[...]


def enc1_call(permutation, spectra, coef, w_enc1, cols):
    windows, frames, bins = spectra.shape
    chunks = bins // LANES
    quarter = frames // 4
    channels = w_enc1.shape[1]
    rows = STEP_WINDOWS * quarter
    grid_spec = pltpu.PrefetchScalarGridSpec(
        num_scalar_prefetch=1,
        grid=(windows // STEP_WINDOWS,),
        in_specs=[
            pl.BlockSpec((STEP_WINDOWS, frames, bins), lambda i, p: (i, 0, 0)),
            pl.BlockSpec((LANES, LANES), lambda i, p: (0, 0)),
            pl.BlockSpec(w_enc1.shape, lambda i, p: (0, 0)),
        ],
        out_specs=[
            pl.BlockSpec((4, rows, bins), lambda i, p: (0, i, 0)),
            pl.BlockSpec((2, rows, channels), lambda i, p: (0, i, 0)),
            pl.BlockSpec((cols, windows, 2 * channels), lambda i, p: (0, 0, 0)),
        ],
        scratch_shapes=[
            pltpu.VMEM((LANES, LANES), F32),
            pltpu.VMEM((2, chunks, frames, LANES), F32),
            pltpu.VMEM((windows, 2 * channels), F32),
        ],
    )
    return pl.pallas_call(
        functools.partial(enc1_kernel, chunks=chunks, cols=cols, copies=cols),
        grid_spec=grid_spec,
        out_shape=[
            jax.ShapeDtypeStruct((4, windows * quarter, bins), BF16),
            jax.ShapeDtypeStruct((2, windows * quarter, channels), F32),
            jax.ShapeDtypeStruct((cols, windows, 2 * channels), F32),
        ],
        compiler_params=pltpu.CompilerParams(vmem_limit_bytes=VMEM_LIMIT),
        name="normalize_enc1",
    )(permutation, spectra, coef, w_enc1)


def window_rows(perm_ref, table, step, windows, quarter, all_windows, cols, first, last):
    parts = []
    for w in range(windows):
        place = group_rank(perm_ref, step * windows + w, all_windows, cols)
        parts.append(jnp.broadcast_to(table[pl.ds(place, 1), first:last], (quarter, last - first)))
    return jnp.concatenate(parts, axis=0)


def middle_kernel(perm_ref, normed_ref, pre_ref, stat_ref, v_ref, b_ref, c_ref,
                  grad_c_ref, grad_b_ref, grad_v_ref, back_ref, moment_ref, sums_ref,
                  moment, sums, *, quarter, cols, total_windows):
    step = pl.program_id(0)
    channels = v_ref.shape[1]
    bins = normed_ref.shape[2]
    rows = normed_ref.shape[1]
    windows = rows // quarter
    all_windows = windows * pl.num_programs(0)
    ch = channels

    @pl.when(step == 0)
    def _():
        means = stat_ref[:, :, 0:ch]
        mean = jnp.mean(means, axis=0)
        diff = means - mean[None]
        variance = jnp.mean(stat_ref[:, :, ch:2 * ch] + diff * diff, axis=0)
        moment[:, 0:ch] = mean
        moment[:, ch:2 * ch] = lax.rsqrt(variance + EPS)
        moment_ref[...] = moment[...]
        grad_c_ref[...] = jnp.zeros_like(grad_c_ref)
        grad_b_ref[...] = jnp.zeros_like(grad_b_ref)
        grad_v_ref[...] = jnp.zeros_like(grad_v_ref)

    mean = window_rows(perm_ref, moment, step, windows, quarter, all_windows, cols, 0, ch)
    inverse = window_rows(perm_ref, moment, step, windows, quarter, all_windows, cols, ch, 2 * ch)
    hat_e = (pre_ref[0] - mean) * inverse
    hat_o = (pre_ref[1] - mean) * inverse
    a_e = (hat_e * sigmoid(hat_e)).astype(BF16)
    a_o = (hat_o * sigmoid(hat_o)).astype(BF16)
    v0, v1, v2, v3 = (v_ref[k * ch:(k + 1) * ch, :] for k in range(4))
    pre2 = shift_down(dot(a_o, v0), quarter) + dot(a_e, v1) + dot(a_o, v2) + shift_up(dot(a_e, v3), quarter)
    gate2 = sigmoid(pre2)
    h32 = (pre2 * gate2).astype(BF16).astype(F32)
    h = h32.astype(BF16)
    b0, b1, b2, b3 = (b_ref[:, k * ch:(k + 1) * ch] for k in range(4))
    d1_e = dot(h, b1) + shift_down(dot(h, b3), quarter)
    d1_o = dot(h, b2) + shift_up(dot(h, b0), quarter)
    gate_e = sigmoid(d1_e)
    gate_o = sigmoid(d1_o)
    de32 = (d1_e * gate_e)
    do32 = (d1_o * gate_o)
    de = de32.astype(BF16)
    do = do32.astype(BF16)
    de_up = shift_up(de32, quarter).astype(BF16)
    do_down = shift_down(do32, quarter).astype(BF16)
    c0, c1, c2, c3 = (c_ref[:, k * bins:(k + 1) * bins] for k in range(4))

    def delta(rebuilt, i):
        return ((rebuilt - normed_ref[i].astype(F32)) / total_windows).astype(BF16)

    g0 = delta(dot(de, c1) + dot(do_down, c3), 0)
    g1 = delta(dot(de, c2) + dot(do, c0), 1)
    g2 = delta(dot(do, c1) + dot(de, c3), 2)
    g3 = delta(dot(do, c2) + dot(de_up, c0), 3)
    halves = bins // ch

    def add_c(k, value):
        for j in range(halves):
            at = (k * halves + j) * ch
            grad_c_ref[at:at + ch, :] += value[:, j * ch:(j + 1) * ch]

    add_c(0, dot_tn(de_up, g3) + dot_tn(do, g1))
    add_c(1, dot_tn(de, g0) + dot_tn(do, g2))
    add_c(2, dot_tn(de, g1) + dot_tn(do, g3))
    add_c(3, dot_tn(de, g2) + dot_tn(do_down, g0))
    back_e = shift_down(dot_nt(g3, c0), quarter) + dot_nt(g0, c1) + dot_nt(g1, c2) + dot_nt(g2, c3)
    back_o = dot_nt(g1, c0) + dot_nt(g2, c1) + dot_nt(g3, c2) + shift_up(dot_nt(g0, c3), quarter)
    dd_e = (back_e * (gate_e * (1.0 + d1_e * (1.0 - gate_e)))).astype(BF16)
    dd_o = (back_o * (gate_o * (1.0 + d1_o * (1.0 - gate_o)))).astype(BF16)
    h_up = shift_up(h32, quarter).astype(BF16)
    h_down = shift_down(h32, quarter).astype(BF16)
    grad_b_ref[0:ch, :] += dot_tn(h_up, dd_o)
    grad_b_ref[ch:2 * ch, :] += dot_tn(h, dd_e)
    grad_b_ref[2 * ch:3 * ch, :] += dot_tn(h, dd_o)
    grad_b_ref[3 * ch:4 * ch, :] += dot_tn(h_down, dd_e)
    back2 = shift_down(dot_nt(dd_o, b0), quarter) + dot_nt(dd_e, b1) + dot_nt(dd_o, b2) + shift_up(dot_nt(dd_e, b3), quarter)
    d2_32 = (back2 * (gate2 * (1.0 + pre2 * (1.0 - gate2)))).astype(BF16).astype(F32)
    d2 = d2_32.astype(BF16)
    d2_up = shift_up(d2_32, quarter).astype(BF16)
    d2_down = shift_down(d2_32, quarter).astype(BF16)
    grad_v_ref[0:ch, :] += dot_tn(a_o, d2_up)
    grad_v_ref[ch:2 * ch, :] += dot_tn(a_e, d2)
    grad_v_ref[2 * ch:3 * ch, :] += dot_tn(a_o, d2)
    grad_v_ref[3 * ch:4 * ch, :] += dot_tn(a_e, d2_down)
    fold_e = dot_nt(d2, v1) + shift_down(dot_nt(d2, v3), quarter)
    fold_o = dot_nt(d2, v2) + shift_up(dot_nt(d2, v0), quarter)
    gate_he = sigmoid(hat_e)
    gate_ho = sigmoid(hat_o)
    fold_e = fold_e * (gate_he * (1.0 + hat_e * (1.0 - gate_he)))
    fold_o = fold_o * (gate_ho * (1.0 + hat_o * (1.0 - gate_ho)))
    back_ref[0] = fold_e
    back_ref[1] = fold_o
    cross_e = fold_e * hat_e
    cross_o = fold_o * hat_o
    for w in range(windows):
        low, high = w * quarter, (w + 1) * quarter
        first = jnp.sum(fold_e[low:high] + fold_o[low:high], axis=0, keepdims=True)
        second = jnp.sum(cross_e[low:high] + cross_o[low:high], axis=0, keepdims=True)
        place = group_rank(perm_ref, step * windows + w, all_windows, cols)
        sums[pl.ds(place, 1), 0:ch] = first
        sums[pl.ds(place, 1), ch:2 * ch] = second

    @pl.when(step == pl.num_programs(0) - 1)
    def _():
        for d in range(cols):
            sums_ref[d] = sums[...]


def middle_call(permutation, normed, pre, stat, w_enc2, w_dec1, w_dec2, quarter, cols, total_windows):
    bins = normed.shape[2]
    channels = w_enc2.shape[1]
    windows = normed.shape[1] // quarter
    rows = STEP_WINDOWS * quarter
    whole2 = lambda i, p: (0, 0)
    whole3 = lambda i, p: (0, 0, 0)
    grid_spec = pltpu.PrefetchScalarGridSpec(
        num_scalar_prefetch=1,
        grid=(windows // STEP_WINDOWS,),
        in_specs=[
            pl.BlockSpec((4, rows, bins), lambda i, p: (0, i, 0)),
            pl.BlockSpec((2, rows, channels), lambda i, p: (0, i, 0)),
            pl.BlockSpec(stat.shape, whole3),
            pl.BlockSpec(w_enc2.shape, whole2),
            pl.BlockSpec(w_dec1.shape, whole2),
            pl.BlockSpec(w_dec2.shape, whole2),
        ],
        out_specs=[
            pl.BlockSpec((4 * bins, channels), whole2),
            pl.BlockSpec((4 * channels, channels), whole2),
            pl.BlockSpec((4 * channels, channels), whole2),
            pl.BlockSpec((2, rows, channels), lambda i, p: (0, i, 0)),
            pl.BlockSpec((windows, 2 * channels), whole2),
            pl.BlockSpec(stat.shape, whole3),
        ],
        scratch_shapes=[
            pltpu.VMEM((windows, 2 * channels), F32),
            pltpu.VMEM((windows, 2 * channels), F32),
        ],
    )
    return pl.pallas_call(
        functools.partial(middle_kernel, quarter=quarter, cols=cols, total_windows=float(total_windows)),
        grid_spec=grid_spec,
        out_shape=[
            jax.ShapeDtypeStruct((4 * bins, channels), F32),
            jax.ShapeDtypeStruct((4 * channels, channels), F32),
            jax.ShapeDtypeStruct((4 * channels, channels), F32),
            jax.ShapeDtypeStruct(pre.shape, F32),
            jax.ShapeDtypeStruct((windows, 2 * channels), F32),
            jax.ShapeDtypeStruct(stat.shape, F32),
        ],
        compiler_params=pltpu.CompilerParams(vmem_limit_bytes=VMEM_LIMIT),
        name="middle",
    )(permutation, normed, pre, stat, w_enc2, w_dec1, w_dec2)


def grad_kernel(perm_ref, normed_ref, pre_ref, back_ref, moment_ref, sums_ref, grad_ref, scale, *, quarter, cols):
    step = pl.program_id(0)
    bins = normed_ref.shape[2]
    rows = normed_ref.shape[1]
    ch = pre_ref.shape[2]
    windows = rows // quarter
    all_windows = windows * pl.num_programs(0)

    @pl.when(step == 0)
    def _():
        scale[...] = jnp.sum(sums_ref[...], axis=0) / (2.0 * quarter * cols)
        grad_ref[...] = jnp.zeros_like(grad_ref)

    pick = functools.partial(window_rows, perm_ref, step=step, windows=windows, quarter=quarter, all_windows=all_windows, cols=cols)
    mean = pick(table=moment_ref, first=0, last=ch)
    inverse = pick(table=moment_ref, first=ch, last=2 * ch)
    first = pick(table=scale, first=0, last=ch)
    second = pick(table=scale, first=ch, last=2 * ch)
    hat_e = (pre_ref[0] - mean) * inverse
    hat_o = (pre_ref[1] - mean) * inverse
    de32 = (back_ref[0] - first - hat_e * second) * inverse
    do32 = (back_ref[1] - first - hat_o * second) * inverse
    de = de32.astype(BF16)
    do = do32.astype(BF16)
    de_up = shift_up(de32, quarter).astype(BF16)
    do_down = shift_down(do32, quarter).astype(BF16)
    f0, f1, f2, f3 = (normed_ref[i] for i in range(4))
    grad_ref[0:bins, :] += dot_tn(f3, de_up) + dot_tn(f1, do)
    grad_ref[bins:2 * bins, :] += dot_tn(f0, de) + dot_tn(f2, do)
    grad_ref[2 * bins:3 * bins, :] += dot_tn(f1, de) + dot_tn(f3, do)
    grad_ref[3 * bins:4 * bins, :] += dot_tn(f2, de) + dot_tn(f0, do_down)


def grad_call(permutation, normed, pre, back, moment, sums, quarter, cols):
    bins = normed.shape[2]
    channels = pre.shape[2]
    windows = normed.shape[1] // quarter
    rows = STEP_WINDOWS * quarter
    grid_spec = pltpu.PrefetchScalarGridSpec(
        num_scalar_prefetch=1,
        grid=(windows // STEP_WINDOWS,),
        in_specs=[
            pl.BlockSpec((4, rows, bins), lambda i, p: (0, i, 0)),
            pl.BlockSpec((2, rows, channels), lambda i, p: (0, i, 0)),
            pl.BlockSpec((2, rows, channels), lambda i, p: (0, i, 0)),
            pl.BlockSpec(moment.shape, lambda i, p: (0, 0)),
            pl.BlockSpec(sums.shape, lambda i, p: (0, 0, 0)),
        ],
        out_specs=pl.BlockSpec((4 * bins, channels), lambda i, p: (0, 0)),
        scratch_shapes=[pltpu.VMEM((windows, 2 * channels), F32)],
    )
    return pl.pallas_call(
        functools.partial(grad_kernel, quarter=quarter, cols=cols),
        grid_spec=grid_spec,
        out_shape=jax.ShapeDtypeStruct((4 * bins, channels), F32),
        compiler_params=pltpu.CompilerParams(vmem_limit_bytes=VMEM_LIMIT),
        name="grad_enc1",
    )(permutation, normed, pre, back, moment, sums)


def exchange(values, axes):
    return lax.all_to_all(values, axes, split_axis=0, concat_axis=0, tiled=True)


def local(spectra, sensor_ids, permutation, w_enc1, w_enc2, w_dec1, w_dec2):
    windows, frames, bins = spectra.shape
    channels = w_enc1.shape[1]
    cols = lax.axis_size("col")
    total_windows = windows * lax.axis_size("row") * cols
    sensors = total_windows // WIN_SENSOR
    chunks = bins // LANES
    quarter = frames // 4
    both = ("row", "col")

    sums = exchange(sums_call(spectra, sensor_ids), both)
    coef = exchange(stats_call(sums, windows, chunks, sensors, WIN_SENSOR * frames), both)
    normed, pre, stat = enc1_call(permutation, spectra, coef, w_enc1, cols)
    stat = exchange(stat.reshape(cols * windows, 2 * channels), "col").reshape(cols, windows, 2 * channels)
    grad_c, grad_b, grad_v, back, moment, moments = middle_call(
        permutation, normed, pre, stat, w_enc2, w_dec1, w_dec2, quarter, cols, total_windows)
    moments = exchange(moments.reshape(cols * windows, 2 * channels), "col").reshape(cols, windows, 2 * channels)
    grad_w = grad_call(permutation, normed, pre, back, moment, moments, quarter, cols)
    grad_w, grad_v, grad_b, grad_c = lax.psum((grad_w, grad_v, grad_b, grad_c), both)
    grad_b = grad_b.reshape(4, channels, channels).transpose(1, 0, 2).reshape(channels, 4 * channels)
    grad_c = grad_c.reshape(4 * bins // channels, channels, channels).transpose(1, 0, 2).reshape(channels, 4 * bins)
    return (grad_w, grad_v, grad_b, grad_c)


def solution(mesh):
    return jax.shard_map(
        local,
        mesh=mesh,
        in_specs=(
            P(("row", "col"), None, None),
            P(("row", "col"), None),
            P(("row", "col")),
            P(),
            P(),
            P(),
            P(),
        ),
        out_specs=(P(), P(), P(), P()),
        check_vma=False,
    )
```

time: 618 us -> 294 us (0.48); the launches traced: 609 us -> 293 us
  waiting for transfers between devices: 334 us -> 162 us
  local copies, waits for them, and re-layouts: 95.4 us -> 14.4 us
  Pallas kernels: 0 us -> 45.7 us
  other arithmetic: 45.3 us -> 0 us
  matrix products: 34.1 us -> 0 us
  blocking collectives: 67.2 us -> 52.6 us
  starting transfers between devices: 17.8 us -> 4.6 us
    all_to_all x3 -> x1, waiting for transfers between devices: 102 us -> 7.41 us  [exchange(): return lax.all_to_all(values, axes, split_axis=0, concat_axis=0, tiled=True)]
    psum x2 -> x1, waiting for transfers between devices: 232 us -> 154 us  [local(): lax.psum((grad_w, grad_v, grad_b, grad_c), both)]
    psum x1 -> x0, blocking collectives: 67.2 us -> none  [local(): lax.psum((totals, squares, counts), ('row', 'col'))]
    all_to_all x0 -> x3, blocking collectives: none -> 52.6 us  [exchange(): return lax.all_to_all(values, axes, split_axis=0, concat_axis=0, tiled=True)]
    pallas_call x0 -> x5, Pallas kernels: none -> 45.7 us  [the longest x1 19.7 us: middle_call(): pl.pallas_call(functools.partial(middle_kernel, quarter=quarter, cols=col...]
    dot_general x15 -> x0, matrix products: 34.1 us -> none  [the longest x4 14.9 us: layer_sum(): jnp.einsum('rk,ro->ko', left_flat, right_flat, preferred_element_type=jnp...]
    reshape x6 -> x2, local copies, waits for them, and re-layouts: 26.6 us -> 4.03 us  [the longest x1 2.43 us: local(): grad_b.reshape(4, channels, channels).transpose(1, 0, 2)]
    another operation x6 -> x0, other arithmetic: 17.1 us -> none  [the longest x5 17 us: fold_taps(): jnp.stack([even_rows, odd_rows], axis=2)]
  transfers between devices with their start and end apart: 5 -> 2, of which waited for: 4 -> 2; matrix products, arithmetic and copies ran while one was open for 3% -> 1% of each run, Pallas kernels for 0% -> 0%
where the time goes in v1:
time: 294 us; the launch traced here: 293 us
  waiting for transfers between devices  162 us (55%)
  blocking collectives  52.6 us (18%)
  Pallas kernels  45.7 us (16%)
  local copies, waits for them, and re-layouts  14.4 us (5%)
  between operations  14.1 us (5%)
  starting transfers between devices  4.6 us (2%)
    psum x1, waiting for transfers between devices, local(): lax.psum((grad_w, grad_v, grad_b, grad_c), both)  154 us
    all_to_all x3, blocking collectives, exchange(): return lax.all_to_all(values, axes, split_axis=0, concat_axis=0, tiled=True)  52.6 us
    pallas_call x1, Pallas kernels, middle_call(): pl.pallas_call(functools.partial(middle_kernel, quarter=quarter, cols=col...  19.7 us
    pallas_call x1, Pallas kernels, enc1_call(): pl.pallas_call(functools.partial(enc1_kernel, chunks=chunks, cols=cols, c...  10.2 us
    unnamed x16, local copies, waits for them, and re-layouts  9.32 us
    pallas_call x1, Pallas kernels, grad_call(): pl.pallas_call(functools.partial(grad_kernel, quarter=quarter, cols=cols)...  7.94 us
    all_to_all x1, waiting for transfers between devices, exchange(): return lax.all_to_all(values, axes, split_axis=0, concat_axis=0, tiled=True)  7.41 us
  transfers between devices with their start and end apart: 2, of which 2 were waited for; matrix products, arithmetic and copies ran while one was open for 1% of the time, Pallas kernels for 0%

profile of v1, /device:TPU:1, one launch (start us, length us, event | category | flops | bytes accessed | tf_op | source)
XLA Modules:
  0.0 293.1 jit_solution(18021178795548715409)
XLA Ops:
  7.2 1.3 copy.14.ids_ref
  8.5 5.3 %window_sums.1 = f32[128,256]{1,0:T(8,128)} custom-call(bf16[16,256,512]{2,1,0:T(8,128)(2,1)} %spec_ref.3, s32[16,1]{1,0:T(8,128)} %copy.14.ids_ref), custom_call_target="tpu_custom_call" | custom-call | tf_op jit(solution)/shard_map/window_sums/pallas_call | solution.py:94
  13.8 1.0 copy.15
  14.8 21.6 %all_to_all.34 = f32[128,1,256]{2,1,0:T(1,128)S(1)} all-to-all(f32[128,1,256]{2,1,0:T(1,128)S(1)} %copy.15), channel_id=1, replica_groups=mesh['row'=8,'col'=16] {'row','col'}, dimensions={0} | all-to-all | bytes 262144 | tf_op jit(solution)/shard_map/all_to_all | solution.py:454
  36.4 0.7 copy.23
  37.0 2.6 sensor_stats.1
  39.6 14.9 %all_to_all.35 = f32[128,1,128]{2,1,0:T(1,128)} all-to-all(f32[128,1,128]{2,1,0:T(1,128)} %bitcast.25), channel_id=1, replica_groups=mesh['row'=8,'col'=16] {'row','col'}, dimensions={0} | all-to-all | bytes 131072 | tf_op jit(solution)/shard_map/all_to_all | solution.py:454
  54.6 10.2 %normalize_enc1.1 = (bf16[4,1024,512]{2,1,0:T(8,128)(2,1)}, f32[2,1024,256]{2,1,0:T(8,128)}, f32[16,16,512]{2,1,0:T(8,128)}) custom-call(s32[16]{0:T(128)} %perm_ref.5, bf16[16,256,512]{2,1,0:T(8,128)(2,1)} %spec_ref.3, f32[128,128]{1,0:T(8,128)} %bitcast.24, bf16[2048,256]{1,0:T(8,128)(2,1)} %w_ref.1), custom_call_target="tpu_custom_call" | custom-call | tf_op jit(solution)/shard_map/normalize_enc1/pallas_call | solution.py:216
  64.7 16.1 %all_to_all.36.stat_ref = f32[16,16,512]{2,1,0:T(8,128)} all-to-all(f32[16,16,512]{2,1,0:T(8,128)} %get-tuple-element.15), channel_id=1, replica_groups=mesh['row'=8,'col'=16] {'col'}, dimensions={0} | all-to-all | bytes 1048576 | tf_op jit(solution)/shard_map/all_to_all | solution.py:454
  80.8 19.7 %middle.1 = (f32[2048,256]{1,0:T(8,128)}, f32[1024,256]{1,0:T(8,128)}, f32[1024,256]{1,0:T(8,128)}, f32[2,1024,256]{2,1,0:T(8,128)}, f32[16,512]{1,0:T(8,128)}, /*index=5*/f32[16,16,512]{2,1,0:T(8,128)}) custom-call(s32[16]{0:T(128)} %perm_ref.5, bf16[4,1024,512]{2,1,0:T(8,128)(2,1)} %get-tuple-element.13.normed_ref, ...), custom_call_target="tpu_custom_call" | custom-call | tf_op jit(solution)/shard_map/middle/pallas_call | solution.py:377
  100.5 0.0 copy-start.2
  100.5 4.6 %all-to-all-start.3 = ((f32[16,16,512]{2,1,0:T(8,128)}), f32[16,16,512]{2,1,0:T(8,128)S(1)}, u32[]{:S(2)}, u32[]{:S(2)}) async-start(f32[16,16,512]{2,1,0:T(8,128)} %get-tuple-element.18), calls=%async_computation.3 | async-start | bytes 1048576 | tf_op jit(solution)/shard_map/all_to_all | solution.py:454
  105.1 0.0 all-reduce.3.cloned.1.call-start
  105.1 2.4 copy.20
  107.6 0.0 copy-done.2
  107.6 1.6 copy.21
  109.2 7.4 %all-to-all-done.3.sums_ref = f32[16,16,512]{2,1,0:T(8,128)S(1)} async-done(((f32[16,16,512]{2,1,0:T(8,128)}), f32[16,16,512]{2,1,0:T(8,128)S(1)}, u32[]{:S(2)}, u32[]{:S(2)}) %all-to-all-start.3) | async-done | bytes 524320 | tf_op jit(solution)/shard_map/all_to_all | solution.py:454
  116.6 0.0 copy-start
  116.6 0.8 copy-done
  117.4 7.9 %grad_enc1.1 = f32[2048,256]{1,0:T(8,128)} custom-call(s32[16]{0:T(128)} %perm_ref.5, bf16[4,1024,512]{2,1,0:T(8,128)(2,1)} %get-tuple-element.13.normed_ref, f32[2,1024,256]{2,1,0:T(8,128)} %get-tuple-element.14.pre_ref, f32[2,1024,256]{2,1,0:T(8,128)} %get-tuple-element.16.back_ref, f32[16,512]{1,0:T(8,128)} %get-tuple-element.17.moment_ref, ...), custom_call_target="tpu_custom_call" | custom-call | tf_op jit(solution)/shard_map/grad_enc1/pallas_call | solution.py:444
  125.3 0.0 all-reduce.3.cloned.1.call-update
  125.3 154.3 %all-reduce.3.cloned.1.call-done = (f32[2048,256]{1,0:T(8,128)}, f32[1024,256]{1,0:T(8,128)}, f32[256,1024]{1,0:T(8,128)}, f32[256,2048]{1,0:T(8,128)}) async-done(((f32[2048,256]{1,0:T(8,128)}, f32[1024,256]{1,0:T(8,128)}, f32[256,1024]{1,0:T(8,128)}, f32[256,2048]{1,0:T(8,128)}), (f32[2048,256]{1,0:T(8,128)}, f32[1024,256]{1,0:T(8,128)}, f32[256,1024]{1,0:T(8,128)}, ...) | async-done | bytes 6291472 | tf_op jit(solution)/shard_map/psum | solution.py:475
  279.7 0.0 copy-start.4
  279.7 0.0 copy-start.3
  279.7 3.2 %copy.28 = f32[2048,256]{1,0:T(8,128)} copy(f32[2048,256]{1,0:T(8,128)} %get-tuple-element.26) | data formatting | bytes 4194304
  282.9 0.0 copy-done.4
  282.9 0.0 copy-start.1
  282.9 1.0 copy.29
  283.8 0.0 copy-done.3
  283.8 1.0 copy.30
  284.8 0.1 copy-done.1
  284.9 1.3 copy.31
Async XLA Ops:
  100.5 7.0 %copy-start.2 = (f32[2048,256]{1,0:T(8,128)S(1)}, f32[2048,256]{1,0:T(8,128)}, u32[]{:S(2)}) copy-start(f32[2048,256]{1,0:T(8,128)} %get-tuple-element.21) | copy-start | bytes 6291460
  100.5 16.1 %all-to-all-start.3 = ((f32[16,16,512]{2,1,0:T(8,128)}), f32[16,16,512]{2,1,0:T(8,128)S(1)}, u32[]{:S(2)}, u32[]{:S(2)}) async-start(f32[16,16,512]{2,1,0:T(8,128)} %get-tuple-element.18), calls=%async_computation.3 | async-start | bytes 1048576 | tf_op jit(solution)/shard_map/all_to_all | solution.py:454
  105.1 174.6 %all-reduce.3.cloned.1.call-start = ((), (), s32[]{:S(2)}) async-start(), calls=%async_computation.4 | async-start | bytes 12582912 | tf_op jit(solution)/shard_map/psum | solution.py:475
  116.6 0.8 copy-start
  279.7 3.2 %copy-start.4 = (f32[1024,256]{1,0:T(8,128)S(1)}, f32[1024,256]{1,0:T(8,128)}, u32[]{:S(2)}) copy-start(f32[1024,256]{1,0:T(8,128)} %get-tuple-element.27) | copy-start | bytes 3145732
  279.7 4.2 %copy-start.3 = (f32[256,1024]{1,0:T(8,128)S(1)}, f32[256,1024]{1,0:T(8,128)}, u32[]{:S(2)}) copy-start(f32[256,1024]{1,0:T(8,128)} %get-tuple-element.28) | copy-start | bytes 3145732
  282.9 2.0 copy-start.1
Sparse Core Ops, SparseCore 0:
  125.4 154.1 all-reduce.2

commit v2 on v1

--- a/solution.py
+++ b/solution.py
@@ -5,7 +5,7 @@
 from jax import lax
 from jax.experimental import pallas as pl
 from jax.experimental.pallas import tpu as pltpu
-from jax.sharding import PartitionSpec as P
+from jax.sharding import Mesh, PartitionSpec as P
 
 WIN_SENSOR = 8
 EPS = 1e-05
@@ -234,9 +234,15 @@
     return jnp.concatenate(parts, axis=0)
 
 
-def middle_kernel(perm_ref, normed_ref, pre_ref, stat_ref, v_ref, b_ref, c_ref,
-                  grad_c_ref, grad_b_ref, grad_v_ref, back_ref, moment_ref, sums_ref,
-                  moment, sums, *, quarter, cols, total_windows):
+def write_halves(core_ref, grads, own_ref, send_ref):
+    half = own_ref.shape[0]
+    own_ref[...] = grads[pl.ds(pl.multiple_of(core_ref[0] * half, half), half), :]
+    send_ref[...] = grads[pl.ds(pl.multiple_of((1 - core_ref[0]) * half, half), half), :]
+
+
+def middle_kernel(perm_ref, core_ref, normed_ref, pre_ref, stat_ref, v_ref, b_ref, c_ref,
+                  own_ref, send_ref, back_ref, moment_ref, sums_ref,
+                  grads, moment, sums, *, quarter, cols, total_windows):
     step = pl.program_id(0)
     channels = v_ref.shape[1]
     bins = normed_ref.shape[2]
@@ -254,9 +260,7 @@
         moment[:, 0:ch] = mean
         moment[:, ch:2 * ch] = lax.rsqrt(variance + EPS)
         moment_ref[...] = moment[...]
-        grad_c_ref[...] = jnp.zeros_like(grad_c_ref)
-        grad_b_ref[...] = jnp.zeros_like(grad_b_ref)
-        grad_v_ref[...] = jnp.zeros_like(grad_v_ref)
+        grads[...] = jnp.zeros_like(grads)
 
     mean = window_rows(perm_ref, moment, step, windows, quarter, all_windows, cols, 0, ch)
     inverse = window_rows(perm_ref, moment, step, windows, quarter, all_windows, cols, ch, 2 * ch)
@@ -290,11 +294,13 @@
     g2 = delta(dot(do, c1) + dot(de, c3), 2)
     g3 = delta(dot(do, c2) + dot(de_up, c0), 3)
     halves = bins // ch
+    base_b = 4 * bins
+    base_v = base_b + 4 * ch
 
     def add_c(k, value):
         for j in range(halves):
             at = (k * halves + j) * ch
-            grad_c_ref[at:at + ch, :] += value[:, j * ch:(j + 1) * ch]
+            grads[at:at + ch, :] += value[:, j * ch:(j + 1) * ch]
 
     add_c(0, dot_tn(de_up, g3) + dot_tn(do, g1))
     add_c(1, dot_tn(de, g0) + dot_tn(do, g2))
@@ -306,19 +312,19 @@
     dd_o = (back_o * (gate_o * (1.0 + d1_o * (1.0 - gate_o)))).astype(BF16)
     h_up = shift_up(h32, quarter).astype(BF16)
     h_down = shift_down(h32, quarter).astype(BF16)
-    grad_b_ref[0:ch, :] += dot_tn(h_up, dd_o)
-    grad_b_ref[ch:2 * ch, :] += dot_tn(h, dd_e)
-    grad_b_ref[2 * ch:3 * ch, :] += dot_tn(h, dd_o)
-    grad_b_ref[3 * ch:4 * ch, :] += dot_tn(h_down, dd_e)
+    grads[base_b:base_b + ch, :] += dot_tn(h_up, dd_o)
+    grads[base_b + ch:base_b + 2 * ch, :] += dot_tn(h, dd_e)
+    grads[base_b + 2 * ch:base_b + 3 * ch, :] += dot_tn(h, dd_o)
+    grads[base_b + 3 * ch:base_b + 4 * ch, :] += dot_tn(h_down, dd_e)
     back2 = shift_down(dot_nt(dd_o, b0), quarter) + dot_nt(dd_e, b1) + dot_nt(dd_o, b2) + shift_up(dot_nt(dd_e, b3), quarter)
     d2_32 = (back2 * (gate2 * (1.0 + pre2 * (1.0 - gate2)))).astype(BF16).astype(F32)
     d2 = d2_32.astype(BF16)
     d2_up = shift_up(d2_32, quarter).astype(BF16)
     d2_down = shift_down(d2_32, quarter).astype(BF16)
-    grad_v_ref[0:ch, :] += dot_tn(a_o, d2_up)
-    grad_v_ref[ch:2 * ch, :] += dot_tn(a_e, d2)
-    grad_v_ref[2 * ch:3 * ch, :] += dot_tn(a_o, d2)
-    grad_v_ref[3 * ch:4 * ch, :] += dot_tn(a_e, d2_down)
+    grads[base_v:base_v + ch, :] += dot_tn(a_o, d2_up)
+    grads[base_v + ch:base_v + 2 * ch, :] += dot_tn(a_e, d2)
+    grads[base_v + 2 * ch:base_v + 3 * ch, :] += dot_tn(a_o, d2)
+    grads[base_v + 3 * ch:base_v + 4 * ch, :] += dot_tn(a_e, d2_down)
     fold_e = dot_nt(d2, v1) + shift_down(dot_nt(d2, v3), quarter)
     fold_o = dot_nt(d2, v2) + shift_up(dot_nt(d2, v0), quarter)
     gate_he = sigmoid(hat_e)
@@ -341,35 +347,37 @@
     def _():
         for d in range(cols):
             sums_ref[d] = sums[...]
-
-
-def middle_call(permutation, normed, pre, stat, w_enc2, w_dec1, w_dec2, quarter, cols, total_windows):
+        write_halves(core_ref, grads, own_ref, send_ref)
+
+
+def middle_call(permutation, core, normed, pre, stat, w_enc2, w_dec1, w_dec2, quarter, cols, total_windows):
     bins = normed.shape[2]
     channels = w_enc2.shape[1]
     windows = normed.shape[1] // quarter
     rows = STEP_WINDOWS * quarter
-    whole2 = lambda i, p: (0, 0)
-    whole3 = lambda i, p: (0, 0, 0)
+    total = 4 * bins + 8 * channels
+    whole2 = lambda i, p, c: (0, 0)
+    whole3 = lambda i, p, c: (0, 0, 0)
     grid_spec = pltpu.PrefetchScalarGridSpec(
-        num_scalar_prefetch=1,
+        num_scalar_prefetch=2,
         grid=(windows // STEP_WINDOWS,),
         in_specs=[
-            pl.BlockSpec((4, rows, bins), lambda i, p: (0, i, 0)),
-            pl.BlockSpec((2, rows, channels), lambda i, p: (0, i, 0)),
+            pl.BlockSpec((4, rows, bins), lambda i, p, c: (0, i, 0)),
+            pl.BlockSpec((2, rows, channels), lambda i, p, c: (0, i, 0)),
             pl.BlockSpec(stat.shape, whole3),
             pl.BlockSpec(w_enc2.shape, whole2),
             pl.BlockSpec(w_dec1.shape, whole2),
             pl.BlockSpec(w_dec2.shape, whole2),
         ],
         out_specs=[
-            pl.BlockSpec((4 * bins, channels), whole2),
-            pl.BlockSpec((4 * channels, channels), whole2),
-            pl.BlockSpec((4 * channels, channels), whole2),
-            pl.BlockSpec((2, rows, channels), lambda i, p: (0, i, 0)),
+            pl.BlockSpec((total // 2, channels), whole2),
+            pl.BlockSpec((total // 2, channels), whole2),
+            pl.BlockSpec((2, rows, channels), lambda i, p, c: (0, i, 0)),
             pl.BlockSpec((windows, 2 * channels), whole2),
             pl.BlockSpec(stat.shape, whole3),
         ],
         scratch_shapes=[
+            pltpu.VMEM((total, channels), F32),
             pltpu.VMEM((windows, 2 * channels), F32),
             pltpu.VMEM((windows, 2 * channels), F32),
         ],
@@ -378,19 +386,18 @@
         functools.partial(middle_kernel, quarter=quarter, cols=cols, total_windows=float(total_windows)),
         grid_spec=grid_spec,
         out_shape=[
-            jax.ShapeDtypeStruct((4 * bins, channels), F32),
-            jax.ShapeDtypeStruct((4 * channels, channels), F32),
-            jax.ShapeDtypeStruct((4 * channels, channels), F32),
+            jax.ShapeDtypeStruct((total // 2, channels), F32),
+            jax.ShapeDtypeStruct((total // 2, channels), F32),
             jax.ShapeDtypeStruct(pre.shape, F32),
             jax.ShapeDtypeStruct((windows, 2 * channels), F32),
             jax.ShapeDtypeStruct(stat.shape, F32),
         ],
         compiler_params=pltpu.CompilerParams(vmem_limit_bytes=VMEM_LIMIT),
         name="middle",
-    )(permutation, normed, pre, stat, w_enc2, w_dec1, w_dec2)
-
-
-def grad_kernel(perm_ref, normed_ref, pre_ref, back_ref, moment_ref, sums_ref, grad_ref, scale, *, quarter, cols):
+    )(permutation, core, normed, pre, stat, w_enc2, w_dec1, w_dec2)
+
+
+def grad_kernel(perm_ref, core_ref, normed_ref, pre_ref, back_ref, moment_ref, sums_ref, own_ref, send_ref, grads, scale, *, quarter, cols):
     step = pl.program_id(0)
     bins = normed_ref.shape[2]
     rows = normed_ref.shape[1]
@@ -401,7 +408,7 @@
     @pl.when(step == 0)
     def _():
         scale[...] = jnp.sum(sums_ref[...], axis=0) / (2.0 * quarter * cols)
-        grad_ref[...] = jnp.zeros_like(grad_ref)
+        grads[...] = jnp.zeros_like(grads)
 
     pick = functools.partial(window_rows, perm_ref, step=step, windows=windows, quarter=quarter, all_windows=all_windows, cols=cols)
     mean = pick(table=moment_ref, first=0, last=ch)
@@ -417,80 +424,114 @@
     de_up = shift_up(de32, quarter).astype(BF16)
     do_down = shift_down(do32, quarter).astype(BF16)
     f0, f1, f2, f3 = (normed_ref[i] for i in range(4))
-    grad_ref[0:bins, :] += dot_tn(f3, de_up) + dot_tn(f1, do)
-    grad_ref[bins:2 * bins, :] += dot_tn(f0, de) + dot_tn(f2, do)
-    grad_ref[2 * bins:3 * bins, :] += dot_tn(f1, de) + dot_tn(f3, do)
-    grad_ref[3 * bins:4 * bins, :] += dot_tn(f2, de) + dot_tn(f0, do_down)
-
-
-def grad_call(permutation, normed, pre, back, moment, sums, quarter, cols):
+    grads[0:bins, :] += dot_tn(f3, de_up) + dot_tn(f1, do)
+    grads[bins:2 * bins, :] += dot_tn(f0, de) + dot_tn(f2, do)
+    grads[2 * bins:3 * bins, :] += dot_tn(f1, de) + dot_tn(f3, do)
+    grads[3 * bins:4 * bins, :] += dot_tn(f2, de) + dot_tn(f0, do_down)
+
+    @pl.when(step == pl.num_programs(0) - 1)
+    def _():
+        write_halves(core_ref, grads, own_ref, send_ref)
+
+
+def grad_call(permutation, core, normed, pre, back, moment, sums, quarter, cols):
     bins = normed.shape[2]
     channels = pre.shape[2]
     windows = normed.shape[1] // quarter
     rows = STEP_WINDOWS * quarter
     grid_spec = pltpu.PrefetchScalarGridSpec(
-        num_scalar_prefetch=1,
+        num_scalar_prefetch=2,
         grid=(windows // STEP_WINDOWS,),
         in_specs=[
-            pl.BlockSpec((4, rows, bins), lambda i, p: (0, i, 0)),
-            pl.BlockSpec((2, rows, channels), lambda i, p: (0, i, 0)),
-            pl.BlockSpec((2, rows, channels), lambda i, p: (0, i, 0)),
-            pl.BlockSpec(moment.shape, lambda i, p: (0, 0)),
-            pl.BlockSpec(sums.shape, lambda i, p: (0, 0, 0)),
-        ],
-        out_specs=pl.BlockSpec((4 * bins, channels), lambda i, p: (0, 0)),
-        scratch_shapes=[pltpu.VMEM((windows, 2 * channels), F32)],
+            pl.BlockSpec((4, rows, bins), lambda i, p, c: (0, i, 0)),
+            pl.BlockSpec((2, rows, channels), lambda i, p, c: (0, i, 0)),
+            pl.BlockSpec((2, rows, channels), lambda i, p, c: (0, i, 0)),
+            pl.BlockSpec(moment.shape, lambda i, p, c: (0, 0)),
+            pl.BlockSpec(sums.shape, lambda i, p, c: (0, 0, 0)),
+        ],
+        out_specs=[pl.BlockSpec((2 * bins, channels), lambda i, p, c: (0, 0))] * 2,
+        scratch_shapes=[pltpu.VMEM((4 * bins, channels), F32), pltpu.VMEM((windows, 2 * channels), F32)],
     )
     return pl.pallas_call(
         functools.partial(grad_kernel, quarter=quarter, cols=cols),
         grid_spec=grid_spec,
-        out_shape=jax.ShapeDtypeStruct((4 * bins, channels), F32),
+        out_shape=[jax.ShapeDtypeStruct((2 * bins, channels), F32)] * 2,
         compiler_params=pltpu.CompilerParams(vmem_limit_bytes=VMEM_LIMIT),
         name="grad_enc1",
-    )(permutation, normed, pre, back, moment, sums)
+    )(permutation, core, normed, pre, back, moment, sums)
+
+
+def swap_cores(values):
+    return lax.ppermute(values, "core", [(0, 1), (1, 0)])
 
 
 def exchange(values, axes):
     return lax.all_to_all(values, axes, split_axis=0, concat_axis=0, tiled=True)
+
+
+def scatter_sum(own, send, axes, chips):
+    total = (own + swap_cores(send)).astype(BF16)
+    pieces = exchange(total, axes)
+    return jnp.sum(pieces.reshape(chips, -1, own.shape[1]).astype(F32), axis=0)
+
+
+def gather_rows(piece, axes, chips):
+    rows, width = piece.shape
+    copies = jnp.broadcast_to(piece[None], (chips, rows, width)).reshape(chips * rows, width)
+    return exchange(copies, axes)
 
 
 def local(spectra, sensor_ids, permutation, w_enc1, w_enc2, w_dec1, w_dec2):
     windows, frames, bins = spectra.shape
     channels = w_enc1.shape[1]
-    cols = lax.axis_size("col")
+    col_axes = ("pair", "core")
+    chip_axes = ("row", "pair")
+    every = ("row", "pair", "core")
+    cols = lax.axis_size("pair") * lax.axis_size("core")
+    chips = lax.axis_size("row") * lax.axis_size("pair")
     total_windows = windows * lax.axis_size("row") * cols
     sensors = total_windows // WIN_SENSOR
     chunks = bins // LANES
     quarter = frames // 4
-    both = ("row", "col")
-
-    sums = exchange(sums_call(spectra, sensor_ids), both)
-    coef = exchange(stats_call(sums, windows, chunks, sensors, WIN_SENSOR * frames), both)
+    core_index = lax.axis_index("core")
+    core = core_index.astype(jnp.int32).reshape(1)
+
+    sums = exchange(sums_call(spectra, sensor_ids), every)
+    coef = exchange(stats_call(sums, windows, chunks, sensors, WIN_SENSOR * frames), every)
     normed, pre, stat = enc1_call(permutation, spectra, coef, w_enc1, cols)
-    stat = exchange(stat.reshape(cols * windows, 2 * channels), "col").reshape(cols, windows, 2 * channels)
-    grad_c, grad_b, grad_v, back, moment, moments = middle_call(
-        permutation, normed, pre, stat, w_enc2, w_dec1, w_dec2, quarter, cols, total_windows)
-    moments = exchange(moments.reshape(cols * windows, 2 * channels), "col").reshape(cols, windows, 2 * channels)
-    grad_w = grad_call(permutation, normed, pre, back, moment, moments, quarter, cols)
-    grad_w, grad_v, grad_b, grad_c = lax.psum((grad_w, grad_v, grad_b, grad_c), both)
+    stat = exchange(stat.reshape(cols * windows, 2 * channels), col_axes).reshape(cols, windows, 2 * channels)
+    own, send, back, moment, moments = middle_call(
+        permutation, core, normed, pre, stat, w_enc2, w_dec1, w_dec2, quarter, cols, total_windows)
+    moments = exchange(moments.reshape(cols * windows, 2 * channels), col_axes).reshape(cols, windows, 2 * channels)
+    early = scatter_sum(own, send, chip_axes, chips)
+    own, send = grad_call(permutation, core, normed, pre, back, moment, moments, quarter, cols)
+    late = scatter_sum(own, send, chip_axes, chips)
+
+    def collect(piece):
+        mine = gather_rows(piece, chip_axes, chips)
+        other = swap_cores(mine)
+        first = jnp.where(core_index == 0, mine, other)
+        second = jnp.where(core_index == 0, other, mine)
+        return jnp.concatenate([first, second], axis=0)
+
+    early = collect(early)
+    grad_w = collect(late)
+    grad_c = early[0:4 * bins]
+    grad_b = early[4 * bins:4 * bins + 4 * channels]
+    grad_v = early[4 * bins + 4 * channels:]
     grad_b = grad_b.reshape(4, channels, channels).transpose(1, 0, 2).reshape(channels, 4 * channels)
     grad_c = grad_c.reshape(4 * bins // channels, channels, channels).transpose(1, 0, 2).reshape(channels, 4 * bins)
     return (grad_w, grad_v, grad_b, grad_c)
 
 
 def solution(mesh):
+    rows, cols = mesh.devices.shape
+    inner = Mesh(mesh.devices.reshape(rows, cols // 2, 2), ("row", "pair", "core"))
+    spread = ("row", "pair", "core")
     return jax.shard_map(
         local,
-        mesh=mesh,
-        in_specs=(
-            P(("row", "col"), None, None),
-            P(("row", "col"), None),
-            P(("row", "col")),
-            P(),
-            P(),
-            P(),
-            P(),
-        ),
+        mesh=inner,
+        in_specs=(P(spread, None, None), P(spread, None), P(spread), P(), P(), P(), P()),
         out_specs=(P(), P(), P(), P()),
         check_vma=False,
     )

time: 294 us -> 235 us (0.80)
  waiting for transfers between devices: 162 us -> 84.8 us
  starting transfers between devices: 4.6 us -> 31.9 us
  between operations: 14.1 us -> 0.72 us
  other arithmetic: 0 us -> 7.07 us
  local copies, waits for them, and re-layouts: 14.4 us -> 11 us
    psum x1 -> x0, waiting for transfers between devices: 154 us -> none  [local(): lax.psum((grad_w, grad_v, grad_b, grad_c), both)]
    all_to_all x1 -> x5, waiting for transfers between devices: 7.41 us -> 82.4 us  [exchange(): return lax.all_to_all(values, axes, split_axis=0, concat_axis=0, tiled=True)]
    all_to_all x1 -> x5, starting transfers between devices: 4.57 us -> 25.1 us  [exchange(): return lax.all_to_all(values, axes, split_axis=0, concat_axis=0, tiled=True)]
    ppermute x0 -> x4, starting transfers between devices: none -> 6.82 us  [swap_cores(): return lax.ppermute(values, 'core', [(0, 1), (1, 0)])]
    unnamed x16 -> x10, local copies, waits for them, and re-layouts: 9.32 us -> 5.56 us
    select_n x0 -> x2, other arithmetic: none -> 3.26 us  [collect(): first = jnp.where(core_index == 0, mine, other)]
  transfers between devices with their start and end apart: 2 -> 9, of which waited for: 2 -> 6; matrix products, arithmetic and copies ran while one was open for 1% -> 2% of each run, Pallas kernels for 0% -> 4%
where the time goes in v2:
time: 235 us; the launch traced here: 234 us
  waiting for transfers between devices  84.8 us (36%)
  blocking collectives  51.9 us (22%)
  Pallas kernels  46.2 us (20%)
  starting transfers between devices  31.9 us (14%)
  local copies, waits for them, and re-layouts  11 us (5%)
  other arithmetic  7.07 us (3%)
    all_to_all x5, waiting for transfers between devices, exchange(): return lax.all_to_all(values, axes, split_axis=0, concat_axis=0, tiled=True)  82.4 us
    all_to_all x3, blocking collectives, exchange(): return lax.all_to_all(values, axes, split_axis=0, concat_axis=0, tiled=True)  51.9 us
    all_to_all x5, starting transfers between devices, exchange(): return lax.all_to_all(values, axes, split_axis=0, concat_axis=0, tiled=True)  25.1 us
    pallas_call x1, Pallas kernels, middle_call(): pl.pallas_call(functools.partial(middle_kernel, quarter=quarter, cols=col...  20 us
    pallas_call x1, Pallas kernels, enc1_call(): pl.pallas_call(functools.partial(enc1_kernel, chunks=chunks, cols=cols, c...  10.2 us
    pallas_call x1, Pallas kernels, grad_call(): pl.pallas_call(functools.partial(grad_kernel, quarter=quarter, cols=cols)...  8.22 us
    ppermute x4, starting transfers between devices, swap_cores(): return lax.ppermute(values, 'core', [(0, 1), (1, 0)])  6.82 us
    unnamed x10, local copies, waits for them, and re-layouts  5.56 us
  transfers between devices with their start and end apart: 9, of which 6 were waited for; matrix products, arithmetic and copies ran while one was open for 2% of the time, Pallas kernels for 4%

profile of v2, /device:TPU:1, one launch (start us, length us, event | category | flops | bytes accessed | tf_op | source)
XLA Modules:
  0.0 233.7 jit_solution(4402099546872438829)
XLA Ops:
  0.6 1.3 copy.14.ids_ref
  2.0 5.3 %window_sums.1 = f32[128,256]{1,0:T(8,128)} custom-call(bf16[16,256,512]{2,1,0:T(8,128)(2,1)} %spec_ref.3, s32[16,1]{1,0:T(8,128)} %copy.14.ids_ref), custom_call_target="tpu_custom_call" | custom-call | tf_op jit(solution)/shard_map/window_sums/pallas_call | solution.py:94
  8.3 21.6 %all_to_all.70 = f32[128,1,256]{2,1,0:T(1,128)S(1)} all-to-all(f32[128,1,256]{2,1,0:T(1,128)S(1)} %copy.15), channel_id=1, replica_groups=mesh['row'=8,'pair'=8,'core'=2] {'row','pair','core'}, dimensions={0} | all-to-all | bytes 262144 | tf_op jit(solution)/shard_map/all_to_all | solution.py:469
  30.5 2.6 %sensor_stats.1 = f32[128,128]{1,0:T(8,128)} custom-call(f32[128,256]{1,0:T(8,128)} %bitcast.35), custom_call_target="tpu_custom_call" | custom-call | tf_op jit(solution)/shard_map/sensor_stats/pallas_call | solution.py:129
  33.1 14.8 %all_to_all.71 = f32[128,1,128]{2,1,0:T(1,128)} all-to-all(f32[128,1,128]{2,1,0:T(1,128)} %bitcast.37), channel_id=1, replica_groups=mesh['row'=8,'pair'=8,'core'=2] {'row','pair','core'}, dimensions={0} | all-to-all | bytes 131072 | tf_op jit(solution)/shard_map/all_to_all | solution.py:469
  47.9 10.2 %normalize_enc1.1 = (bf16[4,1024,512]{2,1,0:T(8,128)(2,1)}, f32[2,1024,256]{2,1,0:T(8,128)}, f32[16,16,512]{2,1,0:T(8,128)}) custom-call(s32[16]{0:T(128)} %perm_ref.5, bf16[16,256,512]{2,1,0:T(8,128)(2,1)} %spec_ref.3, f32[128,128]{1,0:T(8,128)} %bitcast.36, bf16[2048,256]{1,0:T(8,128)(2,1)} %w_ref.1), custom_call_target="tpu_custom_call" | custom-call | tf_op jit(solution)/shard_map/normalize_enc1/pallas_call | solution.py:216
  58.1 4.2 %all-to-all-start.2 = ((f32[16,16,512]{2,1,0:T(8,128)}), f32[16,16,512]{2,1,0:T(8,128)S(1)}, u32[]{:S(2)}, u32[]{:S(2)}) async-start(f32[16,16,512]{2,1,0:T(8,128)} %get-tuple-element.16), calls=%async_computation.2 | async-start | bytes 1048576 | tf_op jit(solution)/shard_map/all_to_all | solution.py:469
  62.2 11.5 %all-to-all-done.2.stat_ref = f32[16,16,512]{2,1,0:T(8,128)S(1)} async-done(((f32[16,16,512]{2,1,0:T(8,128)}), f32[16,16,512]{2,1,0:T(8,128)S(1)}, u32[]{:S(2)}, u32[]{:S(2)}) %all-to-all-start.2) | async-done | bytes 524320 | tf_op jit(solution)/shard_map/all_to_all | solution.py:469
  74.5 20.0 %middle.1 = (f32[2048,256]{1,0:T(8,128)}, f32[2048,256]{1,0:T(8,128)}, f32[2,1024,256]{2,1,0:T(8,128)}, f32[16,512]{1,0:T(8,128)}, f32[16,16,512]{2,1,0:T(8,128)}) custom-call(s32[16]{0:T(128)} %perm_ref.5, s32[1]{0:T(128)} %bitcast.core_ref, bf16[4,1024,512]{2,1,0:T(8,128)(2,1)} %get-tuple-element.14.normed_ref, f32[2,1024,256]{2,1,0:T(8,128)} %get-tuple-element.15.pre_ref, ...), custom_call_target="tpu_custom_call" | custom-call | tf_op jit(solution)/shard_map/middle/pallas_call | solution.py:385
  94.5 1.1 collective-permute-start.2
  95.6 15.6 %all_to_all.72.sums_ref = f32[16,16,512]{2,1,0:T(8,128)} all-to-all(f32[16,16,512]{2,1,0:T(8,128)} %get-tuple-element.19), channel_id=1, replica_groups=mesh['row'=8,'pair'=8,'core'=2] {'pair','core'}, dimensions={0} | all-to-all | bytes 1048576 | tf_op jit(solution)/shard_map/all_to_all | solution.py:469
  111.2 8.2 %grad_enc1.1 = (f32[1024,256]{1,0:T(8,128)}, f32[1024,256]{1,0:T(8,128)}) custom-call(s32[16]{0:T(128)} %perm_ref.5, s32[1]{0:T(128)} %bitcast.core_ref, bf16[4,1024,512]{2,1,0:T(8,128)(2,1)} %get-tuple-element.14.normed_ref, f32[2,1024,256]{2,1,0:T(8,128)} %get-tuple-element.15.pre_ref, f32[2,1024,256]{2,1,0:T(8,128)} %get-tuple-element.17.back_ref, ...), custom_call_target="tpu_custom_call" | custom-call | tf_op jit(solution)/shard_map/grad_enc1/pallas_call | solution.py:455
  120.5 1.2 add_convert_fusion
  121.7 4.8 %all-to-all-start.6 = ((bf16[64,32,256]{2,1,0:T(8,128)(2,1)}), bf16[64,32,256]{2,1,0:T(8,128)(2,1)S(1)}, u32[]{:S(2)}, u32[]{:S(2)}) async-start(bf16[64,32,256]{2,1,0:T(8,128)(2,1)} %bitcast.7), calls=%async_computation.6 | async-start | bytes 2097152 | tf_op jit(solution)/shard_map/all_to_all | solution.py:469
  127.4 17.3 %all-to-all-done.6 = bf16[64,32,256]{2,1,0:T(8,128)(2,1)S(1)} async-done(((bf16[64,32,256]{2,1,0:T(8,128)(2,1)}), bf16[64,32,256]{2,1,0:T(8,128)(2,1)S(1)}, u32[]{:S(2)}, u32[]{:S(2)}) %all-to-all-start.6) | async-done | bytes 1048608 | tf_op jit(solution)/shard_map/all_to_all | solution.py:469
  144.7 4.9 %all-to-all-start.4 = ((bf16[64,16,256]{2,1,0:T(8,128)(2,1)}), bf16[64,16,256]{2,1,0:T(8,128)(2,1)S(1)}, u32[]{:S(2)}, u32[]{:S(2)}) async-start(bf16[64,16,256]{2,1,0:T(8,128)(2,1)} %bitcast.5), calls=%async_computation.4 | async-start | bytes 1048576 | tf_op jit(solution)/shard_map/all_to_all | solution.py:469
  149.7 11.2 %all-to-all-done.4 = bf16[64,16,256]{2,1,0:T(8,128)(2,1)S(1)} async-done(((bf16[64,16,256]{2,1,0:T(8,128)(2,1)}), bf16[64,16,256]{2,1,0:T(8,128)(2,1)S(1)}, u32[]{:S(2)}, u32[]{:S(2)}) %all-to-all-start.4) | async-done | bytes 524320 | tf_op jit(solution)/shard_map/all_to_all | solution.py:469
  160.9 1.6 broadcast_in_dim.5
  162.5 4.7 %all-to-all-start.7 = ((f32[64,32,256]{2,1,0:T(8,128)}), f32[64,32,256]{2,1,0:T(8,128)S(1)}, u32[]{:S(2)}, u32[]{:S(2)}) async-start(f32[64,32,256]{2,1,0:T(8,128)} %broadcast_in_dim.5), calls=%async_computation.7 | async-start | bytes 4194304 | tf_op jit(solution)/shard_map/all_to_all | solution.py:469
  167.3 27.4 %all-to-all-done.7 = f32[64,32,256]{2,1,0:T(8,128)S(1)} async-done(((f32[64,32,256]{2,1,0:T(8,128)}), f32[64,32,256]{2,1,0:T(8,128)S(1)}, u32[]{:S(2)}, u32[]{:S(2)}) %all-to-all-start.7) | async-done | bytes 2097184 | tf_op jit(solution)/shard_map/all_to_all | solution.py:469
  194.7 1.1 broadcast_in_dim.4
  195.8 6.6 %all-to-all-start.5 = ((f32[64,16,256]{2,1,0:T(8,128)}), f32[64,16,256]{2,1,0:T(8,128)S(1)}, u32[]{:S(2)}, u32[]{:S(2)}) async-start(f32[64,16,256]{2,1,0:T(8,128)} %broadcast_in_dim.4), calls=%async_computation.5 | async-start | bytes 2097152 | tf_op jit(solution)/shard_map/all_to_all | solution.py:469
  202.3 1.8 collective-permute-start.3
  204.1 15.0 %all-to-all-done.5 = f32[64,16,256]{2,1,0:T(8,128)S(1)} async-done(((f32[64,16,256]{2,1,0:T(8,128)}), f32[64,16,256]{2,1,0:T(8,128)S(1)}, u32[]{:S(2)}, u32[]{:S(2)}) %all-to-all-start.5) | async-done | bytes 1048608 | tf_op jit(solution)/shard_map/all_to_all | solution.py:469
  219.1 2.9 %collective-permute-start.1 = (f32[1024,256]{1,0:T(8,128)S(1)}, f32[1024,256]{1,0:T(8,128)}, u32[]{:S(2)}, u32[]{:S(2)}) collective-permute-start(f32[1024,256]{1,0:T(8,128)S(1)} %bitcast.29), channel_id=1, source_target_pairs={{0,1},{1,0},{2,3},{3,2},{4,5},{5,4},{6,7},{7,6},{8,9},{9,8},{10,11... | collective-permute-start | bytes 3145736 | tf_op jit(solution)/shard_map/ppermute | solution.py:465
  222.0 2.4 %collective-permute-done.1 = f32[1024,256]{1,0:T(8,128)} collective-permute-done((f32[1024,256]{1,0:T(8,128)S(1)}, f32[1024,256]{1,0:T(8,128)}, u32[]{:S(2)}, u32[]{:S(2)}) %collective-permute-start.1) | collective-permute-done | bytes 1048608 | tf_op jit(solution)/shard_map/ppermute | solution.py:465
  224.4 1.4 broadcast_select_fusion.3
  225.8 1.5 pad_maximum_fusion
  227.3 1.9 broadcast_select_fusion
  229.1 1.1 fusion
  230.9 1.2 copy.20
  232.1 1.6 copy.21
  (16 shorter events, 5.4 us)
Async XLA Ops:
  58.1 15.7 %all-to-all-start.2 = ((f32[16,16,512]{2,1,0:T(8,128)}), f32[16,16,512]{2,1,0:T(8,128)S(1)}, u32[]{:S(2)}, u32[]{:S(2)}) async-start(f32[16,16,512]{2,1,0:T(8,128)} %get-tuple-element.16), calls=%async_computation.2 | async-start | bytes 1048576 | tf_op jit(solution)/shard_map/all_to_all | solution.py:469
  73.7 0.8 copy-start
  94.5 26.0 %collective-permute-start.2 = (f32[2048,256]{1,0:T(8,128)}, f32[2048,256]{1,0:T(8,128)S(1)}, u32[]{:S(2)}, u32[]{:S(2)}) collective-permute-start(f32[2048,256]{1,0:T(8,128)} %get-tuple-element.23), channel_id=1, source_target_pairs={{0,1},{1,0},{2,3},{3,2},{4,5},{5,4},{6,7},{7,6},{8,9},{9,8},{10,11... | collective-permute-start | bytes 6291464 | tf_op jit(solution)/shard_map/ppermute | solution.py:465
  111.2 9.3 %copy-start.1 = (f32[2048,256]{1,0:T(8,128)S(1)}, f32[2048,256]{1,0:T(8,128)}, u32[]{:S(2)}) copy-start(f32[2048,256]{1,0:T(8,128)} %get-tuple-element.22) | copy-start | bytes 6291460
  119.4 7.0 %collective-permute-start = (f32[1024,256]{1,0:T(8,128)}, f32[1024,256]{1,0:T(8,128)S(1)}, u32[]{:S(2)}, u32[]{:S(2)}) collective-permute-start(f32[1024,256]{1,0:T(8,128)} %get-tuple-element.21), channel_id=1, source_target_pairs={{0,1},{1,0},{2,3},{3,2},{4,5},{5,4},{6,7},{7,6},{8,9},{9,8},{10,11... | collective-permute-start | bytes 3145736 | tf_op jit(solution)/shard_map/ppermute | solution.py:465
  121.7 4.8 %copy-start.2 = (f32[1024,256]{1,0:T(8,128)S(1)}, f32[1024,256]{1,0:T(8,128)}, u32[]{:S(2)}) copy-start(f32[1024,256]{1,0:T(8,128)} %get-tuple-element.20) | copy-start | bytes 3145732
  121.7 23.0 %all-to-all-start.6 = ((bf16[64,32,256]{2,1,0:T(8,128)(2,1)}), bf16[64,32,256]{2,1,0:T(8,128)(2,1)S(1)}, u32[]{:S(2)}, u32[]{:S(2)}) async-start(bf16[64,32,256]{2,1,0:T(8,128)(2,1)} %bitcast.7), calls=%async_computation.6 | async-start | bytes 2097152 | tf_op jit(solution)/shard_map/all_to_all | solution.py:469
  144.7 16.2 %all-to-all-start.4 = ((bf16[64,16,256]{2,1,0:T(8,128)(2,1)}), bf16[64,16,256]{2,1,0:T(8,128)(2,1)S(1)}, u32[]{:S(2)}, u32[]{:S(2)}) async-start(bf16[64,16,256]{2,1,0:T(8,128)(2,1)} %bitcast.5), calls=%async_computation.4 | async-start | bytes 1048576 | tf_op jit(solution)/shard_map/all_to_all | solution.py:469
  162.5 32.2 %all-to-all-start.7 = ((f32[64,32,256]{2,1,0:T(8,128)}), f32[64,32,256]{2,1,0:T(8,128)S(1)}, u32[]{:S(2)}, u32[]{:S(2)}) async-start(f32[64,32,256]{2,1,0:T(8,128)} %broadcast_in_dim.5), calls=%async_computation.7 | async-start | bytes 4194304 | tf_op jit(solution)/shard_map/all_to_all | solution.py:469
  195.8 23.3 %all-to-all-start.5 = ((f32[64,16,256]{2,1,0:T(8,128)}), f32[64,16,256]{2,1,0:T(8,128)S(1)}, u32[]{:S(2)}, u32[]{:S(2)}) async-start(f32[64,16,256]{2,1,0:T(8,128)} %broadcast_in_dim.4), calls=%async_computation.5 | async-start | bytes 2097152 | tf_op jit(solution)/shard_map/all_to_all | solution.py:469
  202.3 24.9 %collective-permute-start.3 = (f32[2048,256]{1,0:T(8,128)S(1)}, f32[2048,256]{1,0:T(8,128)}, u32[]{:S(2)}, u32[]{:S(2)}) collective-permute-start(f32[2048,256]{1,0:T(8,128)S(1)} %bitcast.27), channel_id=1, source_target_pairs={{0,1},{1,0},{2,3},{3,2},{4,5},{5,4},{6,7},{7,6},{8,9},{9,8},{10,11... | collective-permute-start | bytes 6291464 | tf_op jit(solution)/shard_map/ppermute | solution.py:465
  219.1 5.3 %collective-permute-start.1 = (f32[1024,256]{1,0:T(8,128)S(1)}, f32[1024,256]{1,0:T(8,128)}, u32[]{:S(2)}, u32[]{:S(2)}) collective-permute-start(f32[1024,256]{1,0:T(8,128)S(1)} %bitcast.29), channel_id=1, source_target_pairs={{0,1},{1,0},{2,3},{3,2},{4,5},{5,4},{6,7},{7,6},{8,9},{9,8},{10,11... | collective-permute-start | bytes 3145736 | tf_op jit(solution)/shard_map/ppermute | solution.py:465

commit v3 on v2

--- a/solution.py
+++ b/solution.py
@@ -13,6 +13,7 @@
 BF16 = jnp.bfloat16
 LANES = 128
 STEP_WINDOWS = 4
+SCALE_ROWS = 8
 VMEM_LIMIT = 56 * 1024 * 1024
 
 
@@ -57,7 +58,7 @@
     return (trainer // col_count) * per_row + trainer % per_row
 
 
-def sums_kernel(spec_ref, ids_ref, out_ref, acc, *, chunks):
+def sums_kernel(ids_ref, spec_ref, out_ref, acc, *, chunks, count):
     step = pl.program_id(0)
     windows, frames, bins = spec_ref.shape
     rows = 16
@@ -81,35 +82,73 @@
 
     @pl.when(step == pl.num_programs(0) - 1)
     def _():
-        count = ids_ref.shape[0]
         acc[LANES:2 * LANES, :] = jnp.zeros((LANES, LANES), F32)
-        acc[LANES:LANES + count, :] = jnp.broadcast_to(ids_ref[...].astype(F32), (count, LANES))
-        out_ref[:, 0:LANES] = acc[0:LANES, :].T
-        out_ref[:, LANES:2 * LANES] = acc[LANES:2 * LANES, :].T
+        for w in range(count):
+            acc[LANES + w:LANES + w + 1, :] = jnp.full((1, LANES), ids_ref[w], jnp.int32).astype(F32)
+        out_ref[pl.ds(0, LANES, stride=2), :] = acc[0:LANES, :].T
+        out_ref[pl.ds(1, LANES, stride=2), :] = acc[LANES:2 * LANES, :].T
 
 
 def sums_call(spectra, sensor_ids):
     windows, frames, bins = spectra.shape
     chunks = bins // LANES
-    return pl.pallas_call(
-        functools.partial(sums_kernel, chunks=chunks),
+    grid_spec = pltpu.PrefetchScalarGridSpec(
+        num_scalar_prefetch=1,
         grid=(windows // STEP_WINDOWS,),
-        in_specs=[
-            pl.BlockSpec((STEP_WINDOWS, frames, bins), lambda i: (i, 0, 0)),
-            pl.BlockSpec(sensor_ids.shape, lambda i: (0, 0)),
-        ],
-        out_specs=pl.BlockSpec((LANES, 2 * LANES), lambda i: (0, 0)),
-        out_shape=jax.ShapeDtypeStruct((LANES, 2 * LANES), F32),
+        in_specs=[pl.BlockSpec((STEP_WINDOWS, frames, bins), lambda i, s: (i, 0, 0))],
+        out_specs=pl.BlockSpec((2 * LANES, LANES), lambda i, s: (0, 0)),
         scratch_shapes=[pltpu.VMEM((2 * LANES, LANES), F32)],
+    )
+    return pl.pallas_call(
+        functools.partial(sums_kernel, chunks=chunks, count=windows),
+        grid_spec=grid_spec,
+        out_shape=jax.ShapeDtypeStruct((2 * LANES, LANES), F32),
         compiler_params=pltpu.CompilerParams(vmem_limit_bytes=VMEM_LIMIT),
         name="window_sums",
-    )(spectra, sensor_ids)
+    )(sensor_ids.reshape(windows), spectra)
+
+
+def sort_kernel(spec_ref, out_ref, lane, *, chunks):
+    windows, frames, bins = spec_ref.shape
+    quarter = frames // 4
+    rows = 32
+    for w in range(windows):
+        def body(i, carry):
+            at = pl.multiple_of(i * rows, rows)
+            value = jnp.log(1.0 + spec_ref[w, pl.ds(at, rows), :].astype(F32))
+            for k in range(chunks):
+                lane[w % 2, k, pl.ds(at, rows), :] = value[:, k * LANES:(k + 1) * LANES]
+            return carry
+
+        lax.fori_loop(0, frames // rows, body, 0, unroll=2)
+        for i in range(4):
+            for k in range(chunks):
+                out_ref[i, w * quarter:(w + 1) * quarter, k * LANES:(k + 1) * LANES] = lane[w % 2, k, pl.ds(i, quarter, stride=4), :]
+
+
+def sort_call(spectra):
+    windows, frames, bins = spectra.shape
+    chunks = bins // LANES
+    quarter = frames // 4
+    rows = STEP_WINDOWS * quarter
+    size = windows * frames * bins
+    return pl.pallas_call(
+        functools.partial(sort_kernel, chunks=chunks),
+        grid=(windows // STEP_WINDOWS,),
+        in_specs=[pl.BlockSpec((STEP_WINDOWS, frames, bins), lambda i: (i, 0, 0))],
+        out_specs=pl.BlockSpec((4, rows, bins), lambda i: (0, i, 0)),
+        out_shape=jax.ShapeDtypeStruct((4, windows * quarter, bins), F32),
+        scratch_shapes=[pltpu.VMEM((2, chunks, frames, LANES), F32)],
+        compiler_params=pltpu.CompilerParams(vmem_limit_bytes=VMEM_LIMIT),
+        cost_estimate=pl.CostEstimate(flops=8 * size, bytes_accessed=6 * size, transcendentals=size),
+        name="sort_frames",
+    )(spectra)
 
 
 def stats_kernel(in_ref, out_ref, *, windows, chunks, sensors, per_sensor):
     width = 2 * chunks
-    data = in_ref[:, 0:LANES].T
-    labels = in_ref[:, LANES:2 * LANES].T
+    data = in_ref[pl.ds(0, LANES, stride=2), :].T
+    labels = in_ref[pl.ds(1, LANES, stride=2), :].T
     sensor_rows = lax.broadcasted_iota(jnp.int32, (sensors, LANES), 0).astype(F32)
     tables = [(sensor_rows == labels[w:w + 1, :]).astype(F32).astype(BF16) for w in range(windows)]
     table = jnp.concatenate(tables, axis=1)
@@ -134,10 +173,10 @@
     )(received)
 
 
-def enc1_kernel(perm_ref, spec_ref, coef_ref, w_ref, normed_ref, pre_ref, stat_ref, coef, lane, stat, *, chunks, cols, copies):
+def enc1_kernel(perm_ref, log_ref, coef_ref, w_ref, normed_ref, pre_ref, stat_ref, coef, stat, *, chunks, quarter, cols, copies):
     step = pl.program_id(0)
-    windows, frames, bins = spec_ref.shape
-    quarter = frames // 4
+    bins = log_ref.shape[2]
+    windows = log_ref.shape[1] // quarter
     channels = w_ref.shape[1]
     all_windows = windows * pl.num_programs(0)
     width = 2 * chunks
@@ -146,24 +185,16 @@
     def _():
         coef[...] = coef_ref[...].T
 
-    rows = 32
     for w in range(windows):
         start = pl.multiple_of((step * windows + w) * width, width)
         both = coef[pl.ds(start, width), :]
-
-        def body(i, carry):
-            at = pl.multiple_of(i * rows, rows)
-            value = jnp.log(1.0 + spec_ref[w, pl.ds(at, rows), :].astype(F32))
-            for k in range(chunks):
-                part = value[:, k * LANES:(k + 1) * LANES]
-                lane[w % 2, k, pl.ds(at, rows), :] = (part - both[k:k + 1, :]) * both[chunks + k:chunks + k + 1, :]
-            return carry
-
-        lax.fori_loop(0, frames // rows, body, 0, unroll=2)
-        for i in range(4):
-            for k in range(chunks):
-                picked = lane[w % 2, k, pl.ds(i, quarter, stride=4), :]
-                normed_ref[i, w * quarter:(w + 1) * quarter, k * LANES:(k + 1) * LANES] = picked.astype(BF16)
+        low, high = w * quarter, (w + 1) * quarter
+        for k in range(chunks):
+            left, right = k * LANES, (k + 1) * LANES
+            center = both[k:k + 1, :]
+            factor = both[chunks + k:chunks + k + 1, :]
+            for i in range(4):
+                normed_ref[i, low:high, left:right] = ((log_ref[i, low:high, left:right] - center) * factor).astype(BF16)
 
     w0, w1, w2, w3 = (w_ref[k * bins:(k + 1) * bins, :] for k in range(4))
     f0, f1, f2, f3 = (normed_ref[i] for i in range(4))
@@ -188,17 +219,17 @@
             stat_ref[d] = stat[...]
 
 
-def enc1_call(permutation, spectra, coef, w_enc1, cols):
-    windows, frames, bins = spectra.shape
+def enc1_call(permutation, logs, coef, w_enc1, quarter, cols):
+    bins = logs.shape[2]
+    windows = logs.shape[1] // quarter
     chunks = bins // LANES
-    quarter = frames // 4
     channels = w_enc1.shape[1]
     rows = STEP_WINDOWS * quarter
     grid_spec = pltpu.PrefetchScalarGridSpec(
         num_scalar_prefetch=1,
         grid=(windows // STEP_WINDOWS,),
         in_specs=[
-            pl.BlockSpec((STEP_WINDOWS, frames, bins), lambda i, p: (i, 0, 0)),
+            pl.BlockSpec((4, rows, bins), lambda i, p: (0, i, 0)),
             pl.BlockSpec((LANES, LANES), lambda i, p: (0, 0)),
             pl.BlockSpec(w_enc1.shape, lambda i, p: (0, 0)),
         ],
@@ -209,12 +240,11 @@
         ],
         scratch_shapes=[
             pltpu.VMEM((LANES, LANES), F32),
-            pltpu.VMEM((2, chunks, frames, LANES), F32),
             pltpu.VMEM((windows, 2 * channels), F32),
         ],
     )
     return pl.pallas_call(
-        functools.partial(enc1_kernel, chunks=chunks, cols=cols, copies=cols),
+        functools.partial(enc1_kernel, chunks=chunks, quarter=quarter, cols=cols, copies=cols),
         grid_spec=grid_spec,
         out_shape=[
             jax.ShapeDtypeStruct((4, windows * quarter, bins), BF16),
@@ -223,7 +253,27 @@
         ],
         compiler_params=pltpu.CompilerParams(vmem_limit_bytes=VMEM_LIMIT),
         name="normalize_enc1",
-    )(permutation, spectra, coef, w_enc1)
+    )(permutation, logs, coef, w_enc1)
+
+
+def turn_kernel(in_ref, out_ref):
+    out_ref[0] = in_ref[0].T
+
+
+def turn_call(normed, steps):
+    classes, total, bins = normed.shape
+    rows = total // steps
+    size = classes * total * bins
+    return pl.pallas_call(
+        turn_kernel,
+        grid=(classes, steps),
+        in_specs=[pl.BlockSpec((1, rows, bins), lambda i, j: (i, j, 0))],
+        out_specs=pl.BlockSpec((1, bins, rows), lambda i, j: (i, 0, j)),
+        out_shape=jax.ShapeDtypeStruct((classes, bins, total), normed.dtype),
+        compiler_params=pltpu.CompilerParams(vmem_limit_bytes=VMEM_LIMIT),
+        cost_estimate=pl.CostEstimate(flops=4 * size, bytes_accessed=4 * size, transcendentals=0),
+        name="turn_normed",
+    )(normed)
 
 
 def window_rows(perm_ref, table, step, windows, quarter, all_windows, cols, first, last):
@@ -397,10 +447,10 @@
     )(permutation, core, normed, pre, stat, w_enc2, w_dec1, w_dec2)
 
 
-def grad_kernel(perm_ref, core_ref, normed_ref, pre_ref, back_ref, moment_ref, sums_ref, own_ref, send_ref, grads, scale, *, quarter, cols):
+def grad_kernel(perm_ref, core_ref, turned_ref, pre_ref, back_ref, moment_ref, sums_ref, own_ref, send_ref, grads, scale, *, quarter, cols):
     step = pl.program_id(0)
-    bins = normed_ref.shape[2]
-    rows = normed_ref.shape[1]
+    bins = turned_ref.shape[1]
+    rows = turned_ref.shape[2]
     ch = pre_ref.shape[2]
     windows = rows // quarter
     all_windows = windows * pl.num_programs(0)
@@ -423,27 +473,27 @@
     do = do32.astype(BF16)
     de_up = shift_up(de32, quarter).astype(BF16)
     do_down = shift_down(do32, quarter).astype(BF16)
-    f0, f1, f2, f3 = (normed_ref[i] for i in range(4))
-    grads[0:bins, :] += dot_tn(f3, de_up) + dot_tn(f1, do)
-    grads[bins:2 * bins, :] += dot_tn(f0, de) + dot_tn(f2, do)
-    grads[2 * bins:3 * bins, :] += dot_tn(f1, de) + dot_tn(f3, do)
-    grads[3 * bins:4 * bins, :] += dot_tn(f2, de) + dot_tn(f0, do_down)
+    f0, f1, f2, f3 = (turned_ref[i] for i in range(4))
+    grads[0:bins, :] += dot(f3, de_up) + dot(f1, do)
+    grads[bins:2 * bins, :] += dot(f0, de) + dot(f2, do)
+    grads[2 * bins:3 * bins, :] += dot(f1, de) + dot(f3, do)
+    grads[3 * bins:4 * bins, :] += dot(f2, de) + dot(f0, do_down)
 
     @pl.when(step == pl.num_programs(0) - 1)
     def _():
         write_halves(core_ref, grads, own_ref, send_ref)
 
 
-def grad_call(permutation, core, normed, pre, back, moment, sums, quarter, cols):
-    bins = normed.shape[2]
+def grad_call(permutation, core, turned, pre, back, moment, sums, quarter, cols):
+    bins = turned.shape[1]
     channels = pre.shape[2]
-    windows = normed.shape[1] // quarter
+    windows = turned.shape[2] // quarter
     rows = STEP_WINDOWS * quarter
     grid_spec = pltpu.PrefetchScalarGridSpec(
         num_scalar_prefetch=2,
         grid=(windows // STEP_WINDOWS,),
         in_specs=[
-            pl.BlockSpec((4, rows, bins), lambda i, p, c: (0, i, 0)),
+            pl.BlockSpec((4, bins, rows), lambda i, p, c: (0, 0, i)),
             pl.BlockSpec((2, rows, channels), lambda i, p, c: (0, i, 0)),
             pl.BlockSpec((2, rows, channels), lambda i, p, c: (0, i, 0)),
             pl.BlockSpec(moment.shape, lambda i, p, c: (0, 0)),
@@ -458,7 +508,7 @@
         out_shape=[jax.ShapeDtypeStruct((2 * bins, channels), F32)] * 2,
         compiler_params=pltpu.CompilerParams(vmem_limit_bytes=VMEM_LIMIT),
         name="grad_enc1",
-    )(permutation, core, normed, pre, back, moment, sums)
+    )(permutation, core, turned, pre, back, moment, sums)
 
 
 def swap_cores(values):
@@ -469,16 +519,95 @@
     return lax.all_to_all(values, axes, split_axis=0, concat_axis=0, tiled=True)
 
 
-def scatter_sum(own, send, axes, chips):
-    total = (own + swap_cores(send)).astype(BF16)
-    pieces = exchange(total, axes)
-    return jnp.sum(pieces.reshape(chips, -1, own.shape[1]).astype(F32), axis=0)
+def chip_sums(parts, axes, chips):
+    total = [(own + swap_cores(send)).astype(BF16).reshape(chips, -1, own.shape[1]) for own, send in parts]
+    total = jnp.concatenate(total, axis=1)
+    return exchange(total.reshape(-1, total.shape[2]), axes).reshape(total.shape)
+
+
+def owner_kernel(in_ref, out_ref):
+    chips, rows, width = in_ref.shape
+
+    def body(i, total):
+        return total + in_ref[i].astype(F32)
+
+    total = lax.fori_loop(0, chips, body, jnp.zeros((rows, width), F32), unroll=4)
+    largest = jnp.max(jnp.max(jnp.abs(total), axis=0, keepdims=True), axis=1, keepdims=True)
+    exponent = jnp.clip(jnp.ceil(jnp.log2(largest)), -110.0, 126.0)
+    out_ref[0:rows, :] = total * jnp.exp2(14.0 - exponent)
+    out_ref[rows:, :] = jnp.broadcast_to(exponent, (SCALE_ROWS, width))
+
+
+def owner_call(pieces):
+    chips, rows, width = pieces.shape
+    return pl.pallas_call(
+        owner_kernel,
+        out_shape=jax.ShapeDtypeStruct((rows + SCALE_ROWS, width), F32),
+        compiler_params=pltpu.CompilerParams(vmem_limit_bytes=VMEM_LIMIT),
+        name="owner_sum",
+    )(pieces)
 
 
 def gather_rows(piece, axes, chips):
     rows, width = piece.shape
-    copies = jnp.broadcast_to(piece[None], (chips, rows, width)).reshape(chips * rows, width)
-    return exchange(copies, axes)
+    copies = jnp.broadcast_to(piece.astype(jnp.float16)[None], (chips, rows, width))
+    return exchange(copies.reshape(-1, width), axes).reshape(chips, rows, width)
+
+
+def place_kernel(core_ref, mine_ref, other_ref, grad_w_ref, grad_v_ref, grad_b_ref, grad_c_ref, *, cut):
+    step = pl.program_id(0)
+    half = pl.num_programs(0) // 2
+    total = mine_ref.shape[1]
+    rows = total - SCALE_ROWS
+    first = core_ref[0] == 0
+    for i in range(mine_ref.shape[0]):
+        mine, other = mine_ref[i], other_ref[i]
+        low = jnp.where(first, mine, other)
+        high = jnp.where(first, other, mine)
+        low = low[0:rows] * jnp.exp2(low[rows:rows + 1] - 14.0)
+        high = high[0:rows] * jnp.exp2(high[rows:rows + 1] - 14.0)
+        early, late = i * cut, i * (rows - cut)
+        grad_c_ref[early:early + cut, :] = low[0:cut]
+        grad_w_ref[0, late:late + rows - cut, :] = low[cut:rows]
+        grad_w_ref[1, late:late + rows - cut, :] = high[cut:rows]
+
+        @pl.when(step < half)
+        def _():
+            grad_b_ref[early:early + cut, :] = high[0:cut]
+
+        @pl.when(step >= half)
+        def _():
+            grad_v_ref[early:early + cut, :] = high[0:cut]
+
+
+def place_call(core, mine, other, cut, channels, bins):
+    chips, total, width = mine.shape
+    late = total - SCALE_ROWS - cut
+    group = channels // cut
+    steps = chips // group
+    grid_spec = pltpu.PrefetchScalarGridSpec(
+        num_scalar_prefetch=1,
+        grid=(steps,),
+        in_specs=[pl.BlockSpec((group, total, width), lambda i, c: (i, 0, 0))] * 2,
+        out_specs=[
+            pl.BlockSpec((2, group * late, width), lambda i, c: (0, i, 0)),
+            pl.BlockSpec((channels, width), lambda i, c: (jnp.maximum(i - steps // 2, 0), 0)),
+            pl.BlockSpec((channels, width), lambda i, c: (0, jnp.minimum(i, steps // 2 - 1))),
+            pl.BlockSpec((channels, width), lambda i, c: (0, i)),
+        ],
+    )
+    return pl.pallas_call(
+        functools.partial(place_kernel, cut=cut),
+        grid_spec=grid_spec,
+        out_shape=[
+            jax.ShapeDtypeStruct((2, chips * late, width), F32),
+            jax.ShapeDtypeStruct((4 * channels, channels), F32),
+            jax.ShapeDtypeStruct((channels, 4 * channels), F32),
+            jax.ShapeDtypeStruct((channels, 4 * bins), F32),
+        ],
+        compiler_params=pltpu.CompilerParams(vmem_limit_bytes=VMEM_LIMIT),
+        name="place_gradients",
+    )(core, mine, other)
 
 
 def local(spectra, sensor_ids, permutation, w_enc1, w_enc2, w_dec1, w_dec2):
@@ -498,30 +627,20 @@
 
     sums = exchange(sums_call(spectra, sensor_ids), every)
     coef = exchange(stats_call(sums, windows, chunks, sensors, WIN_SENSOR * frames), every)
-    normed, pre, stat = enc1_call(permutation, spectra, coef, w_enc1, cols)
+    logs = sort_call(spectra)
+    normed, pre, stat = enc1_call(permutation, logs, coef, w_enc1, quarter, cols)
+    turned = turn_call(normed, windows // STEP_WINDOWS)
     stat = exchange(stat.reshape(cols * windows, 2 * channels), col_axes).reshape(cols, windows, 2 * channels)
     own, send, back, moment, moments = middle_call(
         permutation, core, normed, pre, stat, w_enc2, w_dec1, w_dec2, quarter, cols, total_windows)
     moments = exchange(moments.reshape(cols * windows, 2 * channels), col_axes).reshape(cols, windows, 2 * channels)
-    early = scatter_sum(own, send, chip_axes, chips)
-    own, send = grad_call(permutation, core, normed, pre, back, moment, moments, quarter, cols)
-    late = scatter_sum(own, send, chip_axes, chips)
-
-    def collect(piece):
-        mine = gather_rows(piece, chip_axes, chips)
-        other = swap_cores(mine)
-        first = jnp.where(core_index == 0, mine, other)
-        second = jnp.where(core_index == 0, other, mine)
-        return jnp.concatenate([first, second], axis=0)
-
-    early = collect(early)
-    grad_w = collect(late)
-    grad_c = early[0:4 * bins]
-    grad_b = early[4 * bins:4 * bins + 4 * channels]
-    grad_v = early[4 * bins + 4 * channels:]
-    grad_b = grad_b.reshape(4, channels, channels).transpose(1, 0, 2).reshape(channels, 4 * channels)
-    grad_c = grad_c.reshape(4 * bins // channels, channels, channels).transpose(1, 0, 2).reshape(channels, 4 * bins)
-    return (grad_w, grad_v, grad_b, grad_c)
+    late = grad_call(permutation, core, turned, pre, back, moment, moments, quarter, cols)
+    piece = owner_call(chip_sums([(own, send), late], chip_axes, chips))
+    mine = gather_rows(piece, chip_axes, chips)
+    other = swap_cores(mine)
+    grad_w, grad_v, grad_b, grad_c = place_call(
+        core, mine.astype(F32), other.astype(F32), own.shape[0] // chips, channels, bins)
+    return (grad_w.reshape(4 * bins, channels), grad_v, grad_b, grad_c)
 
 
 def solution(mesh):

time: 235 us -> 207 us (0.88)
  waiting for transfers between devices: 84.8 us -> 18.2 us
  blocking collectives: 51.9 us -> 85.5 us
  Pallas kernels: 46.2 us -> 74.5 us
  starting transfers between devices: 31.9 us -> 17 us
  local copies, waits for them, and re-layouts: 11 us -> 2.38 us
    all_to_all x5 -> x3, waiting for transfers between devices: 82.4 us -> 14.4 us  [exchange(): return lax.all_to_all(values, axes, split_axis=0, concat_axis=0, tiled=True)]
    all_to_all x3, blocking collectives: 51.9 us -> 85.5 us  [exchange(): return lax.all_to_all(values, axes, split_axis=0, concat_axis=0, tiled=True)]
    pallas_call x2 -> x6, Pallas kernels: 15.4 us -> 43.9 us  [the longest x1 11 us: turn_call(): pl.pallas_call(turn_kernel, grid=(classes, steps), in_specs=[pl.BlockSpec...]
    all_to_all x5 -> x3, starting transfers between devices: 25.1 us -> 12.2 us  [exchange(): return lax.all_to_all(values, axes, split_axis=0, concat_axis=0, tiled=True)]
    convert_element_type x2 -> x5, other arithmetic: 2.08 us -> 6.85 us  [the longest x1 2.13 us: local(): other.astype(F32)]
    unnamed x10 -> x8, local copies, waits for them, and re-layouts: 5.56 us -> 2.25 us
    select_n x2 -> x0, other arithmetic: 3.26 us -> none  [collect(): first = jnp.where(core_index == 0, mine, other)]
    broadcast_in_dim x2 -> x1, local copies, waits for them, and re-layouts: 2.67 us -> 0.13 us  [gather_rows(): jnp.broadcast_to(piece.astype(jnp.float16)[None], (chips, rows, width))]
  transfers between devices with their start and end apart: 9 -> 6, of which waited for: 6 -> 5; matrix products, arithmetic and copies ran while one was open for 2% -> 2% of each run, Pallas kernels for 4% -> 13%
where the time goes in v3:
time: 207 us; the launch traced here: 205 us
  blocking collectives  85.5 us (41%)
  Pallas kernels  74.5 us (36%)
  waiting for transfers between devices  18.2 us (9%)
  starting transfers between devices  17 us (8%)
  other arithmetic  6.95 us (3%)
  local copies, waits for them, and re-layouts  2.38 us (1%)
    all_to_all x3, blocking collectives, exchange(): return lax.all_to_all(values, axes, split_axis=0, concat_axis=0, tiled=True)  85.5 us
    pallas_call x1, Pallas kernels, middle_call(): pl.pallas_call(functools.partial(middle_kernel, quarter=quarter, cols=col...  20 us
    all_to_all x3, waiting for transfers between devices, exchange(): return lax.all_to_all(values, axes, split_axis=0, concat_axis=0, tiled=True)  14.4 us
    all_to_all x3, starting transfers between devices, exchange(): return lax.all_to_all(values, axes, split_axis=0, concat_axis=0, tiled=True)  12.2 us
    pallas_call x1, Pallas kernels, turn_call(): pl.pallas_call(turn_kernel, grid=(classes, steps), in_specs=[pl.BlockSpec...  11 us
    pallas_call x1, Pallas kernels, enc1_call(): pl.pallas_call(functools.partial(enc1_kernel, chunks=chunks, quarter=quar...  9.33 us
    pallas_call x1, Pallas kernels, place_call(): pl.pallas_call(functools.partial(place_kernel, cut=cut), grid_spec=grid_s...  8.25 us
    pallas_call x1, Pallas kernels, grad_call(): pl.pallas_call(functools.partial(grad_kernel, quarter=quarter, cols=cols)...  8.06 us
  transfers between devices with their start and end apart: 6, of which 5 were waited for; matrix products, arithmetic and copies ran while one was open for 2% of the time, Pallas kernels for 13%

profile of v3, /device:TPU:1, one launch (start us, length us, event | category | flops | bytes accessed | tf_op | source)
XLA Modules:
  0.0 205.3 jit_solution(17680730601381431070)
XLA Ops:
  0.6 5.9 %window_sums.1 = f32[256,128]{1,0:T(8,128)} custom-call(s32[16]{0:T(128)} %bitcast.17, bf16[16,256,512]{2,1,0:T(8,128)(2,1)} %spec_ref.3), custom_call_target="tpu_custom_call" | custom-call | tf_op jit(solution)/shard_map/window_sums/pallas_call | solution.py:102
  6.5 22.0 %all_to_all.46 = f32[128,2,128]{2,1,0:T(2,128)} all-to-all(f32[128,2,128]{2,1,0:T(2,128)} %bitcast.13), channel_id=1, replica_groups=mesh['row'=8,'pair'=8,'core'=2] {'row','pair','core'}, dimensions={0} | all-to-all | bytes 262144 | tf_op jit(solution)/shard_map/all_to_all | solution.py:519
  28.5 2.6 %sensor_stats.1 = f32[128,128]{1,0:T(8,128)} custom-call(f32[256,128]{1,0:T(8,128)} %bitcast.14), custom_call_target="tpu_custom_call" | custom-call | tf_op jit(solution)/shard_map/sensor_stats/pallas_call | solution.py:168
  31.1 4.1 %all-to-all-start.1 = ((f32[128,1,128]{2,1,0:T(1,128)}), f32[128,1,128]{2,1,0:T(1,128)S(1)}, u32[]{:S(2)}, u32[]{:S(2)}) async-start(f32[128,1,128]{2,1,0:T(1,128)} %bitcast.16), calls=%async_computation.1 | async-start | bytes 131072 | tf_op jit(solution)/shard_map/all_to_all | solution.py:519
  35.1 7.1 %sort_frames.1.log_ref = f32[4,1024,512]{2,1,0:T(8,128)} custom-call(bf16[16,256,512]{2,1,0:T(8,128)(2,1)} %spec_ref.3), custom_call_target="tpu_custom_call" | custom-call | flops 16777216 | bytes 12582912 | tf_op jit(solution)/shard_map/sort_frames/pallas_call | solution.py:135
  42.2 2.6 %all-to-all-done.1 = f32[128,1,128]{2,1,0:T(1,128)S(1)} async-done(((f32[128,1,128]{2,1,0:T(1,128)}), f32[128,1,128]{2,1,0:T(1,128)S(1)}, u32[]{:S(2)}, u32[]{:S(2)}) %all-to-all-start.1) | async-done | bytes 65568 | tf_op jit(solution)/shard_map/all_to_all | solution.py:519
  44.9 0.6 copy-done.3
  45.5 9.3 %normalize_enc1.1 = (bf16[4,1024,512]{2,1,0:T(8,128)(2,1)}, f32[2,1024,256]{2,1,0:T(8,128)}, f32[16,16,512]{2,1,0:T(8,128)}) custom-call(s32[16]{0:T(128)} %perm_ref.5, f32[4,1024,512]{2,1,0:T(8,128)} %sort_frames.1.log_ref, f32[128,128]{1,0:T(8,128)} %bitcast.15, bf16[2048,256]{1,0:T(8,128)(2,1)} %w_ref.1), custom_call_target="tpu_custom_call" | custom-call | tf_op jit(solution)/shard_map/normalize_enc1/pallas_call | solution.py:246
  54.8 4.6 %all-to-all-start.2 = ((f32[16,16,512]{2,1,0:T(8,128)}), f32[16,16,512]{2,1,0:T(8,128)S(1)}, u32[]{:S(2)}, u32[]{:S(2)}) async-start(f32[16,16,512]{2,1,0:T(8,128)} %get-tuple-element.20), calls=%async_computation.2 | async-start | bytes 1048576 | tf_op jit(solution)/shard_map/all_to_all | solution.py:519
  59.4 11.4 %all-to-all-done.2.stat_ref = f32[16,16,512]{2,1,0:T(8,128)S(1)} async-done(((f32[16,16,512]{2,1,0:T(8,128)}), f32[16,16,512]{2,1,0:T(8,128)S(1)}, u32[]{:S(2)}, u32[]{:S(2)}) %all-to-all-start.2) | async-done | bytes 524320 | tf_op jit(solution)/shard_map/all_to_all | solution.py:519
  70.8 0.8 copy-done
  71.6 20.0 %middle.1 = (f32[2048,256]{1,0:T(8,128)}, f32[2048,256]{1,0:T(8,128)}, f32[2,1024,256]{2,1,0:T(8,128)}, f32[16,512]{1,0:T(8,128)}, f32[16,16,512]{2,1,0:T(8,128)}) custom-call(s32[16]{0:T(128)} %perm_ref.5, s32[1]{0:T(128)} %bitcast.core_ref, bf16[4,1024,512]{2,1,0:T(8,128)(2,1)} %get-tuple-element.18.normed_ref.in_ref, ...), custom_call_target="tpu_custom_call" | custom-call | tf_op jit(solution)/shard_map/middle/pallas_call | solution.py:435
  91.6 1.2 collective-permute-start
  92.7 3.5 %all-to-all-start.3 = ((f32[16,16,512]{2,1,0:T(8,128)}), f32[16,16,512]{2,1,0:T(8,128)S(1)}, u32[]{:S(2)}, u32[]{:S(2)}) async-start(f32[16,16,512]{2,1,0:T(8,128)} %get-tuple-element.25), calls=%async_computation.3 | async-start | bytes 1048576 | tf_op jit(solution)/shard_map/all_to_all | solution.py:519
  96.2 11.0 %turn_normed.1.turned_ref = bf16[4,512,1024]{2,1,0:T(8,128)(2,1)} custom-call(bf16[4,1024,512]{2,1,0:T(8,128)(2,1)} %get-tuple-element.18.normed_ref.in_ref), custom_call_target="tpu_custom_call" | custom-call | flops 8388608 | bytes 8388608 | tf_op jit(solution)/shard_map/turn_normed/pallas_call | solution.py:267
  107.2 0.4 all-to-all-done.3.sums_ref
  107.6 0.8 copy-done.1
  108.5 8.1 %grad_enc1.1 = (f32[1024,256]{1,0:T(8,128)}, f32[1024,256]{1,0:T(8,128)}) custom-call(s32[16]{0:T(128)} %perm_ref.5, s32[1]{0:T(128)} %bitcast.core_ref, bf16[4,512,1024]{2,1,0:T(8,128)(2,1)} %turn_normed.1.turned_ref, f32[2,1024,256]{2,1,0:T(8,128)} %get-tuple-element.19.pre_ref, f32[2,1024,256]{2,1,0:T(8,128)} %get-tuple-element.23.back_ref, ...), custom_call_target="tpu_custom_call" | custom-call | tf_op jit(solution)/shard_map/grad_enc1/pallas_call | solution.py:505
  116.5 1.1 collective-permute-start.1
  117.6 2.5 %collective-permute-done.1 = f32[1024,256]{1,0:T(8,128)S(1)} collective-permute-done((f32[1024,256]{1,0:T(8,128)}, f32[1024,256]{1,0:T(8,128)S(1)}, u32[]{:S(2)}, u32[]{:S(2)}) %collective-permute-start.1) | collective-permute-done | bytes 1048608 | tf_op jit(solution)/shard_map/ppermute | solution.py:515
  120.1 1.3 add_convert_fusion.1
  121.4 0.5 add_convert_fusion
  122.0 32.3 %all_to_all.47.in_ref = bf16[64,48,256]{2,1,0:T(8,128)(2,1)} all-to-all(bf16[64,48,256]{2,1,0:T(8,128)(2,1)S(1)} %pad_maximum_fusion), channel_id=1, replica_groups=mesh['row'=8,'pair'=8,'core'=2] {'row','pair'}, dimensions={0} | all-to-all | bytes 3145728 | tf_op jit(solution)/shard_map/all_to_all | solution.py:519
  154.3 2.4 %owner_sum.1 = f32[56,256]{1,0:T(8,128)} custom-call(bf16[64,48,256]{2,1,0:T(8,128)(2,1)} %all_to_all.47.in_ref), custom_call_target="tpu_custom_call" | custom-call | tf_op jit(solution)/shard_map/owner_sum/pallas_call | solution.py:543
  156.7 0.8 convert_element_type.17
  157.5 0.1 broadcast_in_dim.2
  157.6 31.2 %all_to_all.48 = f16[64,56,256]{2,1,0:T(8,128)(2,1)S(1)} all-to-all(f16[64,56,256]{2,1,0:T(8,128)(2,1)S(1)} %broadcast_in_dim.2), channel_id=1, replica_groups=mesh['row'=8,'pair'=8,'core'=2] {'row','pair'}, dimensions={0} | all-to-all | bytes 3670016 | tf_op jit(solution)/shard_map/all_to_all | solution.py:519
  188.9 2.6 %collective-permute-start.2 = (f16[64,56,256]{2,1,0:T(8,128)(2,1)S(1)}, f16[64,56,256]{2,1,0:T(8,128)(2,1)S(1)}, u32[]{:S(2)}, u32[]{:S(2)}) collective-permute-start(f16[64,56,256]{2,1,0:T(8,128)(2,1)S(1)} %all_to_all.48), channel_id=1, source_target_pairs={{0,1},{1,0},{2,3},{3,2},{4,5},{5,4},{6,7},{7,6},{8,9},{9,8},{10,11... | collective-permute-start | bytes 5505032 | tf_op jit(solution)/shard_map/ppermute | solution.py:515
  191.5 2.1 %convert_element_type.18.mine_ref = f32[64,56,256]{2,1,0:T(8,128)} convert(f16[64,56,256]{2,1,0:T(8,128)(2,1)S(1)} %all_to_all.48) | non-fusion elementwise | flops 917504 | bytes 5505024 | tf_op jit(solution)/shard_map/convert_element_type | solution.py:642
  193.6 1.3 collective-permute-done.2
  194.9 2.1 %convert_element_type.19.other_ref = f32[64,56,256]{2,1,0:T(8,128)} convert(f16[64,56,256]{2,1,0:T(8,128)(2,1)S(1)} %collective-permute-done.2) | non-fusion elementwise | flops 917504 | bytes 5505024 | tf_op jit(solution)/shard_map/convert_element_type | solution.py:642
  197.0 8.2 %place_gradients.1 = (f32[2,1024,256]{2,1,0:T(8,128)}, f32[1024,256]{1,0:T(8,128)}, f32[256,1024]{1,0:T(8,128)}, f32[256,2048]{1,0:T(8,128)}) custom-call(s32[1]{0:T(128)} %bitcast.core_ref, f32[64,56,256]{2,1,0:T(8,128)} %convert_element_type.18.mine_ref, f32[64,56,256]{2,1,0:T(8,128)} %convert_element_type.19.other_ref), custom_call_target="tpu_custom_call" | custom-call | tf_op jit(solution)/shard_map/place_gradients/pallas_call | solution.py:599
  (7 shorter events, 0.1 us)
Async XLA Ops:
  31.1 13.8 %all-to-all-start.1 = ((f32[128,1,128]{2,1,0:T(1,128)}), f32[128,1,128]{2,1,0:T(1,128)S(1)}, u32[]{:S(2)}, u32[]{:S(2)}) async-start(f32[128,1,128]{2,1,0:T(1,128)} %bitcast.16), calls=%async_computation.1 | async-start | bytes 131072 | tf_op jit(solution)/shard_map/all_to_all | solution.py:519
  44.8 0.6 copy-start.3
  54.8 16.0 %all-to-all-start.2 = ((f32[16,16,512]{2,1,0:T(8,128)}), f32[16,16,512]{2,1,0:T(8,128)S(1)}, u32[]{:S(2)}, u32[]{:S(2)}) async-start(f32[16,16,512]{2,1,0:T(8,128)} %get-tuple-element.20), calls=%async_computation.2 | async-start | bytes 1048576 | tf_op jit(solution)/shard_map/all_to_all | solution.py:519
  70.8 0.8 copy-start
  91.6 29.8 %collective-permute-start = (f32[2048,256]{1,0:T(8,128)}, f32[2048,256]{1,0:T(8,128)S(1)}, u32[]{:S(2)}, u32[]{:S(2)}) collective-permute-start(f32[2048,256]{1,0:T(8,128)} %get-tuple-element.22), channel_id=1, source_target_pairs={{0,1},{1,0},{2,3},{3,2},{4,5},{5,4},{6,7},{7,6},{8,9},{9,8},{10,11... | collective-permute-start | bytes 6291464 | tf_op jit(solution)/shard_map/ppermute | solution.py:515
  92.7 14.9 %all-to-all-start.3 = ((f32[16,16,512]{2,1,0:T(8,128)}), f32[16,16,512]{2,1,0:T(8,128)S(1)}, u32[]{:S(2)}, u32[]{:S(2)}) async-start(f32[16,16,512]{2,1,0:T(8,128)} %get-tuple-element.25), calls=%async_computation.3 | async-start | bytes 1048576 | tf_op jit(solution)/shard_map/all_to_all | solution.py:519
  107.6 0.8 copy-start.1
  116.5 4.9 %copy-start.2 = (f32[2048,256]{1,0:T(8,128)S(1)}, f32[2048,256]{1,0:T(8,128)}, u32[]{:S(2)}) copy-start(f32[2048,256]{1,0:T(8,128)} %get-tuple-element.21) | copy-start | bytes 6291460
  116.5 3.6 %collective-permute-start.1 = (f32[1024,256]{1,0:T(8,128)}, f32[1024,256]{1,0:T(8,128)S(1)}, u32[]{:S(2)}, u32[]{:S(2)}) collective-permute-start(f32[1024,256]{1,0:T(8,128)} %get-tuple-element.27), channel_id=1, source_target_pairs={{0,1},{1,0},{2,3},{3,2},{4,5},{5,4},{6,7},{7,6},{8,9},{9,8},{10,11... | collective-permute-start | bytes 3145736 | tf_op jit(solution)/shard_map/ppermute | solution.py:515
  188.9 6.1 %collective-permute-start.2 = (f16[64,56,256]{2,1,0:T(8,128)(2,1)S(1)}, f16[64,56,256]{2,1,0:T(8,128)(2,1)S(1)}, u32[]{:S(2)}, u32[]{:S(2)}) collective-permute-start(f16[64,56,256]{2,1,0:T(8,128)(2,1)S(1)} %all_to_all.48), channel_id=1, source_target_pairs={{0,1},{1,0},{2,3},{3,2},{4,5},{5,4},{6,7},{7,6},{8,9},{9,8},{10,11... | collective-permute-start | bytes 5505032 | tf_op jit(solution)/shard_map/ppermute | solution.py:515

commit v4 on v3

--- a/solution.py
+++ b/solution.py
@@ -12,9 +12,21 @@
 F32 = jnp.float32
 BF16 = jnp.bfloat16
 LANES = 128
-STEP_WINDOWS = 4
+STEP_WINDOWS = 8
+SORT_WINDOWS = 4
 SCALE_ROWS = 8
-VMEM_LIMIT = 56 * 1024 * 1024
+MIB = 1024 * 1024
+
+
+ON_CHIP = pl.BlockSpec(memory_space=pltpu.VMEM)
+
+
+def on_chip(values):
+    return pltpu.with_memory_space_constraint(values, pltpu.VMEM)
+
+
+def step_rows(ref, rows):
+    return ref.at[:, pl.ds(pl.multiple_of(pl.program_id(0) * rows, rows), rows), :]
 
 
 def dot(left, right):
@@ -58,16 +70,20 @@
     return (trainer // col_count) * per_row + trainer % per_row
 
 
-def sums_kernel(ids_ref, spec_ref, out_ref, acc, *, chunks, count):
+def sums_kernel(ids_ref, spec_ref, log_ref, out_ref, acc, lane, *, chunks, count):
     step = pl.program_id(0)
     windows, frames, bins = spec_ref.shape
+    quarter = frames // 4
     rows = 16
+    log_ref = step_rows(log_ref, windows * quarter)
 
     for w in range(windows):
         def body(i, carry):
             total, square = carry
             start = pl.multiple_of(i * rows, rows)
             value = jnp.log(1.0 + spec_ref[w, pl.ds(start, rows), :].astype(F32))
+            for k in range(chunks):
+                lane[w % 2, k, pl.ds(start, rows), :] = value[:, k * LANES:(k + 1) * LANES]
             value_sq = value * value
             return (total + value[0:8] + value[8:16], square + value_sq[0:8] + value_sq[8:16])
 
@@ -79,6 +95,9 @@
         pieces += [square[:, k * LANES:(k + 1) * LANES] for k in range(chunks)]
         start = pl.multiple_of((step * windows + w) * 2 * chunks, 2 * chunks)
         acc[pl.ds(start, 2 * chunks), :] = jnp.concatenate(pieces, axis=0)
+        for i in range(4):
+            for k in range(chunks):
+                log_ref[i, w * quarter:(w + 1) * quarter, k * LANES:(k + 1) * LANES] = lane[w % 2, k, pl.ds(i, quarter, stride=4), :]
 
     @pl.when(step == pl.num_programs(0) - 1)
     def _():
@@ -94,55 +113,21 @@
     chunks = bins // LANES
     grid_spec = pltpu.PrefetchScalarGridSpec(
         num_scalar_prefetch=1,
-        grid=(windows // STEP_WINDOWS,),
-        in_specs=[pl.BlockSpec((STEP_WINDOWS, frames, bins), lambda i, s: (i, 0, 0))],
-        out_specs=pl.BlockSpec((2 * LANES, LANES), lambda i, s: (0, 0)),
-        scratch_shapes=[pltpu.VMEM((2 * LANES, LANES), F32)],
+        grid=(windows // SORT_WINDOWS,),
+        in_specs=[pl.BlockSpec((SORT_WINDOWS, frames, bins), lambda i, s: (i, 0, 0))],
+        out_specs=[ON_CHIP, pl.BlockSpec((2 * LANES, LANES), lambda i, s: (0, 0))],
+        scratch_shapes=[pltpu.VMEM((2 * LANES, LANES), F32), pltpu.VMEM((2, chunks, frames, LANES), F32)],
     )
     return pl.pallas_call(
         functools.partial(sums_kernel, chunks=chunks, count=windows),
         grid_spec=grid_spec,
-        out_shape=jax.ShapeDtypeStruct((2 * LANES, LANES), F32),
-        compiler_params=pltpu.CompilerParams(vmem_limit_bytes=VMEM_LIMIT),
-        name="window_sums",
-    )(sensor_ids.reshape(windows), spectra)
-
-
-def sort_kernel(spec_ref, out_ref, lane, *, chunks):
-    windows, frames, bins = spec_ref.shape
-    quarter = frames // 4
-    rows = 32
-    for w in range(windows):
-        def body(i, carry):
-            at = pl.multiple_of(i * rows, rows)
-            value = jnp.log(1.0 + spec_ref[w, pl.ds(at, rows), :].astype(F32))
-            for k in range(chunks):
-                lane[w % 2, k, pl.ds(at, rows), :] = value[:, k * LANES:(k + 1) * LANES]
-            return carry
-
-        lax.fori_loop(0, frames // rows, body, 0, unroll=2)
-        for i in range(4):
-            for k in range(chunks):
-                out_ref[i, w * quarter:(w + 1) * quarter, k * LANES:(k + 1) * LANES] = lane[w % 2, k, pl.ds(i, quarter, stride=4), :]
-
-
-def sort_call(spectra):
-    windows, frames, bins = spectra.shape
-    chunks = bins // LANES
-    quarter = frames // 4
-    rows = STEP_WINDOWS * quarter
-    size = windows * frames * bins
-    return pl.pallas_call(
-        functools.partial(sort_kernel, chunks=chunks),
-        grid=(windows // STEP_WINDOWS,),
-        in_specs=[pl.BlockSpec((STEP_WINDOWS, frames, bins), lambda i: (i, 0, 0))],
-        out_specs=pl.BlockSpec((4, rows, bins), lambda i: (0, i, 0)),
-        out_shape=jax.ShapeDtypeStruct((4, windows * quarter, bins), F32),
-        scratch_shapes=[pltpu.VMEM((2, chunks, frames, LANES), F32)],
-        compiler_params=pltpu.CompilerParams(vmem_limit_bytes=VMEM_LIMIT),
-        cost_estimate=pl.CostEstimate(flops=8 * size, bytes_accessed=6 * size, transcendentals=size),
-        name="sort_frames",
-    )(spectra)
+        out_shape=[
+            pltpu.VMEM((4, windows * frames // 4, bins), F32),
+            jax.ShapeDtypeStruct((2 * LANES, LANES), F32),
+        ],
+        compiler_params=pltpu.CompilerParams(vmem_limit_bytes=10 * MIB),
+        name="sort_and_sum",
+    )(sensor_ids.reshape(windows), pltpu.with_memory_space_constraint(spectra, pltpu.HBM))
 
 
 def stats_kernel(in_ref, out_ref, *, windows, chunks, sensors, per_sensor):
@@ -168,7 +153,7 @@
     return pl.pallas_call(
         functools.partial(stats_kernel, windows=windows, chunks=chunks, sensors=sensors, per_sensor=float(per_sensor)),
         out_shape=jax.ShapeDtypeStruct((LANES, LANES), F32),
-        compiler_params=pltpu.CompilerParams(vmem_limit_bytes=VMEM_LIMIT),
+        compiler_params=pltpu.CompilerParams(vmem_limit_bytes=12 * MIB),
         name="sensor_stats",
     )(received)
 
@@ -176,7 +161,8 @@
 def enc1_kernel(perm_ref, log_ref, coef_ref, w_ref, normed_ref, pre_ref, stat_ref, coef, stat, *, chunks, quarter, cols, copies):
     step = pl.program_id(0)
     bins = log_ref.shape[2]
-    windows = log_ref.shape[1] // quarter
+    windows = STEP_WINDOWS
+    log_ref, normed_ref, pre_ref = (step_rows(ref, windows * quarter) for ref in (log_ref, normed_ref, pre_ref))
     channels = w_ref.shape[1]
     all_windows = windows * pl.num_programs(0)
     width = 2 * chunks
@@ -224,18 +210,17 @@
     windows = logs.shape[1] // quarter
     chunks = bins // LANES
     channels = w_enc1.shape[1]
-    rows = STEP_WINDOWS * quarter
     grid_spec = pltpu.PrefetchScalarGridSpec(
         num_scalar_prefetch=1,
         grid=(windows // STEP_WINDOWS,),
         in_specs=[
-            pl.BlockSpec((4, rows, bins), lambda i, p: (0, i, 0)),
+            ON_CHIP,
             pl.BlockSpec((LANES, LANES), lambda i, p: (0, 0)),
             pl.BlockSpec(w_enc1.shape, lambda i, p: (0, 0)),
         ],
         out_specs=[
-            pl.BlockSpec((4, rows, bins), lambda i, p: (0, i, 0)),
-            pl.BlockSpec((2, rows, channels), lambda i, p: (0, i, 0)),
+            ON_CHIP,
+            ON_CHIP,
             pl.BlockSpec((cols, windows, 2 * channels), lambda i, p: (0, 0, 0)),
         ],
         scratch_shapes=[
@@ -247,33 +232,13 @@
         functools.partial(enc1_kernel, chunks=chunks, quarter=quarter, cols=cols, copies=cols),
         grid_spec=grid_spec,
         out_shape=[
-            jax.ShapeDtypeStruct((4, windows * quarter, bins), BF16),
-            jax.ShapeDtypeStruct((2, windows * quarter, channels), F32),
+            pltpu.VMEM((4, windows * quarter, bins), BF16),
+            pltpu.VMEM((2, windows * quarter, channels), F32),
             jax.ShapeDtypeStruct((cols, windows, 2 * channels), F32),
         ],
-        compiler_params=pltpu.CompilerParams(vmem_limit_bytes=VMEM_LIMIT),
+        compiler_params=pltpu.CompilerParams(vmem_limit_bytes=16 * MIB),
         name="normalize_enc1",
-    )(permutation, logs, coef, w_enc1)
-
-
-def turn_kernel(in_ref, out_ref):
-    out_ref[0] = in_ref[0].T
-
-
-def turn_call(normed, steps):
-    classes, total, bins = normed.shape
-    rows = total // steps
-    size = classes * total * bins
-    return pl.pallas_call(
-        turn_kernel,
-        grid=(classes, steps),
-        in_specs=[pl.BlockSpec((1, rows, bins), lambda i, j: (i, j, 0))],
-        out_specs=pl.BlockSpec((1, bins, rows), lambda i, j: (i, 0, j)),
-        out_shape=jax.ShapeDtypeStruct((classes, bins, total), normed.dtype),
-        compiler_params=pltpu.CompilerParams(vmem_limit_bytes=VMEM_LIMIT),
-        cost_estimate=pl.CostEstimate(flops=4 * size, bytes_accessed=4 * size, transcendentals=0),
-        name="turn_normed",
-    )(normed)
+    )(permutation, on_chip(logs), coef, w_enc1)
 
 
 def window_rows(perm_ref, table, step, windows, quarter, all_windows, cols, first, last):
@@ -296,8 +261,8 @@
     step = pl.program_id(0)
     channels = v_ref.shape[1]
     bins = normed_ref.shape[2]
-    rows = normed_ref.shape[1]
-    windows = rows // quarter
+    windows = STEP_WINDOWS
+    normed_ref, pre_ref, back_ref = (step_rows(ref, windows * quarter) for ref in (normed_ref, pre_ref, back_ref))
     all_windows = windows * pl.num_programs(0)
     ch = channels
 
@@ -404,7 +369,6 @@
     bins = normed.shape[2]
     channels = w_enc2.shape[1]
     windows = normed.shape[1] // quarter
-    rows = STEP_WINDOWS * quarter
     total = 4 * bins + 8 * channels
     whole2 = lambda i, p, c: (0, 0)
     whole3 = lambda i, p, c: (0, 0, 0)
@@ -412,8 +376,8 @@
         num_scalar_prefetch=2,
         grid=(windows // STEP_WINDOWS,),
         in_specs=[
-            pl.BlockSpec((4, rows, bins), lambda i, p, c: (0, i, 0)),
-            pl.BlockSpec((2, rows, channels), lambda i, p, c: (0, i, 0)),
+            ON_CHIP,
+            ON_CHIP,
             pl.BlockSpec(stat.shape, whole3),
             pl.BlockSpec(w_enc2.shape, whole2),
             pl.BlockSpec(w_dec1.shape, whole2),
@@ -422,7 +386,7 @@
         out_specs=[
             pl.BlockSpec((total // 2, channels), whole2),
             pl.BlockSpec((total // 2, channels), whole2),
-            pl.BlockSpec((2, rows, channels), lambda i, p, c: (0, i, 0)),
+            ON_CHIP,
             pl.BlockSpec((windows, 2 * channels), whole2),
             pl.BlockSpec(stat.shape, whole3),
         ],
@@ -438,21 +402,23 @@
         out_shape=[
             jax.ShapeDtypeStruct((total // 2, channels), F32),
             jax.ShapeDtypeStruct((total // 2, channels), F32),
-            jax.ShapeDtypeStruct(pre.shape, F32),
+            pltpu.VMEM(pre.shape, F32),
             jax.ShapeDtypeStruct((windows, 2 * channels), F32),
             jax.ShapeDtypeStruct(stat.shape, F32),
         ],
-        compiler_params=pltpu.CompilerParams(vmem_limit_bytes=VMEM_LIMIT),
+        compiler_params=pltpu.CompilerParams(vmem_limit_bytes=36 * MIB),
         name="middle",
-    )(permutation, core, normed, pre, stat, w_enc2, w_dec1, w_dec2)
-
-
-def grad_kernel(perm_ref, core_ref, turned_ref, pre_ref, back_ref, moment_ref, sums_ref, own_ref, send_ref, grads, scale, *, quarter, cols):
+    )(permutation, core, on_chip(normed), on_chip(pre), stat, w_enc2, w_dec1, w_dec2)
+
+
+def grad_kernel(perm_ref, core_ref, normed_ref, pre_ref, back_ref, moment_ref, sums_ref, own_ref, send_ref, grads, scale, *, quarter, cols):
     step = pl.program_id(0)
-    bins = turned_ref.shape[1]
-    rows = turned_ref.shape[2]
+    bins = normed_ref.shape[2]
     ch = pre_ref.shape[2]
-    windows = rows // quarter
+    windows = STEP_WINDOWS
+    rows = windows * quarter
+    normed_ref = step_rows(normed_ref, rows)
+    pre_ref, back_ref = step_rows(pre_ref, rows), step_rows(back_ref, rows)
     all_windows = windows * pl.num_programs(0)
 
     @pl.when(step == 0)
@@ -473,29 +439,28 @@
     do = do32.astype(BF16)
     de_up = shift_up(de32, quarter).astype(BF16)
     do_down = shift_down(do32, quarter).astype(BF16)
-    f0, f1, f2, f3 = (turned_ref[i] for i in range(4))
-    grads[0:bins, :] += dot(f3, de_up) + dot(f1, do)
-    grads[bins:2 * bins, :] += dot(f0, de) + dot(f2, do)
-    grads[2 * bins:3 * bins, :] += dot(f1, de) + dot(f3, do)
-    grads[3 * bins:4 * bins, :] += dot(f2, de) + dot(f0, do_down)
+    f0, f1, f2, f3 = (normed_ref[i] for i in range(4))
+    grads[0:bins, :] += dot_tn(f3, de_up) + dot_tn(f1, do)
+    grads[bins:2 * bins, :] += dot_tn(f0, de) + dot_tn(f2, do)
+    grads[2 * bins:3 * bins, :] += dot_tn(f1, de) + dot_tn(f3, do)
+    grads[3 * bins:4 * bins, :] += dot_tn(f2, de) + dot_tn(f0, do_down)
 
     @pl.when(step == pl.num_programs(0) - 1)
     def _():
         write_halves(core_ref, grads, own_ref, send_ref)
 
 
-def grad_call(permutation, core, turned, pre, back, moment, sums, quarter, cols):
-    bins = turned.shape[1]
+def grad_call(permutation, core, normed, pre, back, moment, sums, quarter, cols):
+    bins = normed.shape[2]
     channels = pre.shape[2]
-    windows = turned.shape[2] // quarter
-    rows = STEP_WINDOWS * quarter
+    windows = normed.shape[1] // quarter
     grid_spec = pltpu.PrefetchScalarGridSpec(
         num_scalar_prefetch=2,
         grid=(windows // STEP_WINDOWS,),
         in_specs=[
-            pl.BlockSpec((4, bins, rows), lambda i, p, c: (0, 0, i)),
-            pl.BlockSpec((2, rows, channels), lambda i, p, c: (0, i, 0)),
-            pl.BlockSpec((2, rows, channels), lambda i, p, c: (0, i, 0)),
+            ON_CHIP,
+            ON_CHIP,
+            ON_CHIP,
             pl.BlockSpec(moment.shape, lambda i, p, c: (0, 0)),
             pl.BlockSpec(sums.shape, lambda i, p, c: (0, 0, 0)),
         ],
@@ -506,9 +471,9 @@
         functools.partial(grad_kernel, quarter=quarter, cols=cols),
         grid_spec=grid_spec,
         out_shape=[jax.ShapeDtypeStruct((2 * bins, channels), F32)] * 2,
-        compiler_params=pltpu.CompilerParams(vmem_limit_bytes=VMEM_LIMIT),
+        compiler_params=pltpu.CompilerParams(vmem_limit_bytes=16 * MIB),
         name="grad_enc1",
-    )(permutation, core, turned, pre, back, moment, sums)
+    )(permutation, core, on_chip(normed), on_chip(pre), on_chip(back), moment, sums)
 
 
 def swap_cores(values):
@@ -543,7 +508,7 @@
     return pl.pallas_call(
         owner_kernel,
         out_shape=jax.ShapeDtypeStruct((rows + SCALE_ROWS, width), F32),
-        compiler_params=pltpu.CompilerParams(vmem_limit_bytes=VMEM_LIMIT),
+        compiler_params=pltpu.CompilerParams(vmem_limit_bytes=6 * MIB),
         name="owner_sum",
     )(pieces)
 
@@ -605,7 +570,7 @@
             jax.ShapeDtypeStruct((channels, 4 * channels), F32),
             jax.ShapeDtypeStruct((channels, 4 * bins), F32),
         ],
-        compiler_params=pltpu.CompilerParams(vmem_limit_bytes=VMEM_LIMIT),
+        compiler_params=pltpu.CompilerParams(vmem_limit_bytes=12 * MIB),
         name="place_gradients",
     )(core, mine, other)
 
@@ -625,16 +590,16 @@
     core_index = lax.axis_index("core")
     core = core_index.astype(jnp.int32).reshape(1)
 
-    sums = exchange(sums_call(spectra, sensor_ids), every)
+    logs, sums = sums_call(spectra, sensor_ids)
+    sums, core = lax.optimization_barrier((sums, core))
+    sums = exchange(sums, every)
     coef = exchange(stats_call(sums, windows, chunks, sensors, WIN_SENSOR * frames), every)
-    logs = sort_call(spectra)
     normed, pre, stat = enc1_call(permutation, logs, coef, w_enc1, quarter, cols)
-    turned = turn_call(normed, windows // STEP_WINDOWS)
     stat = exchange(stat.reshape(cols * windows, 2 * channels), col_axes).reshape(cols, windows, 2 * channels)
     own, send, back, moment, moments = middle_call(
         permutation, core, normed, pre, stat, w_enc2, w_dec1, w_dec2, quarter, cols, total_windows)
     moments = exchange(moments.reshape(cols * windows, 2 * channels), col_axes).reshape(cols, windows, 2 * channels)
-    late = grad_call(permutation, core, turned, pre, back, moment, moments, quarter, cols)
+    late = grad_call(permutation, core, normed, pre, back, moment, moments, quarter, cols)
     piece = owner_call(chip_sums([(own, send), late], chip_axes, chips))
     mine = gather_rows(piece, chip_axes, chips)
     other = swap_cores(mine)

time: 207 us -> 168 us (0.81)
  Pallas kernels: 74.5 us -> 32.4 us
  blocking collectives: 85.5 us -> 122 us
  waiting for transfers between devices: 18.2 us -> 5.41 us
  starting transfers between devices: 17 us -> 4.98 us
  other arithmetic: 6.95 us -> 1.24 us
    all_to_all x3 -> x6, blocking collectives: 85.5 us -> 122 us  [exchange(): return lax.all_to_all(values, axes, split_axis=0, concat_axis=0, tiled=True)]
    pallas_call x2 -> x0, Pallas kernels: 18.1 us -> none  [the longest x1 11 us: turn_call(): pl.pallas_call(turn_kernel, grid=(classes, steps), in_specs=[pl.BlockSpec...]
    all_to_all x3 -> x0, waiting for transfers between devices: 14.4 us -> none  [exchange(): return lax.all_to_all(values, axes, split_axis=0, concat_axis=0, tiled=True)]
    all_to_all x3 -> x0, starting transfers between devices: 12.2 us -> none  [exchange(): return lax.all_to_all(values, axes, split_axis=0, concat_axis=0, tiled=True)]
    pallas_call x1, Pallas kernels: 20 us -> 13.6 us  [middle_call(): pl.pallas_call(functools.partial(middle_kernel, quarter=quarter, cols=col...]
    pallas_call x1, Pallas kernels: 9.33 us -> 3.79 us  [enc1_call(): pl.pallas_call(functools.partial(enc1_kernel, chunks=chunks, quarter=quar...]
    pallas_call x1, Pallas kernels: 8.06 us -> 3.74 us  [grad_call(): pl.pallas_call(functools.partial(grad_kernel, quarter=quarter, cols=cols)...]
    pallas_call x1, Pallas kernels: 8.25 us -> 4.48 us  [place_call(): pl.pallas_call(functools.partial(place_kernel, cut=cut), grid_spec=grid_s...]
  transfers between devices with their start and end apart: 6 -> 3, of which waited for: 5 -> 2; matrix products, arithmetic and copies ran while one was open for 2% -> 0% of each run, Pallas kernels for 13% -> 2%
where the time goes in v4:
time: 168 us
  blocking collectives  122 us (73%)
  Pallas kernels  32.4 us (19%)
  waiting for transfers between devices  5.41 us (3%)
  starting transfers between devices  4.98 us (3%)
    all_to_all x6, blocking collectives, exchange(): return lax.all_to_all(values, axes, split_axis=0, concat_axis=0, tiled=True)  122 us
    pallas_call x1, Pallas kernels, middle_call(): pl.pallas_call(functools.partial(middle_kernel, quarter=quarter, cols=col...  13.6 us
    ppermute x3, waiting for transfers between devices, swap_cores(): return lax.ppermute(values, 'core', [(0, 1), (1, 0)])  5.41 us
    pallas_call x1, Pallas kernels, sums_call(): pl.pallas_call(functools.partial(sums_kernel, chunks=chunks, count=window...  5.39 us
    ppermute x3, starting transfers between devices, swap_cores(): return lax.ppermute(values, 'core', [(0, 1), (1, 0)])  4.98 us
    pallas_call x1, Pallas kernels, place_call(): pl.pallas_call(functools.partial(place_kernel, cut=cut), grid_spec=grid_s...  4.48 us
    pallas_call x1, Pallas kernels, enc1_call(): pl.pallas_call(functools.partial(enc1_kernel, chunks=chunks, quarter=quar...  3.79 us
    pallas_call x1, Pallas kernels, grad_call(): pl.pallas_call(functools.partial(grad_kernel, quarter=quarter, cols=cols)...  3.74 us
  transfers between devices with their start and end apart: 3, of which 2 were waited for; matrix products, arithmetic and copies ran while one was open for 0% of the time, Pallas kernels for 2%

profile of v4, /device:TPU:1, one launch (start us, length us, event | category | flops | bytes accessed | tf_op | source)
XLA Modules:
  0.0 167.6 jit_solution(9540965906252282337)
XLA Ops:
  0.6 0.0 copy-start.5
  0.6 0.6 copy-done.5
  1.3 5.4 %sort_and_sum.1 = (f32[4,1024,512]{2,1,0:T(8,128)S(1)}, f32[256,128]{1,0:T(8,128)S(1)}) custom-call(s32[16]{0:T(128)S(1)} %bitcast.15, bf16[16,256,512]{2,1,0:T(8,128)(2,1)} %spec_ref.1), custom_call_target="tpu_custom_call" | custom-call | tf_op jit(solution)/shard_map/sort_and_sum/pallas_call | solution.py:121
  6.7 21.6 %all_to_all.46 = f32[128,2,128]{2,1,0:T(2,128)S(1)} all-to-all(f32[128,2,128]{2,1,0:T(2,128)S(1)} %bitcast.14), channel_id=1, replica_groups=mesh['row'=8,'pair'=8,'core'=2] {'row','pair','core'}, dimensions={0} | all-to-all | bytes 262144 | tf_op jit(solution)/shard_map/all_to_all | solution.py:484
  28.3 1.1 sensor_stats.1
  29.3 13.6 %all_to_all.47 = f32[128,1,128]{2,1,0:T(1,128)S(1)} all-to-all(f32[128,1,128]{2,1,0:T(1,128)S(1)} %bitcast.13), channel_id=1, replica_groups=mesh['row'=8,'pair'=8,'core'=2] {'row','pair','core'}, dimensions={0} | all-to-all | bytes 131072 | tf_op jit(solution)/shard_map/all_to_all | solution.py:484
  43.0 0.0 copy-done
  43.0 0.0 copy-done.4
  43.0 0.0 copy-start.3
  43.0 3.8 %normalize_enc1.1 = (bf16[4,1024,512]{2,1,0:T(8,128)(2,1)S(1)}, f32[2,1024,256]{2,1,0:T(8,128)S(1)}, f32[16,16,512]{2,1,0:T(8,128)S(1)}) custom-call(s32[16]{0:T(128)S(1)} %copy-done.4, f32[4,1024,512]{2,1,0:T(8,128)S(1)} %get-tuple-element.24.log_ref, f32[128,128]{1,0:T(8,128)S(1)} %bitcast.12, bf16[2048,256]{1,0:T(8,128)(2,1)S(1)} %copy-done), custom_call_target="tpu_custom_call" | custom-call | tf_op jit(solution)/shard_map/normalize_enc1/pallas_call | solution.py:231
  46.8 14.9 %all_to_all.48.stat_ref = f32[16,16,512]{2,1,0:T(8,128)S(1)} all-to-all(f32[16,16,512]{2,1,0:T(8,128)S(1)} %get-tuple-element.28), channel_id=1, replica_groups=mesh['row'=8,'pair'=8,'core'=2] {'pair','core'}, dimensions={0} | all-to-all | bytes 1048576 | tf_op jit(solution)/shard_map/all_to_all | solution.py:484
  61.7 0.0 copy-done.1
  61.7 0.0 copy-done.3
  61.7 13.6 %middle.1 = (f32[2048,256]{1,0:T(8,128)S(1)}, f32[2048,256]{1,0:T(8,128)S(1)}, f32[2,1024,256]{2,1,0:T(8,128)S(1)}, f32[16,512]{1,0:T(8,128)S(1)}, f32[16,16,512]{2,1,0:T(8,128)S(1)}) custom-call(s32[16]{0:T(128)S(1)} %copy-done.4, s32[1]{0:T(128)} %bitcast.1.core_ref, bf16[4,1024,512]{2,1,0:T(8,128)(2,1)S(1)} %get-tuple-element.26.normed_ref, ...), custom_call_target="tpu_custom_call" | custom-call | tf_op jit(solution)/shard_map/middle/pallas_call | solution.py:399
  75.3 1.2 collective-permute-start
  76.5 13.9 %all_to_all.49.sums_ref = f32[16,16,512]{2,1,0:T(8,128)S(1)} all-to-all(f32[16,16,512]{2,1,0:T(8,128)S(1)} %get-tuple-element.33), channel_id=1, replica_groups=mesh['row'=8,'pair'=8,'core'=2] {'pair','core'}, dimensions={0} | all-to-all | bytes 1048576 | tf_op jit(solution)/shard_map/all_to_all | solution.py:484
  90.4 3.7 %grad_enc1.1 = (f32[1024,256]{1,0:T(8,128)S(1)}, f32[1024,256]{1,0:T(8,128)S(1)}) custom-call(s32[16]{0:T(128)S(1)} %copy-done.4, s32[1]{0:T(128)} %bitcast.1.core_ref, bf16[4,1024,512]{2,1,0:T(8,128)(2,1)S(1)} %get-tuple-element.26.normed_ref, f32[2,1024,256]{2,1,0:T(8,128)S(1)} %get-tuple-element.27.pre_ref, ...), custom_call_target="tpu_custom_call" | custom-call | tf_op jit(solution)/shard_map/grad_enc1/pallas_call | solution.py:470
  94.2 1.1 collective-permute-start.1
  95.3 2.3 %collective-permute-done.1 = f32[1024,256]{1,0:T(8,128)S(1)} collective-permute-done((f32[1024,256]{1,0:T(8,128)S(1)}, f32[1024,256]{1,0:T(8,128)S(1)}, u32[]{:S(2)}, u32[]{:S(2)}) %collective-permute-start.1) | collective-permute-done | bytes 1048608 | tf_op jit(solution)/shard_map/ppermute | solution.py:480
  97.6 0.2 add_convert_fusion.1
  97.8 0.0 collective-permute-done
  97.8 0.4 add_convert_fusion
  98.2 0.1 pad_maximum_fusion
  98.3 27.2 %all_to_all.50.in_ref = bf16[64,48,256]{2,1,0:T(8,128)(2,1)S(1)} all-to-all(bf16[64,48,256]{2,1,0:T(8,128)(2,1)S(1)} %pad_maximum_fusion), channel_id=1, replica_groups=mesh['row'=8,'pair'=8,'core'=2] {'row','pair'}, dimensions={0} | all-to-all | bytes 3145728 | tf_op jit(solution)/shard_map/all_to_all | solution.py:484
  125.5 0.4 owner_sum.1
  125.9 0.1 broadcast_in_dim.2
  126.0 30.8 %all_to_all.51 = f16[64,56,256]{2,1,0:T(8,128)(2,1)S(1)} all-to-all(f16[64,56,256]{2,1,0:T(8,128)(2,1)S(1)} %broadcast_in_dim.2), channel_id=1, replica_groups=mesh['row'=8,'pair'=8,'core'=2] {'row','pair'}, dimensions={0} | all-to-all | bytes 3670016 | tf_op jit(solution)/shard_map/all_to_all | solution.py:484
  156.8 2.7 %collective-permute-start.2 = (f16[64,56,256]{2,1,0:T(8,128)(2,1)S(1)}, f16[64,56,256]{2,1,0:T(8,128)(2,1)S(1)}, u32[]{:S(2)}, u32[]{:S(2)}) collective-permute-start(f16[64,56,256]{2,1,0:T(8,128)(2,1)S(1)} %all_to_all.51), channel_id=1, source_target_pairs={{0,1},{1,0},{2,3},{3,2},{4,5},{5,4},{6,7},{7,6},{8,9},{9,8},{10,11... | collective-permute-start | bytes 5505032 | tf_op jit(solution)/shard_map/ppermute | solution.py:480
  159.5 0.3 convert_element_type.18.mine_ref
  159.7 3.1 %collective-permute-done.2 = f16[64,56,256]{2,1,0:T(8,128)(2,1)S(1)} collective-permute-done((f16[64,56,256]{2,1,0:T(8,128)(2,1)S(1)}, f16[64,56,256]{2,1,0:T(8,128)(2,1)S(1)}, u32[]{:S(2)}, u32[]{:S(2)}) %collective-permute-start.2) | collective-permute-done | bytes 1835040 | tf_op jit(solution)/shard_map/ppermute | solution.py:480
  162.9 0.3 convert_element_type.19.other_ref
  163.2 4.5 %place_gradients.1 = (f32[2,1024,256]{2,1,0:T(8,128)}, f32[1024,256]{1,0:T(8,128)}, f32[256,1024]{1,0:T(8,128)}, f32[256,2048]{1,0:T(8,128)}) custom-call(s32[1]{0:T(128)} %bitcast.1.core_ref, f32[64,56,256]{2,1,0:T(8,128)S(1)} %convert_element_type.18.mine_ref, f32[64,56,256]{2,1,0:T(8,128)S(1)} %convert_element_type.19.other_ref), custom_call_target="tpu_custom_call" | custom-call | tf_op jit(solution)/shard_map/place_gradients/pallas_call | solution.py:564
  (6 shorter events, 0.0 us)
Async XLA Ops:
  0.6 0.7 copy-start.5
  1.3 41.7 %copy-start = (bf16[2048,256]{1,0:T(8,128)(2,1)S(1)}, bf16[2048,256]{1,0:T(8,128)(2,1)}, u32[]{:S(2)}) copy-start(bf16[2048,256]{1,0:T(8,128)(2,1)} %w_ref.1) | copy-start | bytes 3145732
  1.3 41.7 %copy-start.4 = (s32[16]{0:T(128)S(1)}, s32[16]{0:T(128)}, u32[]{:S(2)}) copy-start(s32[16]{0:T(128)} %perm_ref.5) | copy-start | bytes 196
  43.0 18.7 %copy-start.1 = (bf16[256,2048]{1,0:T(8,128)(2,1)S(1)}, bf16[256,2048]{1,0:T(8,128)(2,1)}, u32[]{:S(2)}) copy-start(bf16[256,2048]{1,0:T(8,128)(2,1)} %c_ref.1) | copy-start | bytes 3145732
  43.0 18.7 %copy-start.2 = (bf16[1024,256]{1,0:T(8,128)(2,1)S(1)}, bf16[1024,256]{1,0:T(8,128)(2,1)}, u32[]{:S(2)}) copy-start(bf16[1024,256]{1,0:T(8,128)(2,1)} %v_ref.1) | copy-start | bytes 1572868
  43.0 18.7 %copy-start.3 = (bf16[256,1024]{1,0:T(8,128)(2,1)S(1)}, bf16[256,1024]{1,0:T(8,128)(2,1)}, u32[]{:S(2)}) copy-start(bf16[256,1024]{1,0:T(8,128)(2,1)} %b_ref.1) | copy-start | bytes 1572868
  75.3 22.4 %collective-permute-start = (f32[2048,256]{1,0:T(8,128)S(1)}, f32[2048,256]{1,0:T(8,128)S(1)}, u32[]{:S(2)}, u32[]{:S(2)}) collective-permute-start(f32[2048,256]{1,0:T(8,128)S(1)} %get-tuple-element.30), channel_id=1, source_target_pairs={{0,1},{1,0},{2,3},{3,2},{4,5},{5,4},{6,7},{7,6},{8,9},{9,8},{10,11... | collective-permute-start | bytes 6291464 | tf_op jit(solution)/shard_map/ppermute | solution.py:480
  94.2 3.4 %collective-permute-start.1 = (f32[1024,256]{1,0:T(8,128)S(1)}, f32[1024,256]{1,0:T(8,128)S(1)}, u32[]{:S(2)}, u32[]{:S(2)}) collective-permute-start(f32[1024,256]{1,0:T(8,128)S(1)} %get-tuple-element.35), channel_id=1, source_target_pairs={{0,1},{1,0},{2,3},{3,2},{4,5},{5,4},{6,7},{7,6},{8,9},{9,8},{10,11... | collective-permute-start | bytes 3145736 | tf_op jit(solution)/shard_map/ppermute | solution.py:480
  156.8 6.1 %collective-permute-start.2 = (f16[64,56,256]{2,1,0:T(8,128)(2,1)S(1)}, f16[64,56,256]{2,1,0:T(8,128)(2,1)S(1)}, u32[]{:S(2)}, u32[]{:S(2)}) collective-permute-start(f16[64,56,256]{2,1,0:T(8,128)(2,1)S(1)} %all_to_all.51), channel_id=1, source_target_pairs={{0,1},{1,0},{2,3},{3,2},{4,5},{5,4},{6,7},{7,6},{8,9},{9,8},{10,11... | collective-permute-start | bytes 5505032 | tf_op jit(solution)/shard_map/ppermute | solution.py:480

commit v5 on v4

--- a/solution.py
+++ b/solution.py
@@ -23,6 +23,10 @@
 
 def on_chip(values):
     return pltpu.with_memory_space_constraint(values, pltpu.VMEM)
+
+
+def in_hbm(values):
+    return pltpu.with_memory_space_constraint(values, pltpu.HBM)
 
 
 def step_rows(ref, rows):
@@ -127,7 +131,7 @@
         ],
         compiler_params=pltpu.CompilerParams(vmem_limit_bytes=10 * MIB),
         name="sort_and_sum",
-    )(sensor_ids.reshape(windows), pltpu.with_memory_space_constraint(spectra, pltpu.HBM))
+    )(in_hbm(sensor_ids.reshape(windows)), in_hbm(spectra))
 
 
 def stats_kernel(in_ref, out_ref, *, windows, chunks, sensors, per_sensor):
@@ -216,7 +220,7 @@
         in_specs=[
             ON_CHIP,
             pl.BlockSpec((LANES, LANES), lambda i, p: (0, 0)),
-            pl.BlockSpec(w_enc1.shape, lambda i, p: (0, 0)),
+            ON_CHIP,
         ],
         out_specs=[
             ON_CHIP,
@@ -238,7 +242,7 @@
         ],
         compiler_params=pltpu.CompilerParams(vmem_limit_bytes=16 * MIB),
         name="normalize_enc1",
-    )(permutation, on_chip(logs), coef, w_enc1)
+    )(permutation, on_chip(logs), coef, on_chip(w_enc1))
 
 
 def window_rows(perm_ref, table, step, windows, quarter, all_windows, cols, first, last):
@@ -249,10 +253,14 @@
     return jnp.concatenate(parts, axis=0)
 
 
-def write_halves(core_ref, grads, own_ref, send_ref):
-    half = own_ref.shape[0]
-    own_ref[...] = grads[pl.ds(pl.multiple_of(core_ref[0] * half, half), half), :]
-    send_ref[...] = grads[pl.ds(pl.multiple_of((1 - core_ref[0]) * half, half), half), :]
+def write_halves(core_ref, grads, own_ref, send_ref, bounds):
+    for first, last in zip(bounds[:-1], bounds[1:]):
+        half = (last - first) // 2
+        at = first // 2
+        own = pl.multiple_of(first + core_ref[0] * half, half)
+        send = pl.multiple_of(first + (1 - core_ref[0]) * half, half)
+        own_ref[at:at + half, :] = grads[pl.ds(own, half), :]
+        send_ref[at:at + half, :] = grads[pl.ds(send, half), :]
 
 
 def middle_kernel(perm_ref, core_ref, normed_ref, pre_ref, stat_ref, v_ref, b_ref, c_ref,
@@ -362,7 +370,7 @@
     def _():
         for d in range(cols):
             sums_ref[d] = sums[...]
-        write_halves(core_ref, grads, own_ref, send_ref)
+        write_halves(core_ref, grads, own_ref, send_ref, (0, base_b, base_v, base_v + 4 * ch))
 
 
 def middle_call(permutation, core, normed, pre, stat, w_enc2, w_dec1, w_dec2, quarter, cols, total_windows):
@@ -378,14 +386,14 @@
         in_specs=[
             ON_CHIP,
             ON_CHIP,
-            pl.BlockSpec(stat.shape, whole3),
-            pl.BlockSpec(w_enc2.shape, whole2),
-            pl.BlockSpec(w_dec1.shape, whole2),
-            pl.BlockSpec(w_dec2.shape, whole2),
+            ON_CHIP,
+            ON_CHIP,
+            ON_CHIP,
+            ON_CHIP,
         ],
         out_specs=[
-            pl.BlockSpec((total // 2, channels), whole2),
-            pl.BlockSpec((total // 2, channels), whole2),
+            ON_CHIP,
+            ON_CHIP,
             ON_CHIP,
             pl.BlockSpec((windows, 2 * channels), whole2),
             pl.BlockSpec(stat.shape, whole3),
@@ -400,15 +408,15 @@
         functools.partial(middle_kernel, quarter=quarter, cols=cols, total_windows=float(total_windows)),
         grid_spec=grid_spec,
         out_shape=[
-            jax.ShapeDtypeStruct((total // 2, channels), F32),
-            jax.ShapeDtypeStruct((total // 2, channels), F32),
+            pltpu.VMEM((total // 2, channels), F32),
+            pltpu.VMEM((total // 2, channels), F32),
             pltpu.VMEM(pre.shape, F32),
             jax.ShapeDtypeStruct((windows, 2 * channels), F32),
             jax.ShapeDtypeStruct(stat.shape, F32),
         ],
-        compiler_params=pltpu.CompilerParams(vmem_limit_bytes=36 * MIB),
+        compiler_params=pltpu.CompilerParams(vmem_limit_bytes=30 * MIB),
         name="middle",
-    )(permutation, core, on_chip(normed), on_chip(pre), stat, w_enc2, w_dec1, w_dec2)
+    )(permutation, core, on_chip(normed), on_chip(pre), on_chip(stat), on_chip(w_enc2), on_chip(w_dec1), on_chip(w_dec2))
 
 
 def grad_kernel(perm_ref, core_ref, normed_ref, pre_ref, back_ref, moment_ref, sums_ref, own_ref, send_ref, grads, scale, *, quarter, cols):
@@ -447,7 +455,7 @@
 
     @pl.when(step == pl.num_programs(0) - 1)
     def _():
-        write_halves(core_ref, grads, own_ref, send_ref)
+        write_halves(core_ref, grads, own_ref, send_ref, (0, 4 * bins))
 
 
 def grad_call(permutation, core, normed, pre, back, moment, sums, quarter, cols):
@@ -462,18 +470,18 @@
             ON_CHIP,
             ON_CHIP,
             pl.BlockSpec(moment.shape, lambda i, p, c: (0, 0)),
-            pl.BlockSpec(sums.shape, lambda i, p, c: (0, 0, 0)),
-        ],
-        out_specs=[pl.BlockSpec((2 * bins, channels), lambda i, p, c: (0, 0))] * 2,
+            ON_CHIP,
+        ],
+        out_specs=[ON_CHIP] * 2,
         scratch_shapes=[pltpu.VMEM((4 * bins, channels), F32), pltpu.VMEM((windows, 2 * channels), F32)],
     )
     return pl.pallas_call(
         functools.partial(grad_kernel, quarter=quarter, cols=cols),
         grid_spec=grid_spec,
-        out_shape=[jax.ShapeDtypeStruct((2 * bins, channels), F32)] * 2,
+        out_shape=[pltpu.VMEM((2 * bins, channels), F32)] * 2,
         compiler_params=pltpu.CompilerParams(vmem_limit_bytes=16 * MIB),
         name="grad_enc1",
-    )(permutation, core, on_chip(normed), on_chip(pre), on_chip(back), moment, sums)
+    )(permutation, core, on_chip(normed), on_chip(pre), on_chip(back), moment, on_chip(sums))
 
 
 def swap_cores(values):
@@ -499,15 +507,17 @@
     total = lax.fori_loop(0, chips, body, jnp.zeros((rows, width), F32), unroll=4)
     largest = jnp.max(jnp.max(jnp.abs(total), axis=0, keepdims=True), axis=1, keepdims=True)
     exponent = jnp.clip(jnp.ceil(jnp.log2(largest)), -110.0, 126.0)
-    out_ref[0:rows, :] = total * jnp.exp2(14.0 - exponent)
-    out_ref[rows:, :] = jnp.broadcast_to(exponent, (SCALE_ROWS, width))
+    total = total * jnp.exp2(14.0 - exponent)
+    for k in range(width // LANES):
+        out_ref[k * rows:(k + 1) * rows, :] = total[:, k * LANES:(k + 1) * LANES]
+    out_ref[width // LANES * rows:, :] = jnp.broadcast_to(exponent, (SCALE_ROWS, LANES))
 
 
 def owner_call(pieces):
     chips, rows, width = pieces.shape
     return pl.pallas_call(
         owner_kernel,
-        out_shape=jax.ShapeDtypeStruct((rows + SCALE_ROWS, width), F32),
+        out_shape=jax.ShapeDtypeStruct((width // LANES * rows + SCALE_ROWS, LANES), F32),
         compiler_params=pltpu.CompilerParams(vmem_limit_bytes=6 * MIB),
         name="owner_sum",
     )(pieces)
@@ -519,60 +529,66 @@
     return exchange(copies.reshape(-1, width), axes).reshape(chips, rows, width)
 
 
-def place_kernel(core_ref, mine_ref, other_ref, grad_w_ref, grad_v_ref, grad_b_ref, grad_c_ref, *, cut):
+def place_kernel(half_ref, blocks_ref, *refs, rows, cut):
+    grad_w_ref, grad_v_ref, grad_b_ref, grad_c_ref = refs[-4:]
     step = pl.program_id(0)
-    half = pl.num_programs(0) // 2
-    total = mine_ref.shape[1]
-    rows = total - SCALE_ROWS
-    first = core_ref[0] == 0
-    for i in range(mine_ref.shape[0]):
-        mine, other = mine_ref[i], other_ref[i]
-        low = jnp.where(first, mine, other)
-        high = jnp.where(first, other, mine)
-        low = low[0:rows] * jnp.exp2(low[rows:rows + 1] - 14.0)
-        high = high[0:rows] * jnp.exp2(high[rows:rows + 1] - 14.0)
-        early, late = i * cut, i * (rows - cut)
-        grad_c_ref[early:early + cut, :] = low[0:cut]
-        grad_w_ref[0, late:late + rows - cut, :] = low[cut:rows]
-        grad_w_ref[1, late:late + rows - cut, :] = high[cut:rows]
-
-        @pl.when(step < half)
-        def _():
-            grad_b_ref[early:early + cut, :] = high[0:cut]
-
-        @pl.when(step >= half)
-        def _():
-            grad_v_ref[early:early + cut, :] = high[0:cut]
-
-
-def place_call(core, mine, other, cut, channels, bins):
-    chips, total, width = mine.shape
-    late = total - SCALE_ROWS - cut
+    steps = pl.num_programs(0)
+    late = rows - cut
+    for i in range(blocks_ref.shape[0]):
+        scale = jnp.exp2(blocks_ref[i, 2 * rows:2 * rows + 1, :] - 14.0)
+        for k in range(2):
+            lanes = slice(k * LANES, (k + 1) * LANES)
+            block = blocks_ref[i, k * rows:(k + 1) * rows, :] * scale
+            grad_w_ref[i * late:(i + 1) * late, lanes] = block[cut:rows]
+            top = block[0:cut]
+            at = slice(i * cut, (i + 1) * cut)
+
+            @pl.when(step < steps // 2)
+            def _():
+                grad_c_ref[at, lanes] = top
+
+            @pl.when((step >= steps // 2) & (step < 3 * steps // 4))
+            def _():
+                grad_b_ref[at, lanes] = top
+
+            @pl.when(step >= 3 * steps // 4)
+            def _():
+                grad_v_ref[at, lanes] = top
+
+
+def place_call(half, blocks, rows, cut, channels, bins, earlier=()):
+    chips, total, _ = blocks.shape
+    late = rows - cut
     group = channels // cut
     steps = chips // group
+    quarter = steps // 4
+    within = lambda i, low, count: jnp.clip(i - low, 0, count - 1)
     grid_spec = pltpu.PrefetchScalarGridSpec(
         num_scalar_prefetch=1,
         grid=(steps,),
-        in_specs=[pl.BlockSpec((group, total, width), lambda i, c: (i, 0, 0))] * 2,
+        in_specs=[pl.BlockSpec((group, total, LANES), lambda i, h: (i, 0, 0))]
+        + [pl.BlockSpec(memory_space=pl.ANY)] * len(earlier),
         out_specs=[
-            pl.BlockSpec((2, group * late, width), lambda i, c: (0, i, 0)),
-            pl.BlockSpec((channels, width), lambda i, c: (jnp.maximum(i - steps // 2, 0), 0)),
-            pl.BlockSpec((channels, width), lambda i, c: (0, jnp.minimum(i, steps // 2 - 1))),
-            pl.BlockSpec((channels, width), lambda i, c: (0, i)),
+            pl.BlockSpec((group * late, channels), lambda i, h: (h[0] * steps + i, 0)),
+            pl.BlockSpec((channels, channels), lambda i, h: (h[0] * quarter + within(i, 3 * quarter, quarter), 0)),
+            pl.BlockSpec((channels, channels), lambda i, h: (0, h[0] * quarter + within(i, 2 * quarter, quarter))),
+            pl.BlockSpec((channels, channels), lambda i, h: (0, h[0] * 2 * quarter + within(i, 0, 2 * quarter))),
         ],
     )
     return pl.pallas_call(
-        functools.partial(place_kernel, cut=cut),
+        functools.partial(place_kernel, rows=rows, cut=cut),
         grid_spec=grid_spec,
         out_shape=[
-            jax.ShapeDtypeStruct((2, chips * late, width), F32),
+            jax.ShapeDtypeStruct((4 * bins, channels), F32),
             jax.ShapeDtypeStruct((4 * channels, channels), F32),
             jax.ShapeDtypeStruct((channels, 4 * channels), F32),
             jax.ShapeDtypeStruct((channels, 4 * bins), F32),
         ],
+        input_output_aliases={2 + k: k for k in range(len(earlier))},
         compiler_params=pltpu.CompilerParams(vmem_limit_bytes=12 * MIB),
+        cost_estimate=pl.CostEstimate(flops=chips * total * LANES, bytes_accessed=8 * chips * total * LANES, transcendentals=0),
         name="place_gradients",
-    )(core, mine, other)
+    )(half, blocks, *earlier)
 
 
 def local(spectra, sensor_ids, permutation, w_enc1, w_enc2, w_dec1, w_dec2):
@@ -603,9 +619,9 @@
     piece = owner_call(chip_sums([(own, send), late], chip_axes, chips))
     mine = gather_rows(piece, chip_axes, chips)
     other = swap_cores(mine)
-    grad_w, grad_v, grad_b, grad_c = place_call(
-        core, mine.astype(F32), other.astype(F32), own.shape[0] // chips, channels, bins)
-    return (grad_w.reshape(4 * bins, channels), grad_v, grad_b, grad_c)
+    rows, cut = own.shape[0] // chips + late[0].shape[0] // chips, own.shape[0] // chips
+    placed = place_call(core, mine.astype(F32), rows, cut, channels, bins)
+    return tuple(place_call(1 - core, other.astype(F32), rows, cut, channels, bins, placed))
 
 
 def solution(mesh):

time: 168 us -> 167 us (level)
  Pallas kernels: 32.4 us -> 36.6 us
  waiting for transfers between devices: 5.41 us -> 2.29 us
    pallas_call x2 -> x3, Pallas kernels: 4.83 us -> 8.76 us  [the longest x2 8.41 us: place_call(): pl.pallas_call(functools.partial(place_kernel, rows=rows, cut=cut), grid_...]
    ppermute x3, waiting for transfers between devices: 5.41 us -> 2.29 us  [swap_cores(): return lax.ppermute(values, 'core', [(0, 1), (1, 0)])]
  transfers between devices with their start and end apart: 3 -> 3, of which waited for: 2 -> 1; matrix products, arithmetic and copies ran while one was open for 0% -> 0% of each run, Pallas kernels for 2% -> 5%
where the time goes in v5:
time: 167 us
  blocking collectives  121 us (72%)
  Pallas kernels  36.6 us (22%)
  starting transfers between devices  4.98 us (3%)
  waiting for transfers between devices  2.29 us (1%)
    all_to_all x6, blocking collectives, exchange(): return lax.all_to_all(values, axes, split_axis=0, concat_axis=0, tiled=True)  121 us
    pallas_call x1, Pallas kernels, middle_call(): pl.pallas_call(functools.partial(middle_kernel, quarter=quarter, cols=col...  13.6 us
    pallas_call x2, Pallas kernels, place_call(): pl.pallas_call(functools.partial(place_kernel, rows=rows, cut=cut), grid_...  8.41 us
    pallas_call x1, Pallas kernels, sums_call(): pl.pallas_call(functools.partial(sums_kernel, chunks=chunks, count=window...  5.64 us
    ppermute x3, starting transfers between devices, swap_cores(): return lax.ppermute(values, 'core', [(0, 1), (1, 0)])  4.98 us
    pallas_call x1, Pallas kernels, enc1_call(): pl.pallas_call(functools.partial(enc1_kernel, chunks=chunks, quarter=quar...  3.89 us
    pallas_call x1, Pallas kernels, grad_call(): pl.pallas_call(functools.partial(grad_kernel, quarter=quarter, cols=cols)...  3.68 us
  transfers between devices with their start and end apart: 3, of which 1 were waited for; matrix products, arithmetic and copies ran while one was open for 0% of the time, Pallas kernels for 5%

profile of v5, /device:TPU:1, one launch (start us, length us, event | category | flops | bytes accessed | tf_op | source)
XLA Modules:
  0.0 166.7 jit_solution(15187860803279863054)
XLA Ops:
  0.6 0.0 copy-start
  0.6 0.0 copy-start.4
  0.7 5.6 %sort_and_sum.1 = (f32[4,1024,512]{2,1,0:T(8,128)S(1)}, f32[256,128]{1,0:T(8,128)S(1)}) custom-call(s32[16]{0:T(128)} %bitcast.16, bf16[16,256,512]{2,1,0:T(8,128)(2,1)} %spec_ref.1), custom_call_target="tpu_custom_call" | custom-call | tf_op jit(solution)/shard_map/sort_and_sum/pallas_call | solution.py:125
  6.3 21.6 %all_to_all.46 = f32[128,2,128]{2,1,0:T(2,128)S(1)} all-to-all(f32[128,2,128]{2,1,0:T(2,128)S(1)} %bitcast.13), channel_id=1, replica_groups=mesh['row'=8,'pair'=8,'core'=2] {'row','pair','core'}, dimensions={0} | all-to-all | bytes 262144 | tf_op jit(solution)/shard_map/all_to_all | solution.py:492
  27.9 1.1 sensor_stats.1
  28.9 13.6 %all_to_all.47 = f32[128,1,128]{2,1,0:T(1,128)S(1)} all-to-all(f32[128,1,128]{2,1,0:T(1,128)S(1)} %bitcast.12), channel_id=1, replica_groups=mesh['row'=8,'pair'=8,'core'=2] {'row','pair','core'}, dimensions={0} | all-to-all | bytes 131072 | tf_op jit(solution)/shard_map/all_to_all | solution.py:492
  42.6 0.0 copy-done
  42.6 0.0 copy-done.4
  42.6 0.0 copy-start.3
  42.6 3.9 %normalize_enc1.1 = (bf16[4,1024,512]{2,1,0:T(8,128)(2,1)S(1)}, f32[2,1024,256]{2,1,0:T(8,128)S(1)}, f32[16,16,512]{2,1,0:T(8,128)S(1)}) custom-call(s32[16]{0:T(128)S(1)} %copy-done.4, f32[4,1024,512]{2,1,0:T(8,128)S(1)} %get-tuple-element.24.log_ref, f32[128,128]{1,0:T(8,128)S(1)} %bitcast.11, bf16[2048,256]{1,0:T(8,128)(2,1)S(1)} %copy-done), custom_call_target="tpu_custom_call" | custom-call | tf_op jit(solution)/shard_map/normalize_enc1/pallas_call | solution.py:235
  46.5 14.9 %all_to_all.48.stat_ref = f32[16,16,512]{2,1,0:T(8,128)S(1)} all-to-all(f32[16,16,512]{2,1,0:T(8,128)S(1)} %get-tuple-element.28), channel_id=1, replica_groups=mesh['row'=8,'pair'=8,'core'=2] {'pair','core'}, dimensions={0} | all-to-all | bytes 1048576 | tf_op jit(solution)/shard_map/all_to_all | solution.py:492
  61.4 0.0 copy-done.2
  61.5 13.6 %middle.1 = (f32[2048,256]{1,0:T(8,128)S(1)}, f32[2048,256]{1,0:T(8,128)S(1)}, f32[2,1024,256]{2,1,0:T(8,128)S(1)}, f32[16,512]{1,0:T(8,128)S(1)}, f32[16,16,512]{2,1,0:T(8,128)S(1)}) custom-call(s32[16]{0:T(128)S(1)} %copy-done.4, s32[1]{0:T(128)} %bitcast.1.core_ref.half_ref, bf16[4,1024,512]{2,1,0:T(8,128)(2,1)S(1)} %get-tuple-element.26.normed_ref, ...), custom_call_target="tpu_custom_call" | custom-call | tf_op jit(solution)/shard_map/middle/pallas_call | solution.py:407
  75.0 1.2 collective-permute-start
  76.2 13.9 %all_to_all.49.sums_ref = f32[16,16,512]{2,1,0:T(8,128)S(1)} all-to-all(f32[16,16,512]{2,1,0:T(8,128)S(1)} %get-tuple-element.33), channel_id=1, replica_groups=mesh['row'=8,'pair'=8,'core'=2] {'pair','core'}, dimensions={0} | all-to-all | bytes 1048576 | tf_op jit(solution)/shard_map/all_to_all | solution.py:492
  90.1 3.7 %grad_enc1.1 = (f32[1024,256]{1,0:T(8,128)S(1)}, f32[1024,256]{1,0:T(8,128)S(1)}) custom-call(s32[16]{0:T(128)S(1)} %copy-done.4, s32[1]{0:T(128)} %bitcast.1.core_ref.half_ref, bf16[4,1024,512]{2,1,0:T(8,128)(2,1)S(1)} %get-tuple-element.26.normed_ref, f32[2,1024,256]{2,1,0:T(8,128)S(1)} %get-tuple-element.27.pre_ref, ...), custom_call_target="tpu_custom_call" | custom-call | tf_op jit(solution)/shard_map/grad_enc1/pallas_call | solution.py:478
  93.8 1.1 collective-permute-start.1
  94.9 2.3 %collective-permute-done.1 = f32[1024,256]{1,0:T(8,128)S(1)} collective-permute-done((f32[1024,256]{1,0:T(8,128)S(1)}, f32[1024,256]{1,0:T(8,128)S(1)}, u32[]{:S(2)}, u32[]{:S(2)}) %collective-permute-start.1) | collective-permute-done | bytes 1048608 | tf_op jit(solution)/shard_map/ppermute | solution.py:488
  97.2 0.2 add_convert_fusion.1
  97.4 0.0 collective-permute-done
  97.4 0.4 add_convert_fusion
  97.8 0.1 pad_maximum_fusion
  97.9 27.2 %all_to_all.50.in_ref = bf16[64,48,256]{2,1,0:T(8,128)(2,1)S(1)} all-to-all(bf16[64,48,256]{2,1,0:T(8,128)(2,1)S(1)} %pad_maximum_fusion), channel_id=1, replica_groups=mesh['row'=8,'pair'=8,'core'=2] {'row','pair'}, dimensions={0} | all-to-all | bytes 3145728 | tf_op jit(solution)/shard_map/all_to_all | solution.py:492
  125.1 0.4 owner_sum.1
  125.5 0.2 broadcast_in_dim.2
  125.7 29.4 %all_to_all.51 = f16[64,104,128]{2,1,0:T(8,128)(2,1)S(1)} all-to-all(f16[64,104,128]{2,1,0:T(8,128)(2,1)S(1)} %broadcast_in_dim.2), channel_id=1, replica_groups=mesh['row'=8,'pair'=8,'core'=2] {'row','pair'}, dimensions={0} | all-to-all | bytes 3407872 | tf_op jit(solution)/shard_map/all_to_all | solution.py:492
  155.1 2.7 %collective-permute-start.2 = (f16[64,104,128]{2,1,0:T(8,128)(2,1)S(1)}, f16[64,104,128]{2,1,0:T(8,128)(2,1)S(1)}, u32[]{:S(2)}, u32[]{:S(2)}) collective-permute-start(f16[64,104,128]{2,1,0:T(8,128)(2,1)S(1)} %all_to_all.51), channel_id=1, source_target_pairs={{0,1},{1,0},{2,3},{3,2},{4,5},{5,4},{6,7},{7,6},{8,9},{9,8},{10,11... | collective-permute-start | bytes 5111816 | tf_op jit(solution)/shard_map/ppermute | solution.py:488
  157.8 0.2 convert_element_type.19.blocks_ref
  158.1 4.2 %place_gradients.2 = (f32[2048,256]{1,0:T(8,128)}, f32[1024,256]{1,0:T(8,128)}, f32[256,1024]{1,0:T(8,128)}, f32[256,2048]{1,0:T(8,128)}) custom-call(s32[1]{0:T(128)} %bitcast.1.core_ref.half_ref, f32[64,104,128]{2,1,0:T(8,128)S(1)} %convert_element_type.19.blocks_ref), custom_call_target="tpu_custom_call" | custom-call | flops 851968 | bytes 6815744 | tf_op jit(solution)/shard_map/place_gradients/pallas_call | solution.py:578
  162.3 0.0 collective-permute-done.2
  162.3 0.2 convert_element_type.18.blocks_ref
  162.5 4.2 %place_gradients.3 = (f32[2048,256]{1,0:T(8,128)}, f32[1024,256]{1,0:T(8,128)}, f32[256,1024]{1,0:T(8,128)}, f32[256,2048]{1,0:T(8,128)}) custom-call(s32[1]{0:T(128)S(6)} %sub.3.half_ref, f32[64,104,128]{2,1,0:T(8,128)S(1)} %convert_element_type.18.blocks_ref, ...), custom_call_target="tpu_custom_call", output_to_operand_aliasing={{0}: (2, {}), {1}: (3, {}), {2}: (4, {}), {3}: (5, {})} | custom-call | flops 851968 | bytes 6815744 | tf_op jit(solution)/shard_map/place_gradients/pallas_call | solution.py:578
  (5 shorter events, 0.0 us)
Async XLA Ops:
  0.6 42.0 %copy-start = (bf16[2048,256]{1,0:T(8,128)(2,1)S(1)}, bf16[2048,256]{1,0:T(8,128)(2,1)}, u32[]{:S(2)}) copy-start(bf16[2048,256]{1,0:T(8,128)(2,1)} %w_ref.1) | copy-start | bytes 3145732
  0.6 42.0 %copy-start.4 = (s32[16]{0:T(128)S(1)}, s32[16]{0:T(128)}, u32[]{:S(2)}) copy-start(s32[16]{0:T(128)} %perm_ref.5) | copy-start | bytes 196
  42.6 18.8 %copy-start.1 = (bf16[256,2048]{1,0:T(8,128)(2,1)S(1)}, bf16[256,2048]{1,0:T(8,128)(2,1)}, u32[]{:S(2)}) copy-start(bf16[256,2048]{1,0:T(8,128)(2,1)} %c_ref.1) | copy-start | bytes 3145732
  42.6 18.8 %copy-start.2 = (bf16[1024,256]{1,0:T(8,128)(2,1)S(1)}, bf16[1024,256]{1,0:T(8,128)(2,1)}, u32[]{:S(2)}) copy-start(bf16[1024,256]{1,0:T(8,128)(2,1)} %v_ref.1) | copy-start | bytes 1572868
  42.6 18.8 %copy-start.3 = (bf16[256,1024]{1,0:T(8,128)(2,1)S(1)}, bf16[256,1024]{1,0:T(8,128)(2,1)}, u32[]{:S(2)}) copy-start(bf16[256,1024]{1,0:T(8,128)(2,1)} %b_ref.1) | copy-start | bytes 1572868
  75.0 22.4 %collective-permute-start = (f32[2048,256]{1,0:T(8,128)S(1)}, f32[2048,256]{1,0:T(8,128)S(1)}, u32[]{:S(2)}, u32[]{:S(2)}) collective-permute-start(f32[2048,256]{1,0:T(8,128)S(1)} %get-tuple-element.30), channel_id=1, source_target_pairs={{0,1},{1,0},{2,3},{3,2},{4,5},{5,4},{6,7},{7,6},{8,9},{9,8},{10,11... | collective-permute-start | bytes 6291464 | tf_op jit(solution)/shard_map/ppermute | solution.py:488
  93.8 3.4 %collective-permute-start.1 = (f32[1024,256]{1,0:T(8,128)S(1)}, f32[1024,256]{1,0:T(8,128)S(1)}, u32[]{:S(2)}, u32[]{:S(2)}) collective-permute-start(f32[1024,256]{1,0:T(8,128)S(1)} %get-tuple-element.35), channel_id=1, source_target_pairs={{0,1},{1,0},{2,3},{3,2},{4,5},{5,4},{6,7},{7,6},{8,9},{9,8},{10,11... | collective-permute-start | bytes 3145736 | tf_op jit(solution)/shard_map/ppermute | solution.py:488
  155.1 7.1 %collective-permute-start.2 = (f16[64,104,128]{2,1,0:T(8,128)(2,1)S(1)}, f16[64,104,128]{2,1,0:T(8,128)(2,1)S(1)}, u32[]{:S(2)}, u32[]{:S(2)}) collective-permute-start(f16[64,104,128]{2,1,0:T(8,128)(2,1)S(1)} %all_to_all.51), channel_id=1, source_target_pairs={{0,1},{1,0},{2,3},{3,2},{4,5},{5,4},{6,7},{7,6},{8,9},{9,8},{10,11... | collective-permute-start | bytes 5111816 | tf_op jit(solution)/shard_map/ppermute | solution.py:488

commit v6 on v5

--- a/solution.py
+++ b/solution.py
@@ -12,7 +12,7 @@
 F32 = jnp.float32
 BF16 = jnp.bfloat16
 LANES = 128
-STEP_WINDOWS = 8
+STEP_WINDOWS = 16
 SORT_WINDOWS = 4
 SCALE_ROWS = 8
 MIB = 1024 * 1024
@@ -532,47 +532,47 @@
 def place_kernel(half_ref, blocks_ref, *refs, rows, cut):
     grad_w_ref, grad_v_ref, grad_b_ref, grad_c_ref = refs[-4:]
     step = pl.program_id(0)
-    steps = pl.num_programs(0)
+    channels = grad_w_ref.shape[1]
     late = rows - cut
-    for i in range(blocks_ref.shape[0]):
+    group = channels // cut
+
+    def copy(out_ref, i, row, column):
         scale = jnp.exp2(blocks_ref[i, 2 * rows:2 * rows + 1, :] - 14.0)
         for k in range(2):
-            lanes = slice(k * LANES, (k + 1) * LANES)
             block = blocks_ref[i, k * rows:(k + 1) * rows, :] * scale
-            grad_w_ref[i * late:(i + 1) * late, lanes] = block[cut:rows]
-            top = block[0:cut]
-            at = slice(i * cut, (i + 1) * cut)
-
-            @pl.when(step < steps // 2)
-            def _():
-                grad_c_ref[at, lanes] = top
-
-            @pl.when((step >= steps // 2) & (step < 3 * steps // 4))
-            def _():
-                grad_b_ref[at, lanes] = top
-
-            @pl.when(step >= 3 * steps // 4)
-            def _():
-                grad_v_ref[at, lanes] = top
+            grad_w_ref[i * late:(i + 1) * late, k * LANES:(k + 1) * LANES] = block[cut:rows]
+            out_ref[row:row + cut, column + k * LANES:column + (k + 1) * LANES] = block[0:cut]
+
+    @pl.when(step < 2)
+    def _():
+        for i in range(2 * group):
+            copy(grad_c_ref, i, i % group * cut, i // group * channels)
+
+    @pl.when(step == 2)
+    def _():
+        for i in range(2 * group):
+            copy(grad_b_ref, i, i % group * cut, i // group * channels)
+
+    @pl.when(step == 3)
+    def _():
+        for i in range(2 * group):
+            copy(grad_v_ref, i, i * cut, 0)
 
 
 def place_call(half, blocks, rows, cut, channels, bins, earlier=()):
     chips, total, _ = blocks.shape
+    group = channels // cut
     late = rows - cut
-    group = channels // cut
-    steps = chips // group
-    quarter = steps // 4
-    within = lambda i, low, count: jnp.clip(i - low, 0, count - 1)
     grid_spec = pltpu.PrefetchScalarGridSpec(
         num_scalar_prefetch=1,
-        grid=(steps,),
-        in_specs=[pl.BlockSpec((group, total, LANES), lambda i, h: (i, 0, 0))]
+        grid=(4,),
+        in_specs=[pl.BlockSpec((2 * group, total, LANES), lambda i, h: (i, 0, 0))]
         + [pl.BlockSpec(memory_space=pl.ANY)] * len(earlier),
         out_specs=[
-            pl.BlockSpec((group * late, channels), lambda i, h: (h[0] * steps + i, 0)),
-            pl.BlockSpec((channels, channels), lambda i, h: (h[0] * quarter + within(i, 3 * quarter, quarter), 0)),
-            pl.BlockSpec((channels, channels), lambda i, h: (0, h[0] * quarter + within(i, 2 * quarter, quarter))),
-            pl.BlockSpec((channels, channels), lambda i, h: (0, h[0] * 2 * quarter + within(i, 0, 2 * quarter))),
+            pl.BlockSpec((2 * group * late, channels), lambda i, h: (h[0] * 4 + i, 0)),
+            pl.BlockSpec((2 * channels, channels), lambda i, h: (h[0], 0)),
+            pl.BlockSpec((channels, 2 * channels), lambda i, h: (0, h[0])),
+            pl.BlockSpec((channels, 2 * channels), lambda i, h: (0, h[0] * 2 + jnp.minimum(i, 1))),
         ],
     )
     return pl.pallas_call(
@@ -585,7 +585,7 @@
             jax.ShapeDtypeStruct((channels, 4 * bins), F32),
         ],
         input_output_aliases={2 + k: k for k in range(len(earlier))},
-        compiler_params=pltpu.CompilerParams(vmem_limit_bytes=12 * MIB),
+        compiler_params=pltpu.CompilerParams(vmem_limit_bytes=16 * MIB),
         cost_estimate=pl.CostEstimate(flops=chips * total * LANES, bytes_accessed=8 * chips * total * LANES, transcendentals=0),
         name="place_gradients",
     )(half, blocks, *earlier)

time: 167 us -> 163 us (0.976)
  Pallas kernels: 36.6 us -> 31.6 us
    pallas_call x2, Pallas kernels: 8.41 us -> 4.88 us  [place_call(): pl.pallas_call(functools.partial(place_kernel, rows=rows, cut=cut), grid_...]
  transfers between devices with their start and end apart: 3 -> 3, of which waited for: 1 -> 2; matrix products, arithmetic and copies ran while one was open for 0% -> 0% of each run, Pallas kernels for 5% -> 3%
where the time goes in v6:
time: 163 us; the launch traced here: 162 us
  blocking collectives  121 us (74%)
  Pallas kernels  31.6 us (19%)
  starting transfers between devices  4.98 us (3%)
  waiting for transfers between devices  2.85 us (2%)
    all_to_all x6, blocking collectives, exchange(): return lax.all_to_all(values, axes, split_axis=0, concat_axis=0, tiled=True)  121 us
    pallas_call x1, Pallas kernels, middle_call(): pl.pallas_call(functools.partial(middle_kernel, quarter=quarter, cols=col...  12.9 us
    pallas_call x1, Pallas kernels, sums_call(): pl.pallas_call(functools.partial(sums_kernel, chunks=chunks, count=window...  5.64 us
    ppermute x3, starting transfers between devices, swap_cores(): return lax.ppermute(values, 'core', [(0, 1), (1, 0)])  4.98 us
    pallas_call x2, Pallas kernels, place_call(): pl.pallas_call(functools.partial(place_kernel, rows=rows, cut=cut), grid_...  4.88 us
    pallas_call x1, Pallas kernels, enc1_call(): pl.pallas_call(functools.partial(enc1_kernel, chunks=chunks, quarter=quar...  3.55 us
  transfers between devices with their start and end apart: 3, of which 2 were waited for; matrix products, arithmetic and copies ran while one was open for 0% of the time, Pallas kernels for 3%

profile of v6, /device:TPU:1, one launch (start us, length us, event | category | flops | bytes accessed | tf_op | source)
XLA Modules:
  0.0 162.2 jit_solution(14439432112230904190)
XLA Ops:
  0.6 0.0 copy-start
  0.6 0.0 copy-start.4
  0.7 5.6 %sort_and_sum.1 = (f32[4,1024,512]{2,1,0:T(8,128)S(1)}, f32[256,128]{1,0:T(8,128)S(1)}) custom-call(s32[16]{0:T(128)} %bitcast.16, bf16[16,256,512]{2,1,0:T(8,128)(2,1)} %spec_ref.1), custom_call_target="tpu_custom_call" | custom-call | tf_op jit(solution)/shard_map/sort_and_sum/pallas_call | solution.py:125
  6.3 21.6 %all_to_all.46 = f32[128,2,128]{2,1,0:T(2,128)S(1)} all-to-all(f32[128,2,128]{2,1,0:T(2,128)S(1)} %bitcast.13), channel_id=1, replica_groups=mesh['row'=8,'pair'=8,'core'=2] {'row','pair','core'}, dimensions={0} | all-to-all | bytes 262144 | tf_op jit(solution)/shard_map/all_to_all | solution.py:492
  27.9 1.1 sensor_stats.1
  28.9 13.6 %all_to_all.47 = f32[128,1,128]{2,1,0:T(1,128)S(1)} all-to-all(f32[128,1,128]{2,1,0:T(1,128)S(1)} %bitcast.12), channel_id=1, replica_groups=mesh['row'=8,'pair'=8,'core'=2] {'row','pair','core'}, dimensions={0} | all-to-all | bytes 131072 | tf_op jit(solution)/shard_map/all_to_all | solution.py:492
  42.6 0.0 copy-done
  42.6 0.0 copy-done.4
  42.6 0.0 copy-start.3
  42.6 3.6 %normalize_enc1.1 = (bf16[4,1024,512]{2,1,0:T(8,128)(2,1)S(1)}, f32[2,1024,256]{2,1,0:T(8,128)S(1)}, f32[16,16,512]{2,1,0:T(8,128)S(1)}) custom-call(s32[16]{0:T(128)S(1)} %copy-done.4, f32[4,1024,512]{2,1,0:T(8,128)S(1)} %get-tuple-element.24.log_ref, f32[128,128]{1,0:T(8,128)S(1)} %bitcast.11, bf16[2048,256]{1,0:T(8,128)(2,1)S(1)} %copy-done), custom_call_target="tpu_custom_call" | custom-call | tf_op jit(solution)/shard_map/normalize_enc1/pallas_call | solution.py:235
  46.2 14.9 %all_to_all.48.stat_ref = f32[16,16,512]{2,1,0:T(8,128)S(1)} all-to-all(f32[16,16,512]{2,1,0:T(8,128)S(1)} %get-tuple-element.28), channel_id=1, replica_groups=mesh['row'=8,'pair'=8,'core'=2] {'pair','core'}, dimensions={0} | all-to-all | bytes 1048576 | tf_op jit(solution)/shard_map/all_to_all | solution.py:492
  61.1 0.0 copy-done.3
  61.1 12.9 %middle.1 = (f32[2048,256]{1,0:T(8,128)S(1)}, f32[2048,256]{1,0:T(8,128)S(1)}, f32[2,1024,256]{2,1,0:T(8,128)S(1)}, f32[16,512]{1,0:T(8,128)S(1)}, f32[16,16,512]{2,1,0:T(8,128)S(1)}) custom-call(s32[16]{0:T(128)S(1)} %copy-done.4, s32[1]{0:T(128)} %bitcast.1.core_ref.half_ref, bf16[4,1024,512]{2,1,0:T(8,128)(2,1)S(1)} %get-tuple-element.26.normed_ref, ...), custom_call_target="tpu_custom_call" | custom-call | tf_op jit(solution)/shard_map/middle/pallas_call | solution.py:407
  74.0 1.2 collective-permute-start
  75.2 13.9 %all_to_all.49.sums_ref = f32[16,16,512]{2,1,0:T(8,128)S(1)} all-to-all(f32[16,16,512]{2,1,0:T(8,128)S(1)} %get-tuple-element.33), channel_id=1, replica_groups=mesh['row'=8,'pair'=8,'core'=2] {'pair','core'}, dimensions={0} | all-to-all | bytes 1048576 | tf_op jit(solution)/shard_map/all_to_all | solution.py:492
  89.1 3.2 %grad_enc1.1 = (f32[1024,256]{1,0:T(8,128)S(1)}, f32[1024,256]{1,0:T(8,128)S(1)}) custom-call(s32[16]{0:T(128)S(1)} %copy-done.4, s32[1]{0:T(128)} %bitcast.1.core_ref.half_ref, bf16[4,1024,512]{2,1,0:T(8,128)(2,1)S(1)} %get-tuple-element.26.normed_ref, f32[2,1024,256]{2,1,0:T(8,128)S(1)} %get-tuple-element.27.pre_ref, ...), custom_call_target="tpu_custom_call" | custom-call | tf_op jit(solution)/shard_map/grad_enc1/pallas_call | solution.py:478
  92.3 1.1 collective-permute-start.1
  93.5 2.3 %collective-permute-done.1 = f32[1024,256]{1,0:T(8,128)S(1)} collective-permute-done((f32[1024,256]{1,0:T(8,128)S(1)}, f32[1024,256]{1,0:T(8,128)S(1)}, u32[]{:S(2)}, u32[]{:S(2)}) %collective-permute-start.1) | collective-permute-done | bytes 1048608 | tf_op jit(solution)/shard_map/ppermute | solution.py:488
  95.8 0.2 add_convert_fusion.1
  95.9 0.0 collective-permute-done
  96.0 0.4 add_convert_fusion
  96.3 0.1 pad_maximum_fusion
  96.4 27.2 %all_to_all.50.in_ref = bf16[64,48,256]{2,1,0:T(8,128)(2,1)S(1)} all-to-all(bf16[64,48,256]{2,1,0:T(8,128)(2,1)S(1)} %pad_maximum_fusion), channel_id=1, replica_groups=mesh['row'=8,'pair'=8,'core'=2] {'row','pair'}, dimensions={0} | all-to-all | bytes 3145728 | tf_op jit(solution)/shard_map/all_to_all | solution.py:492
  123.6 0.4 owner_sum.1
  124.0 0.2 broadcast_in_dim.2
  124.2 29.4 %all_to_all.51 = f16[64,104,128]{2,1,0:T(8,128)(2,1)S(1)} all-to-all(f16[64,104,128]{2,1,0:T(8,128)(2,1)S(1)} %broadcast_in_dim.2), channel_id=1, replica_groups=mesh['row'=8,'pair'=8,'core'=2] {'row','pair'}, dimensions={0} | all-to-all | bytes 3407872 | tf_op jit(solution)/shard_map/all_to_all | solution.py:492
  153.7 2.7 %collective-permute-start.2 = (f16[64,104,128]{2,1,0:T(8,128)(2,1)S(1)}, f16[64,104,128]{2,1,0:T(8,128)(2,1)S(1)}, u32[]{:S(2)}, u32[]{:S(2)}) collective-permute-start(f16[64,104,128]{2,1,0:T(8,128)(2,1)S(1)} %all_to_all.51), channel_id=1, source_target_pairs={{0,1},{1,0},{2,3},{3,2},{4,5},{5,4},{6,7},{7,6},{8,9},{9,8},{10,11... | collective-permute-start | bytes 5111816 | tf_op jit(solution)/shard_map/ppermute | solution.py:488
  156.4 0.2 convert_element_type.19.blocks_ref
  156.6 2.4 %place_gradients.2 = (f32[2048,256]{1,0:T(8,128)}, f32[1024,256]{1,0:T(8,128)}, f32[256,1024]{1,0:T(8,128)}, f32[256,2048]{1,0:T(8,128)}) custom-call(s32[1]{0:T(128)} %bitcast.1.core_ref.half_ref, f32[64,104,128]{2,1,0:T(8,128)S(1)} %convert_element_type.19.blocks_ref), custom_call_target="tpu_custom_call" | custom-call | flops 851968 | bytes 6815744 | tf_op jit(solution)/shard_map/place_gradients/pallas_call | solution.py:578
  159.0 0.6 collective-permute-done.2
  159.6 0.2 convert_element_type.18.blocks_ref
  159.8 2.4 %place_gradients.3 = (f32[2048,256]{1,0:T(8,128)}, f32[1024,256]{1,0:T(8,128)}, f32[256,1024]{1,0:T(8,128)}, f32[256,2048]{1,0:T(8,128)}) custom-call(s32[1]{0:T(128)S(6)} %sub.3.half_ref, f32[64,104,128]{2,1,0:T(8,128)S(1)} %convert_element_type.18.blocks_ref, ...), custom_call_target="tpu_custom_call", output_to_operand_aliasing={{0}: (2, {}), {1}: (3, {}), {2}: (4, {}), {3}: (5, {})} | custom-call | flops 851968 | bytes 6815744 | tf_op jit(solution)/shard_map/place_gradients/pallas_call | solution.py:578
  (5 shorter events, 0.0 us)
Async XLA Ops:
  0.6 42.0 %copy-start = (bf16[2048,256]{1,0:T(8,128)(2,1)S(1)}, bf16[2048,256]{1,0:T(8,128)(2,1)}, u32[]{:S(2)}) copy-start(bf16[2048,256]{1,0:T(8,128)(2,1)} %w_ref.1) | copy-start | bytes 3145732
  0.6 42.0 %copy-start.4 = (s32[16]{0:T(128)S(1)}, s32[16]{0:T(128)}, u32[]{:S(2)}) copy-start(s32[16]{0:T(128)} %perm_ref.5) | copy-start | bytes 196
  42.6 18.5 %copy-start.1 = (bf16[256,2048]{1,0:T(8,128)(2,1)S(1)}, bf16[256,2048]{1,0:T(8,128)(2,1)}, u32[]{:S(2)}) copy-start(bf16[256,2048]{1,0:T(8,128)(2,1)} %c_ref.1) | copy-start | bytes 3145732
  42.6 18.5 %copy-start.2 = (bf16[1024,256]{1,0:T(8,128)(2,1)S(1)}, bf16[1024,256]{1,0:T(8,128)(2,1)}, u32[]{:S(2)}) copy-start(bf16[1024,256]{1,0:T(8,128)(2,1)} %v_ref.1) | copy-start | bytes 1572868
  42.6 18.5 %copy-start.3 = (bf16[256,1024]{1,0:T(8,128)(2,1)S(1)}, bf16[256,1024]{1,0:T(8,128)(2,1)}, u32[]{:S(2)}) copy-start(bf16[256,1024]{1,0:T(8,128)(2,1)} %b_ref.1) | copy-start | bytes 1572868
  74.0 21.9 %collective-permute-start = (f32[2048,256]{1,0:T(8,128)S(1)}, f32[2048,256]{1,0:T(8,128)S(1)}, u32[]{:S(2)}, u32[]{:S(2)}) collective-permute-start(f32[2048,256]{1,0:T(8,128)S(1)} %get-tuple-element.30), channel_id=1, source_target_pairs={{0,1},{1,0},{2,3},{3,2},{4,5},{5,4},{6,7},{7,6},{8,9},{9,8},{10,11... | collective-permute-start | bytes 6291464 | tf_op jit(solution)/shard_map/ppermute | solution.py:488
  92.3 3.4 %collective-permute-start.1 = (f32[1024,256]{1,0:T(8,128)S(1)}, f32[1024,256]{1,0:T(8,128)S(1)}, u32[]{:S(2)}, u32[]{:S(2)}) collective-permute-start(f32[1024,256]{1,0:T(8,128)S(1)} %get-tuple-element.35), channel_id=1, source_target_pairs={{0,1},{1,0},{2,3},{3,2},{4,5},{5,4},{6,7},{7,6},{8,9},{9,8},{10,11... | collective-permute-start | bytes 3145736 | tf_op jit(solution)/shard_map/ppermute | solution.py:488
  153.7 5.9 %collective-permute-start.2 = (f16[64,104,128]{2,1,0:T(8,128)(2,1)S(1)}, f16[64,104,128]{2,1,0:T(8,128)(2,1)S(1)}, u32[]{:S(2)}, u32[]{:S(2)}) collective-permute-start(f16[64,104,128]{2,1,0:T(8,128)(2,1)S(1)} %all_to_all.51), channel_id=1, source_target_pairs={{0,1},{1,0},{2,3},{3,2},{4,5},{5,4},{6,7},{7,6},{8,9},{9,8},{10,11... | collective-permute-start | bytes 5111816 | tf_op jit(solution)/shard_map/ppermute | solution.py:488

commit v7 on v6

--- a/solution.py
+++ b/solution.py
@@ -13,7 +13,7 @@
 BF16 = jnp.bfloat16
 LANES = 128
 STEP_WINDOWS = 16
-SORT_WINDOWS = 4
+SORT_WINDOWS = 8
 SCALE_ROWS = 8
 MIB = 1024 * 1024
 
@@ -74,12 +74,10 @@
     return (trainer // col_count) * per_row + trainer % per_row
 
 
-def sums_kernel(ids_ref, spec_ref, log_ref, out_ref, acc, lane, *, chunks, count):
+def sums_kernel(ids_ref, spec_ref, log_ref, out_ref, acc, *, chunks, count):
     step = pl.program_id(0)
     windows, frames, bins = spec_ref.shape
-    quarter = frames // 4
     rows = 16
-    log_ref = step_rows(log_ref, windows * quarter)
 
     for w in range(windows):
         def body(i, carry):
@@ -87,7 +85,7 @@
             start = pl.multiple_of(i * rows, rows)
             value = jnp.log(1.0 + spec_ref[w, pl.ds(start, rows), :].astype(F32))
             for k in range(chunks):
-                lane[w % 2, k, pl.ds(start, rows), :] = value[:, k * LANES:(k + 1) * LANES]
+                log_ref[step * windows + w, k, pl.ds(start, rows), :] = value[:, k * LANES:(k + 1) * LANES]
             value_sq = value * value
             return (total + value[0:8] + value[8:16], square + value_sq[0:8] + value_sq[8:16])
 
@@ -99,9 +97,6 @@
         pieces += [square[:, k * LANES:(k + 1) * LANES] for k in range(chunks)]
         start = pl.multiple_of((step * windows + w) * 2 * chunks, 2 * chunks)
         acc[pl.ds(start, 2 * chunks), :] = jnp.concatenate(pieces, axis=0)
-        for i in range(4):
-            for k in range(chunks):
-                log_ref[i, w * quarter:(w + 1) * quarter, k * LANES:(k + 1) * LANES] = lane[w % 2, k, pl.ds(i, quarter, stride=4), :]
 
     @pl.when(step == pl.num_programs(0) - 1)
     def _():
@@ -120,17 +115,17 @@
         grid=(windows // SORT_WINDOWS,),
         in_specs=[pl.BlockSpec((SORT_WINDOWS, frames, bins), lambda i, s: (i, 0, 0))],
         out_specs=[ON_CHIP, pl.BlockSpec((2 * LANES, LANES), lambda i, s: (0, 0))],
-        scratch_shapes=[pltpu.VMEM((2 * LANES, LANES), F32), pltpu.VMEM((2, chunks, frames, LANES), F32)],
+        scratch_shapes=[pltpu.VMEM((2 * LANES, LANES), F32)],
     )
     return pl.pallas_call(
         functools.partial(sums_kernel, chunks=chunks, count=windows),
         grid_spec=grid_spec,
         out_shape=[
-            pltpu.VMEM((4, windows * frames // 4, bins), F32),
+            pltpu.VMEM((windows, chunks, frames, LANES), F32),
             jax.ShapeDtypeStruct((2 * LANES, LANES), F32),
         ],
         compiler_params=pltpu.CompilerParams(vmem_limit_bytes=10 * MIB),
-        name="sort_and_sum",
+        name="log_and_sum",
     )(in_hbm(sensor_ids.reshape(windows)), in_hbm(spectra))
 
 
@@ -162,13 +157,14 @@
     )(received)
 
 
-def enc1_kernel(perm_ref, log_ref, coef_ref, w_ref, normed_ref, pre_ref, stat_ref, coef, stat, *, chunks, quarter, cols, copies):
+def enc1_kernel(perm_ref, log_ref, coef_ref, w_ref, normed_ref, pre_ref, stat_ref, coef, *, cols):
     step = pl.program_id(0)
-    bins = log_ref.shape[2]
+    all_windows, chunks, frames, _ = log_ref.shape
+    quarter = frames // 4
+    bins = chunks * LANES
     windows = STEP_WINDOWS
-    log_ref, normed_ref, pre_ref = (step_rows(ref, windows * quarter) for ref in (log_ref, normed_ref, pre_ref))
+    normed_ref, pre_ref = (step_rows(ref, windows * quarter) for ref in (normed_ref, pre_ref))
     channels = w_ref.shape[1]
-    all_windows = windows * pl.num_programs(0)
     width = 2 * chunks
 
     @pl.when(step == 0)
@@ -180,11 +176,11 @@
         both = coef[pl.ds(start, width), :]
         low, high = w * quarter, (w + 1) * quarter
         for k in range(chunks):
-            left, right = k * LANES, (k + 1) * LANES
             center = both[k:k + 1, :]
             factor = both[chunks + k:chunks + k + 1, :]
             for i in range(4):
-                normed_ref[i, low:high, left:right] = ((log_ref[i, low:high, left:right] - center) * factor).astype(BF16)
+                value = log_ref[step * windows + w, k, pl.ds(i, quarter, stride=4), :]
+                normed_ref[i, low:high, k * LANES:(k + 1) * LANES] = ((value - center) * factor).astype(BF16)
 
     w0, w1, w2, w3 = (w_ref[k * bins:(k + 1) * bins, :] for k in range(4))
     f0, f1, f2, f3 = (normed_ref[i] for i in range(4))
@@ -200,45 +196,28 @@
         diff_o = part_o - mean
         spread = (jnp.sum(diff_e * diff_e, axis=0, keepdims=True) + jnp.sum(diff_o * diff_o, axis=0, keepdims=True)) / (2 * quarter)
         place = group_rank(perm_ref, step * windows + w, all_windows, cols)
-        stat[pl.ds(place, 1), 0:channels] = mean
-        stat[pl.ds(place, 1), channels:2 * channels] = spread
-
-    @pl.when(step == pl.num_programs(0) - 1)
-    def _():
-        for d in range(copies):
-            stat_ref[d] = stat[...]
-
-
-def enc1_call(permutation, logs, coef, w_enc1, quarter, cols):
-    bins = logs.shape[2]
-    windows = logs.shape[1] // quarter
-    chunks = bins // LANES
+        stat_ref[pl.ds(place, 1), 0:channels] = mean
+        stat_ref[pl.ds(place, 1), channels:2 * channels] = spread
+
+
+def enc1_call(permutation, logs, coef, w_enc1, cols):
+    windows, chunks, frames, _ = logs.shape
     channels = w_enc1.shape[1]
+    rows = windows * frames // 4
     grid_spec = pltpu.PrefetchScalarGridSpec(
         num_scalar_prefetch=1,
         grid=(windows // STEP_WINDOWS,),
-        in_specs=[
-            ON_CHIP,
-            pl.BlockSpec((LANES, LANES), lambda i, p: (0, 0)),
-            ON_CHIP,
-        ],
-        out_specs=[
-            ON_CHIP,
-            ON_CHIP,
-            pl.BlockSpec((cols, windows, 2 * channels), lambda i, p: (0, 0, 0)),
-        ],
-        scratch_shapes=[
-            pltpu.VMEM((LANES, LANES), F32),
-            pltpu.VMEM((windows, 2 * channels), F32),
-        ],
+        in_specs=[ON_CHIP, pl.BlockSpec((LANES, LANES), lambda i, p: (0, 0)), ON_CHIP],
+        out_specs=[ON_CHIP] * 3,
+        scratch_shapes=[pltpu.VMEM((LANES, LANES), F32)],
     )
     return pl.pallas_call(
-        functools.partial(enc1_kernel, chunks=chunks, quarter=quarter, cols=cols, copies=cols),
+        functools.partial(enc1_kernel, cols=cols),
         grid_spec=grid_spec,
         out_shape=[
-            pltpu.VMEM((4, windows * quarter, bins), BF16),
-            pltpu.VMEM((2, windows * quarter, channels), F32),
-            jax.ShapeDtypeStruct((cols, windows, 2 * channels), F32),
+            pltpu.VMEM((4, rows, chunks * LANES), BF16),
+            pltpu.VMEM((2, rows, channels), F32),
+            pltpu.VMEM((windows, 2 * channels), F32),
         ],
         compiler_params=pltpu.CompilerParams(vmem_limit_bytes=16 * MIB),
         name="normalize_enc1",
@@ -265,7 +244,7 @@
 
 def middle_kernel(perm_ref, core_ref, normed_ref, pre_ref, stat_ref, v_ref, b_ref, c_ref,
                   own_ref, send_ref, back_ref, moment_ref, sums_ref,
-                  grads, moment, sums, *, quarter, cols, total_windows):
+                  grads, moment, *, quarter, cols, total_windows):
     step = pl.program_id(0)
     channels = v_ref.shape[1]
     bins = normed_ref.shape[2]
@@ -363,13 +342,11 @@
         first = jnp.sum(fold_e[low:high] + fold_o[low:high], axis=0, keepdims=True)
         second = jnp.sum(cross_e[low:high] + cross_o[low:high], axis=0, keepdims=True)
         place = group_rank(perm_ref, step * windows + w, all_windows, cols)
-        sums[pl.ds(place, 1), 0:ch] = first
-        sums[pl.ds(place, 1), ch:2 * ch] = second
+        sums_ref[pl.ds(place, 1), 0:ch] = first
+        sums_ref[pl.ds(place, 1), ch:2 * ch] = second
 
     @pl.when(step == pl.num_programs(0) - 1)
     def _():
-        for d in range(cols):
-            sums_ref[d] = sums[...]
         write_halves(core_ref, grads, own_ref, send_ref, (0, base_b, base_v, base_v + 4 * ch))
 
 
@@ -379,7 +356,6 @@
     windows = normed.shape[1] // quarter
     total = 4 * bins + 8 * channels
     whole2 = lambda i, p, c: (0, 0)
-    whole3 = lambda i, p, c: (0, 0, 0)
     grid_spec = pltpu.PrefetchScalarGridSpec(
         num_scalar_prefetch=2,
         grid=(windows // STEP_WINDOWS,),
@@ -396,11 +372,10 @@
             ON_CHIP,
             ON_CHIP,
             pl.BlockSpec((windows, 2 * channels), whole2),
-            pl.BlockSpec(stat.shape, whole3),
+            ON_CHIP,
         ],
         scratch_shapes=[
             pltpu.VMEM((total, channels), F32),
-            pltpu.VMEM((windows, 2 * channels), F32),
             pltpu.VMEM((windows, 2 * channels), F32),
         ],
     )
@@ -412,7 +387,7 @@
             pltpu.VMEM((total // 2, channels), F32),
             pltpu.VMEM(pre.shape, F32),
             jax.ShapeDtypeStruct((windows, 2 * channels), F32),
-            jax.ShapeDtypeStruct(stat.shape, F32),
+            pltpu.VMEM((windows, 2 * channels), F32),
         ],
         compiler_params=pltpu.CompilerParams(vmem_limit_bytes=30 * MIB),
         name="middle",
@@ -492,6 +467,33 @@
     return lax.all_to_all(values, axes, split_axis=0, concat_axis=0, tiled=True)
 
 
+def join_kernel(mine_ref, other_ref, out_ref, *, moments):
+    mine, other = mine_ref[...], other_ref[...]
+    total = mine + other
+    width = total.shape[1] // 2
+    if moments:
+        apart = 0.5 * (mine[:, 0:width] - other[:, 0:width])
+        total = jnp.concatenate([0.5 * total[:, 0:width], 0.5 * total[:, width:] + apart * apart], axis=1)
+    for d in range(out_ref.shape[0]):
+        out_ref[d] = total
+
+
+def join_cores(mine, chips, moments):
+    rows, width = mine.shape
+    return pl.pallas_call(
+        functools.partial(join_kernel, moments=moments),
+        in_specs=[ON_CHIP] * 2,
+        out_specs=ON_CHIP,
+        out_shape=pltpu.VMEM((chips, rows, width), F32),
+        compiler_params=pltpu.CompilerParams(vmem_limit_bytes=2 * MIB),
+        name="join_cores",
+    )(on_chip(mine), on_chip(swap_cores(mine)))
+
+
+def exchange_copies(copies):
+    return exchange(copies.reshape(-1, copies.shape[2]), "pair").reshape(copies.shape)
+
+
 def chip_sums(parts, axes, chips):
     total = [(own + swap_cores(send)).astype(BF16).reshape(chips, -1, own.shape[1]) for own, send in parts]
     total = jnp.concatenate(total, axis=1)
@@ -594,7 +596,6 @@
 def local(spectra, sensor_ids, permutation, w_enc1, w_enc2, w_dec1, w_dec2):
     windows, frames, bins = spectra.shape
     channels = w_enc1.shape[1]
-    col_axes = ("pair", "core")
     chip_axes = ("row", "pair")
     every = ("row", "pair", "core")
     cols = lax.axis_size("pair") * lax.axis_size("core")
@@ -610,11 +611,12 @@
     sums, core = lax.optimization_barrier((sums, core))
     sums = exchange(sums, every)
     coef = exchange(stats_call(sums, windows, chunks, sensors, WIN_SENSOR * frames), every)
-    normed, pre, stat = enc1_call(permutation, logs, coef, w_enc1, quarter, cols)
-    stat = exchange(stat.reshape(cols * windows, 2 * channels), col_axes).reshape(cols, windows, 2 * channels)
+    normed, pre, stat = enc1_call(permutation, logs, coef, w_enc1, cols)
+    stat = exchange_copies(join_cores(stat, cols // 2, True))
     own, send, back, moment, moments = middle_call(
         permutation, core, normed, pre, stat, w_enc2, w_dec1, w_dec2, quarter, cols, total_windows)
-    moments = exchange(moments.reshape(cols * windows, 2 * channels), col_axes).reshape(cols, windows, 2 * channels)
+    moments, send = lax.optimization_barrier((join_cores(moments, cols // 2, False), send))
+    moments = exchange_copies(moments)
     late = grad_call(permutation, core, normed, pre, back, moment, moments, quarter, cols)
     piece = owner_call(chip_sums([(own, send), late], chip_axes, chips))
     mine = gather_rows(piece, chip_axes, chips)

time: 163 us -> 158 us (0.969)
  blocking collectives: 121 us -> 115 us
  waiting for transfers between devices: 2.85 us -> 4.57 us
    all_to_all x6, blocking collectives: 121 us -> 115 us  [exchange(): return lax.all_to_all(values, axes, split_axis=0, concat_axis=0, tiled=True)]
    ppermute x3 -> x5, waiting for transfers between devices: 2.85 us -> 4.57 us  [swap_cores(): return lax.ppermute(values, 'core', [(0, 1), (1, 0)])]
    ppermute x3 -> x5, starting transfers between devices: 4.98 us -> 5.92 us  [swap_cores(): return lax.ppermute(values, 'core', [(0, 1), (1, 0)])]
    pallas_call x1 -> x3, Pallas kernels: 3.55 us -> 3.45 us  [the longest x1 3.41 us: enc1_call(): pl.pallas_call(functools.partial(enc1_kernel, cols=cols), grid_spec=grid_...]
  transfers between devices with their start and end apart: 3 -> 5, of which waited for: 2 -> 4; matrix products, arithmetic and copies ran while one was open for 0% -> 0% of each run, Pallas kernels for 3% -> 4%
where the time goes in v7:
time: 158 us
  blocking collectives  115 us (73%)
  Pallas kernels  30.7 us (19%)
  starting transfers between devices  5.92 us (4%)
  waiting for transfers between devices  4.57 us (3%)
    all_to_all x6, blocking collectives, exchange(): return lax.all_to_all(values, axes, split_axis=0, concat_axis=0, tiled=True)  115 us
    pallas_call x1, Pallas kernels, middle_call(): pl.pallas_call(functools.partial(middle_kernel, quarter=quarter, cols=col...  12.8 us
    ppermute x5, starting transfers between devices, swap_cores(): return lax.ppermute(values, 'core', [(0, 1), (1, 0)])  5.92 us
    pallas_call x1, Pallas kernels, sums_call(): pl.pallas_call(functools.partial(sums_kernel, chunks=chunks, count=window...  4.93 us
    pallas_call x2, Pallas kernels, place_call(): pl.pallas_call(functools.partial(place_kernel, rows=rows, cut=cut), grid_...  4.88 us
    ppermute x5, waiting for transfers between devices, swap_cores(): return lax.ppermute(values, 'core', [(0, 1), (1, 0)])  4.57 us
    pallas_call x1, Pallas kernels, enc1_call(): pl.pallas_call(functools.partial(enc1_kernel, cols=cols), grid_spec=grid_...  3.41 us
    pallas_call x1, Pallas kernels, grad_call(): pl.pallas_call(functools.partial(grad_kernel, quarter=quarter, cols=cols)...  3.21 us
  transfers between devices with their start and end apart: 5, of which 4 were waited for; matrix products, arithmetic and copies ran while one was open for 0% of the time, Pallas kernels for 4%

profile of v7, /device:TPU:1, one launch (start us, length us, event | category | flops | bytes accessed | tf_op | source)
XLA Modules:
  0.0 158.0 jit_solution(4985563948146986555)
XLA Ops:
  0.7 4.9 %log_and_sum.1 = (f32[16,4,256,128]{3,2,1,0:T(8,128)S(1)}, f32[256,128]{1,0:T(8,128)S(1)}) custom-call(s32[16]{0:T(128)} %bitcast.16, bf16[16,256,512]{2,1,0:T(8,128)(2,1)} %spec_ref.1), custom_call_target="tpu_custom_call" | custom-call | tf_op jit(solution)/shard_map/log_and_sum/pallas_call | solution.py:120
  5.6 21.6 %all_to_all.46 = f32[128,2,128]{2,1,0:T(2,128)S(1)} all-to-all(f32[128,2,128]{2,1,0:T(2,128)S(1)} %bitcast.13), channel_id=1, replica_groups=mesh['row'=8,'pair'=8,'core'=2] {'row','pair','core'}, dimensions={0} | all-to-all | bytes 262144 | tf_op jit(solution)/shard_map/all_to_all | solution.py:467
  27.2 1.1 sensor_stats.1
  28.2 13.6 %all_to_all.47 = f32[128,1,128]{2,1,0:T(1,128)S(1)} all-to-all(f32[128,1,128]{2,1,0:T(1,128)S(1)} %bitcast.12), channel_id=1, replica_groups=mesh['row'=8,'pair'=8,'core'=2] {'row','pair','core'}, dimensions={0} | all-to-all | bytes 131072 | tf_op jit(solution)/shard_map/all_to_all | solution.py:467
  41.9 0.0 copy-done.4
  41.9 0.0 copy-start.3
  41.9 3.4 %normalize_enc1.1 = (bf16[4,1024,512]{2,1,0:T(8,128)(2,1)S(1)}, f32[2,1024,256]{2,1,0:T(8,128)S(1)}, f32[16,512]{1,0:T(8,128)S(1)}) custom-call(s32[16]{0:T(128)S(1)} %copy-done.4, f32[16,4,256,128]{3,2,1,0:T(8,128)S(1)} %get-tuple-element.26.log_ref, f32[128,128]{1,0:T(8,128)S(1)} %bitcast.11, bf16[2048,256]{1,0:T(8,128)(2,1)S(1)} %copy-done), custom_call_target="tpu_custom_call" | custom-call | tf_op jit(solution)/shard_map/normalize_enc1/pallas_call | solution.py:214
  45.3 0.7 collective-permute-start
  46.0 0.9 collective-permute-done.other_ref
  46.9 11.2 %all_to_all.48.stat_ref = f32[8,16,512]{2,1,0:T(8,128)S(1)} all-to-all(f32[8,16,512]{2,1,0:T(8,128)S(1)} %join_cores.2), channel_id=1, replica_groups=mesh['row'=8,'pair'=8,'core'=2] {'pair'}, dimensions={0} | all-to-all | bytes 524288 | tf_op jit(solution)/shard_map/all_to_all | solution.py:467
  58.1 12.8 %middle.1 = (f32[2048,256]{1,0:T(8,128)S(1)}, f32[2048,256]{1,0:T(8,128)S(1)}, f32[2,1024,256]{2,1,0:T(8,128)S(1)}, f32[16,512]{1,0:T(8,128)S(1)}, f32[16,512]{1,0:T(8,128)S(1)}) custom-call(s32[16]{0:T(128)S(1)} %copy-done.4, s32[1]{0:T(128)} %bitcast.1.core_ref.half_ref, bf16[4,1024,512]{2,1,0:T(8,128)(2,1)S(1)} %get-tuple-element.28.normed_ref, ...), custom_call_target="tpu_custom_call" | custom-call | tf_op jit(solution)/shard_map/middle/pallas_call | solution.py:382
  70.9 1.3 collective-permute-start.1
  72.2 0.9 collective-permute-done.1.other_ref
  73.1 0.4 collective-permute-start.2
  73.5 11.3 %all_to_all.49.sums_ref = f32[8,16,512]{2,1,0:T(8,128)S(1)} all-to-all(f32[8,16,512]{2,1,0:T(8,128)S(1)} %join_cores.3), channel_id=1, replica_groups=mesh['row'=8,'pair'=8,'core'=2] {'pair'}, dimensions={0} | all-to-all | bytes 524288 | tf_op jit(solution)/shard_map/all_to_all | solution.py:467
  84.8 3.2 %grad_enc1.1 = (f32[1024,256]{1,0:T(8,128)S(1)}, f32[1024,256]{1,0:T(8,128)S(1)}) custom-call(s32[16]{0:T(128)S(1)} %copy-done.4, s32[1]{0:T(128)} %bitcast.1.core_ref.half_ref, bf16[4,1024,512]{2,1,0:T(8,128)(2,1)S(1)} %get-tuple-element.28.normed_ref, f32[2,1024,256]{2,1,0:T(8,128)S(1)} %get-tuple-element.29.pre_ref, ...), custom_call_target="tpu_custom_call" | custom-call | tf_op jit(solution)/shard_map/grad_enc1/pallas_call | solution.py:453
  88.0 0.9 collective-permute-start.3
  88.9 2.3 %collective-permute-done.3 = f32[1024,256]{1,0:T(8,128)S(1)} collective-permute-done((f32[1024,256]{1,0:T(8,128)S(1)}, f32[1024,256]{1,0:T(8,128)S(1)}, u32[]{:S(2)}, u32[]{:S(2)}) %collective-permute-start.3) | collective-permute-done | bytes 1048608 | tf_op jit(solution)/shard_map/ppermute | solution.py:463
  91.2 0.2 add_convert_fusion.1
  91.4 0.0 collective-permute-done.2
  91.4 0.4 add_convert_fusion
  91.8 0.1 pad_maximum_fusion
  91.9 27.2 %all_to_all.50.in_ref = bf16[64,48,256]{2,1,0:T(8,128)(2,1)S(1)} all-to-all(bf16[64,48,256]{2,1,0:T(8,128)(2,1)S(1)} %pad_maximum_fusion), channel_id=1, replica_groups=mesh['row'=8,'pair'=8,'core'=2] {'row','pair'}, dimensions={0} | all-to-all | bytes 3145728 | tf_op jit(solution)/shard_map/all_to_all | solution.py:467
  119.0 0.4 owner_sum.1
  119.4 0.2 broadcast_in_dim.2
  119.7 29.9 %all_to_all.51 = f16[64,104,128]{2,1,0:T(8,128)(2,1)S(1)} all-to-all(f16[64,104,128]{2,1,0:T(8,128)(2,1)S(1)} %broadcast_in_dim.2), channel_id=1, replica_groups=mesh['row'=8,'pair'=8,'core'=2] {'row','pair'}, dimensions={0} | all-to-all | bytes 3407872 | tf_op jit(solution)/shard_map/all_to_all | solution.py:467
  149.5 2.6 %collective-permute-start.4 = (f16[64,104,128]{2,1,0:T(8,128)(2,1)S(1)}, f16[64,104,128]{2,1,0:T(8,128)(2,1)S(1)}, u32[]{:S(2)}, u32[]{:S(2)}) collective-permute-start(f16[64,104,128]{2,1,0:T(8,128)(2,1)S(1)} %all_to_all.51), channel_id=1, source_target_pairs={{0,1},{1,0},{2,3},{3,2},{4,5},{5,4},{6,7},{7,6},{8,9},{9,8},{10,11... | collective-permute-start | bytes 5111816 | tf_op jit(solution)/shard_map/ppermute | solution.py:463
  152.1 0.2 convert_element_type.19.blocks_ref
  152.4 2.4 %place_gradients.2 = (f32[2048,256]{1,0:T(8,128)}, f32[1024,256]{1,0:T(8,128)}, f32[256,1024]{1,0:T(8,128)}, f32[256,2048]{1,0:T(8,128)}) custom-call(s32[1]{0:T(128)} %bitcast.1.core_ref.half_ref, f32[64,104,128]{2,1,0:T(8,128)S(1)} %convert_element_type.19.blocks_ref), custom_call_target="tpu_custom_call" | custom-call | flops 851968 | bytes 6815744 | tf_op jit(solution)/shard_map/place_gradients/pallas_call | solution.py:580
  154.8 0.6 collective-permute-done.4
  155.4 0.2 convert_element_type.18.blocks_ref
  155.6 2.4 %place_gradients.3 = (f32[2048,256]{1,0:T(8,128)}, f32[1024,256]{1,0:T(8,128)}, f32[256,1024]{1,0:T(8,128)}, f32[256,2048]{1,0:T(8,128)}) custom-call(s32[1]{0:T(128)S(6)} %sub.3.half_ref, f32[64,104,128]{2,1,0:T(8,128)S(1)} %convert_element_type.18.blocks_ref, ...), custom_call_target="tpu_custom_call", output_to_operand_aliasing={{0}: (2, {}), {1}: (3, {}), {2}: (4, {}), {3}: (5, {})} | custom-call | flops 851968 | bytes 6815744 | tf_op jit(solution)/shard_map/place_gradients/pallas_call | solution.py:580
  (11 shorter events, 0.1 us)
Async XLA Ops:
  0.6 41.3 %copy-start = (bf16[2048,256]{1,0:T(8,128)(2,1)S(1)}, bf16[2048,256]{1,0:T(8,128)(2,1)}, u32[]{:S(2)}) copy-start(bf16[2048,256]{1,0:T(8,128)(2,1)} %w_ref.1) | copy-start | bytes 3145732
  0.6 41.2 %copy-start.4 = (s32[16]{0:T(128)S(1)}, s32[16]{0:T(128)}, u32[]{:S(2)}) copy-start(s32[16]{0:T(128)} %perm_ref.5) | copy-start | bytes 196
  41.9 16.2 %copy-start.1 = (bf16[256,2048]{1,0:T(8,128)(2,1)S(1)}, bf16[256,2048]{1,0:T(8,128)(2,1)}, u32[]{:S(2)}) copy-start(bf16[256,2048]{1,0:T(8,128)(2,1)} %c_ref.1) | copy-start | bytes 3145732
  41.9 16.2 %copy-start.2 = (bf16[1024,256]{1,0:T(8,128)(2,1)S(1)}, bf16[1024,256]{1,0:T(8,128)(2,1)}, u32[]{:S(2)}) copy-start(bf16[1024,256]{1,0:T(8,128)(2,1)} %v_ref.1) | copy-start | bytes 1572868
  41.9 16.2 %copy-start.3 = (bf16[256,1024]{1,0:T(8,128)(2,1)S(1)}, bf16[256,1024]{1,0:T(8,128)(2,1)}, u32[]{:S(2)}) copy-start(bf16[256,1024]{1,0:T(8,128)(2,1)} %b_ref.1) | copy-start | bytes 1572868
  45.3 1.6 collective-permute-start
  70.9 2.1 %collective-permute-start.1 = (f32[16,512]{1,0:T(8,128)S(1)}, f32[16,512]{1,0:T(8,128)S(1)}, u32[]{:S(2)}, u32[]{:S(2)}) collective-permute-start(f32[16,512]{1,0:T(8,128)S(1)} %get-tuple-element.32.mine_ref), channel_id=1, source_target_pairs={{0,1},{1,0},{2,3},{3,2},{4,5},{5,4},{6,7},{7,6},{8,9},{9,8},{10,11... | collective-permute-start | bytes 98312 | tf_op jit(solution)/shard_map/ppermute | solution.py:463
  73.1 18.3 %collective-permute-start.2 = (f32[2048,256]{1,0:T(8,128)S(1)}, f32[2048,256]{1,0:T(8,128)S(1)}, u32[]{:S(2)}, u32[]{:S(2)}) collective-permute-start(f32[2048,256]{1,0:T(8,128)S(1)} %get-tuple-element.34), channel_id=1, source_target_pairs={{0,1},{1,0},{2,3},{3,2},{4,5},{5,4},{6,7},{7,6},{8,9},{9,8},{10,11... | collective-permute-start | bytes 6291464 | tf_op jit(solution)/shard_map/ppermute | solution.py:463
  88.0 3.2 %collective-permute-start.3 = (f32[1024,256]{1,0:T(8,128)S(1)}, f32[1024,256]{1,0:T(8,128)S(1)}, u32[]{:S(2)}, u32[]{:S(2)}) collective-permute-start(f32[1024,256]{1,0:T(8,128)S(1)} %get-tuple-element.39), channel_id=1, source_target_pairs={{0,1},{1,0},{2,3},{3,2},{4,5},{5,4},{6,7},{7,6},{8,9},{9,8},{10,11... | collective-permute-start | bytes 3145736 | tf_op jit(solution)/shard_map/ppermute | solution.py:463
  149.5 5.9 %collective-permute-start.4 = (f16[64,104,128]{2,1,0:T(8,128)(2,1)S(1)}, f16[64,104,128]{2,1,0:T(8,128)(2,1)S(1)}, u32[]{:S(2)}, u32[]{:S(2)}) collective-permute-start(f16[64,104,128]{2,1,0:T(8,128)(2,1)S(1)} %all_to_all.51), channel_id=1, source_target_pairs={{0,1},{1,0},{2,3},{3,2},{4,5},{5,4},{6,7},{7,6},{8,9},{9,8},{10,11... | collective-permute-start | bytes 5111816 | tf_op jit(solution)/shard_map/ppermute | solution.py:463

commit v8 on v7

--- a/solution.py
+++ b/solution.py
@@ -74,7 +74,7 @@
     return (trainer // col_count) * per_row + trainer % per_row
 
 
-def sums_kernel(ids_ref, spec_ref, log_ref, out_ref, acc, *, chunks, count):
+def sums_kernel(ids_ref, core_ref, spec_ref, log_ref, own_ref, send_ref, acc, turned, *, chunks, count):
     step = pl.program_id(0)
     windows, frames, bins = spec_ref.shape
     rows = 16
@@ -100,39 +100,67 @@
 
     @pl.when(step == pl.num_programs(0) - 1)
     def _():
-        acc[LANES:2 * LANES, :] = jnp.zeros((LANES, LANES), F32)
+        half = LANES // 2
+        turned[...] = acc[...].T
+        own_ref[0:half, :] = turned[pl.ds(pl.multiple_of(core_ref[0] * half, half), half), :]
+        send_ref[0:half, :] = turned[pl.ds(pl.multiple_of((1 - core_ref[0]) * half, half), half), :]
+        lanes = lax.broadcasted_iota(jnp.int32, (8, LANES), 1)
+        ids = jnp.zeros((8, LANES), jnp.int32)
         for w in range(count):
-            acc[LANES + w:LANES + w + 1, :] = jnp.full((1, LANES), ids_ref[w], jnp.int32).astype(F32)
-        out_ref[pl.ds(0, LANES, stride=2), :] = acc[0:LANES, :].T
-        out_ref[pl.ds(1, LANES, stride=2), :] = acc[LANES:2 * LANES, :].T
-
-
-def sums_call(spectra, sensor_ids):
+            ids = jnp.where(lanes == w, ids_ref[w], ids)
+        own_ref[half:, :] = ids.astype(F32)
+        send_ref[half:, :] = ids.astype(F32)
+
+
+def sums_call(spectra, sensor_ids, core):
     windows, frames, bins = spectra.shape
     chunks = bins // LANES
     grid_spec = pltpu.PrefetchScalarGridSpec(
-        num_scalar_prefetch=1,
+        num_scalar_prefetch=2,
         grid=(windows // SORT_WINDOWS,),
-        in_specs=[pl.BlockSpec((SORT_WINDOWS, frames, bins), lambda i, s: (i, 0, 0))],
-        out_specs=[ON_CHIP, pl.BlockSpec((2 * LANES, LANES), lambda i, s: (0, 0))],
-        scratch_shapes=[pltpu.VMEM((2 * LANES, LANES), F32)],
+        in_specs=[pl.BlockSpec((SORT_WINDOWS, frames, bins), lambda i, s, c: (i, 0, 0))],
+        out_specs=[ON_CHIP] * 3,
+        scratch_shapes=[pltpu.VMEM((LANES, LANES), F32)] * 2,
     )
     return pl.pallas_call(
         functools.partial(sums_kernel, chunks=chunks, count=windows),
         grid_spec=grid_spec,
         out_shape=[
             pltpu.VMEM((windows, chunks, frames, LANES), F32),
-            jax.ShapeDtypeStruct((2 * LANES, LANES), F32),
+            pltpu.VMEM((LANES // 2 + 8, LANES), F32),
+            pltpu.VMEM((LANES // 2 + 8, LANES), F32),
         ],
         compiler_params=pltpu.CompilerParams(vmem_limit_bytes=10 * MIB),
         name="log_and_sum",
-    )(in_hbm(sensor_ids.reshape(windows)), in_hbm(spectra))
+    )(in_hbm(sensor_ids.reshape(windows)), core, in_hbm(spectra))
+
+
+def pack_kernel(mine_ref, other_ref, out_ref, *, count):
+    half = LANES // 2
+    out_ref[pl.ds(0, half, stride=4), :] = mine_ref[0:half, :]
+    out_ref[pl.ds(1, half, stride=4), :] = other_ref[0:half, :]
+    ids = mine_ref[half:half + 8, :] + pltpu.roll(other_ref[half:half + 8, :], count, 1)
+    out_ref[pl.ds(2, half, stride=4), :] = jnp.broadcast_to(ids[0:1, :], (half, LANES))
+    out_ref[pl.ds(3, half, stride=4), :] = jnp.zeros((half, LANES), F32)
+
+
+def pack_call(mine, other, count):
+    return pl.pallas_call(
+        functools.partial(pack_kernel, count=count),
+        in_specs=[ON_CHIP] * 2,
+        out_specs=ON_CHIP,
+        out_shape=pltpu.VMEM((2 * LANES, LANES), F32),
+        compiler_params=pltpu.CompilerParams(vmem_limit_bytes=2 * MIB),
+        name="pack_sums",
+    )(on_chip(mine), on_chip(other))
 
 
 def stats_kernel(in_ref, out_ref, *, windows, chunks, sensors, per_sensor):
     width = 2 * chunks
-    data = in_ref[pl.ds(0, LANES, stride=2), :].T
-    labels = in_ref[pl.ds(1, LANES, stride=2), :].T
+    half = LANES // 2
+    data = jnp.concatenate([in_ref[pl.ds(n, half, stride=4), :] for n in range(2)], axis=0).T
+    ids = in_ref[pl.ds(2, half, stride=4), :].T
+    labels = jnp.concatenate([ids[0:windows], ids[windows:2 * windows]], axis=1)
     sensor_rows = lax.broadcasted_iota(jnp.int32, (sensors, LANES), 0).astype(F32)
     tables = [(sensor_rows == labels[w:w + 1, :]).astype(F32).astype(BF16) for w in range(windows)]
     table = jnp.concatenate(tables, axis=1)
@@ -145,7 +173,9 @@
     back = dot(jnp.concatenate(split3(both), axis=0), table)
     back = back[0:width] + back[width:2 * width] + back[2 * width:3 * width]
     rows = jnp.concatenate([back[:, w * LANES:(w + 1) * LANES] for w in range(windows)], axis=0)
-    out_ref[...] = rows.T
+    rows = rows.T
+    for n in range(2):
+        out_ref[pl.ds(n, half, stride=2), :] = rows[n * half:(n + 1) * half]
 
 
 def stats_call(received, windows, chunks, sensors, per_sensor):
@@ -157,7 +187,7 @@
     )(received)
 
 
-def enc1_kernel(perm_ref, log_ref, coef_ref, w_ref, normed_ref, pre_ref, stat_ref, coef, *, cols):
+def enc1_kernel(perm_ref, core_ref, log_ref, coef_ref, other_ref, w_ref, normed_ref, pre_ref, stat_ref, coef, *, cols):
     step = pl.program_id(0)
     all_windows, chunks, frames, _ = log_ref.shape
     quarter = frames // 4
@@ -169,7 +199,11 @@
 
     @pl.when(step == 0)
     def _():
-        coef[...] = coef_ref[...].T
+        half = LANES // 2
+        own = pl.multiple_of(core_ref[0] * half, half)
+        coef[pl.ds(own, half), :] = coef_ref[pl.ds(0, half, stride=2), :]
+        coef[pl.ds(half - own, half), :] = other_ref[pl.ds(1, half, stride=2), :]
+        coef[...] = coef[...].T
 
     for w in range(windows):
         start = pl.multiple_of((step * windows + w) * width, width)
@@ -200,14 +234,14 @@
         stat_ref[pl.ds(place, 1), channels:2 * channels] = spread
 
 
-def enc1_call(permutation, logs, coef, w_enc1, cols):
+def enc1_call(permutation, core, logs, coef, other, w_enc1, cols):
     windows, chunks, frames, _ = logs.shape
     channels = w_enc1.shape[1]
     rows = windows * frames // 4
     grid_spec = pltpu.PrefetchScalarGridSpec(
-        num_scalar_prefetch=1,
+        num_scalar_prefetch=2,
         grid=(windows // STEP_WINDOWS,),
-        in_specs=[ON_CHIP, pl.BlockSpec((LANES, LANES), lambda i, p: (0, 0)), ON_CHIP],
+        in_specs=[ON_CHIP] * 4,
         out_specs=[ON_CHIP] * 3,
         scratch_shapes=[pltpu.VMEM((LANES, LANES), F32)],
     )
@@ -221,7 +255,7 @@
         ],
         compiler_params=pltpu.CompilerParams(vmem_limit_bytes=16 * MIB),
         name="normalize_enc1",
-    )(permutation, on_chip(logs), coef, on_chip(w_enc1))
+    )(permutation, core, on_chip(logs), on_chip(coef), on_chip(other), on_chip(w_enc1))
 
 
 def window_rows(perm_ref, table, step, windows, quarter, all_windows, cols, first, last):
@@ -597,7 +631,6 @@
     windows, frames, bins = spectra.shape
     channels = w_enc1.shape[1]
     chip_axes = ("row", "pair")
-    every = ("row", "pair", "core")
     cols = lax.axis_size("pair") * lax.axis_size("core")
     chips = lax.axis_size("row") * lax.axis_size("pair")
     total_windows = windows * lax.axis_size("row") * cols
@@ -607,11 +640,10 @@
     core_index = lax.axis_index("core")
     core = core_index.astype(jnp.int32).reshape(1)
 
-    logs, sums = sums_call(spectra, sensor_ids)
-    sums, core = lax.optimization_barrier((sums, core))
-    sums = exchange(sums, every)
-    coef = exchange(stats_call(sums, windows, chunks, sensors, WIN_SENSOR * frames), every)
-    normed, pre, stat = enc1_call(permutation, logs, coef, w_enc1, cols)
+    logs, mine, send = sums_call(spectra, sensor_ids, core)
+    sums = exchange(pack_call(mine, swap_cores(send), windows), chip_axes)
+    coef = exchange(stats_call(sums, windows, chunks, sensors, WIN_SENSOR * frames), chip_axes)
+    normed, pre, stat = enc1_call(permutation, core, logs, coef, swap_cores(coef), w_enc1, cols)
     stat = exchange_copies(join_cores(stat, cols // 2, True))
     own, send, back, moment, moments = middle_call(
         permutation, core, normed, pre, stat, w_enc2, w_dec1, w_dec2, quarter, cols, total_windows)

time: 158 us -> 162 us (1.025)
  starting transfers between devices: 5.92 us -> 10.1 us
  blocking collectives: 115 us -> 112 us
  waiting for transfers between devices: 4.57 us -> 6.34 us
    ppermute x5 -> x7, starting transfers between devices: 5.92 us -> 10.1 us  [swap_cores(): return lax.ppermute(values, 'core', [(0, 1), (1, 0)])]
    all_to_all x6, blocking collectives: 115 us -> 112 us  [exchange(): return lax.all_to_all(values, axes, split_axis=0, concat_axis=0, tiled=True)]
    ppermute x5 -> x7, waiting for transfers between devices: 4.57 us -> 6.34 us  [swap_cores(): return lax.ppermute(values, 'core', [(0, 1), (1, 0)])]
  transfers between devices with their start and end apart: 5 -> 7, of which waited for: 4 -> 6; matrix products, arithmetic and copies ran while one was open for 0% -> 0% of each run, Pallas kernels for 4% -> 3%
where the time goes in v8:
time: 162 us
  blocking collectives  112 us (69%)
  Pallas kernels  30.7 us (19%)
  starting transfers between devices  10.1 us (6%)
  waiting for transfers between devices  6.34 us (4%)
    all_to_all x6, blocking collectives, exchange(): return lax.all_to_all(values, axes, split_axis=0, concat_axis=0, tiled=True)  112 us
    pallas_call x1, Pallas kernels, middle_call(): pl.pallas_call(functools.partial(middle_kernel, quarter=quarter, cols=col...  12.8 us
    ppermute x7, starting transfers between devices, swap_cores(): return lax.ppermute(values, 'core', [(0, 1), (1, 0)])  10.1 us
    ppermute x7, waiting for transfers between devices, swap_cores(): return lax.ppermute(values, 'core', [(0, 1), (1, 0)])  6.34 us
    pallas_call x1, Pallas kernels, sums_call(): pl.pallas_call(functools.partial(sums_kernel, chunks=chunks, count=window...  4.93 us
    pallas_call x2, Pallas kernels, place_call(): pl.pallas_call(functools.partial(place_kernel, rows=rows, cut=cut), grid_...  4.88 us
    pallas_call x1, Pallas kernels, enc1_call(): pl.pallas_call(functools.partial(enc1_kernel, cols=cols), grid_spec=grid_...  3.4 us
  transfers between devices with their start and end apart: 7, of which 6 were waited for; matrix products, arithmetic and copies ran while one was open for 0% of the time, Pallas kernels for 3%

profile of v8, /device:TPU:1, one launch (start us, length us, event | category | flops | bytes accessed | tf_op | source)
XLA Modules:
  0.0 161.6 jit_solution(15421997880006837066)
XLA Ops:
  0.7 4.9 %log_and_sum.1 = (f32[16,4,256,128]{3,2,1,0:T(8,128)S(1)}, f32[72,128]{1,0:T(8,128)S(1)}, f32[72,128]{1,0:T(8,128)S(1)}) custom-call(s32[16]{0:T(128)} %bitcast.15, s32[1]{0:T(128)} %bitcast.core_ref.half_ref, bf16[16,256,512]{2,1,0:T(8,128)(2,1)} %spec_ref.1), custom_call_target="tpu_custom_call" | custom-call | tf_op jit(solution)/shard_map/log_and_sum/pallas_call | solution.py:125
  5.6 1.5 collective-permute-start
  7.1 0.9 collective-permute-done.other_ref
  8.0 19.7 %all_to_all.46 = f32[64,4,128]{2,1,0:T(4,128)S(1)} all-to-all(f32[64,4,128]{2,1,0:T(4,128)S(1)} %bitcast.8), channel_id=1, replica_groups=mesh['row'=8,'pair'=8,'core'=2] {'row','pair'}, dimensions={0} | all-to-all | bytes 262144 | tf_op jit(solution)/shard_map/all_to_all | solution.py:501
  27.7 1.1 sensor_stats.1
  28.8 13.2 %all_to_all.47 = f32[64,2,128]{2,1,0:T(2,128)S(1)} all-to-all(f32[64,2,128]{2,1,0:T(2,128)S(1)} %bitcast.12), channel_id=1, replica_groups=mesh['row'=8,'pair'=8,'core'=2] {'row','pair'}, dimensions={0} | all-to-all | bytes 131072 | tf_op jit(solution)/shard_map/all_to_all | solution.py:501
  42.1 2.9 %collective-permute-start.1 = (f32[128,128]{1,0:T(8,128)S(1)}, f32[128,128]{1,0:T(8,128)S(1)}, u32[]{:S(2)}, u32[]{:S(2)}) collective-permute-start(f32[128,128]{1,0:T(8,128)S(1)} %bitcast.10), channel_id=1, source_target_pairs={{0,1},{1,0},{2,3},{3,2},{4,5},{5,4},{6,7},{7,6},{8,9},{9,8},{10,11... | collective-permute-start | bytes 196616 | tf_op jit(solution)/shard_map/ppermute | solution.py:497
  45.0 0.9 collective-permute-done.1.other_ref
  45.9 3.4 %normalize_enc1.1 = (bf16[4,1024,512]{2,1,0:T(8,128)(2,1)S(1)}, f32[2,1024,256]{2,1,0:T(8,128)S(1)}, f32[16,512]{1,0:T(8,128)S(1)}) custom-call(s32[16]{0:T(128)S(1)} %copy-done.4, s32[1]{0:T(128)} %bitcast.core_ref.half_ref, f32[16,4,256,128]{3,2,1,0:T(8,128)S(1)} %get-tuple-element.23.log_ref, f32[128,128]{1,0:T(8,128)S(1)} %bitcast.11, ...), custom_call_target="tpu_custom_call" | custom-call | tf_op jit(solution)/shard_map/normalize_enc1/pallas_call | solution.py:248
  49.3 0.4 collective-permute-start.2
  49.7 0.9 collective-permute-done.2.other_ref
  50.6 11.1 %all_to_all.48.stat_ref = f32[8,16,512]{2,1,0:T(8,128)S(1)} all-to-all(f32[8,16,512]{2,1,0:T(8,128)S(1)} %join_cores.2), channel_id=1, replica_groups=mesh['row'=8,'pair'=8,'core'=2] {'pair'}, dimensions={0} | all-to-all | bytes 524288 | tf_op jit(solution)/shard_map/all_to_all | solution.py:501
  61.8 12.8 %middle.1 = (f32[2048,256]{1,0:T(8,128)S(1)}, f32[2048,256]{1,0:T(8,128)S(1)}, f32[2,1024,256]{2,1,0:T(8,128)S(1)}, f32[16,512]{1,0:T(8,128)S(1)}, f32[16,512]{1,0:T(8,128)S(1)}) custom-call(s32[16]{0:T(128)S(1)} %copy-done.4, s32[1]{0:T(128)} %bitcast.core_ref.half_ref, bf16[4,1024,512]{2,1,0:T(8,128)(2,1)S(1)} %get-tuple-element.26.normed_ref, ...), custom_call_target="tpu_custom_call" | custom-call | tf_op jit(solution)/shard_map/middle/pallas_call | solution.py:416
  74.6 1.3 collective-permute-start.3
  75.9 0.9 collective-permute-done.3.other_ref
  76.8 0.4 collective-permute-start.4
  77.2 11.3 %all_to_all.49.sums_ref = f32[8,16,512]{2,1,0:T(8,128)S(1)} all-to-all(f32[8,16,512]{2,1,0:T(8,128)S(1)} %join_cores.3), channel_id=1, replica_groups=mesh['row'=8,'pair'=8,'core'=2] {'pair'}, dimensions={0} | all-to-all | bytes 524288 | tf_op jit(solution)/shard_map/all_to_all | solution.py:501
  88.5 3.1 %grad_enc1.1 = (f32[1024,256]{1,0:T(8,128)S(1)}, f32[1024,256]{1,0:T(8,128)S(1)}) custom-call(s32[16]{0:T(128)S(1)} %copy-done.4, s32[1]{0:T(128)} %bitcast.core_ref.half_ref, bf16[4,1024,512]{2,1,0:T(8,128)(2,1)S(1)} %get-tuple-element.26.normed_ref, f32[2,1024,256]{2,1,0:T(8,128)S(1)} %get-tuple-element.27.pre_ref, ...), custom_call_target="tpu_custom_call" | custom-call | tf_op jit(solution)/shard_map/grad_enc1/pallas_call | solution.py:487
  91.7 0.9 collective-permute-start.5
  92.5 2.3 %collective-permute-done.5 = f32[1024,256]{1,0:T(8,128)S(1)} collective-permute-done((f32[1024,256]{1,0:T(8,128)S(1)}, f32[1024,256]{1,0:T(8,128)S(1)}, u32[]{:S(2)}, u32[]{:S(2)}) %collective-permute-start.5) | collective-permute-done | bytes 1048608 | tf_op jit(solution)/shard_map/ppermute | solution.py:497
  94.8 0.2 add_convert_fusion.1
  95.0 0.4 add_convert_fusion
  95.5 27.1 %all_to_all.50.in_ref = bf16[64,48,256]{2,1,0:T(8,128)(2,1)S(1)} all-to-all(bf16[64,48,256]{2,1,0:T(8,128)(2,1)S(1)} %pad_maximum_fusion), channel_id=1, replica_groups=mesh['row'=8,'pair'=8,'core'=2] {'row','pair'}, dimensions={0} | all-to-all | bytes 3145728 | tf_op jit(solution)/shard_map/all_to_all | solution.py:501
  122.6 0.4 owner_sum.1
  123.0 0.2 broadcast_in_dim.2
  123.2 29.9 %all_to_all.51 = f16[64,104,128]{2,1,0:T(8,128)(2,1)S(1)} all-to-all(f16[64,104,128]{2,1,0:T(8,128)(2,1)S(1)} %broadcast_in_dim.2), channel_id=1, replica_groups=mesh['row'=8,'pair'=8,'core'=2] {'row','pair'}, dimensions={0} | all-to-all | bytes 3407872 | tf_op jit(solution)/shard_map/all_to_all | solution.py:501
  153.1 2.6 %collective-permute-start.6 = (f16[64,104,128]{2,1,0:T(8,128)(2,1)S(1)}, f16[64,104,128]{2,1,0:T(8,128)(2,1)S(1)}, u32[]{:S(2)}, u32[]{:S(2)}) collective-permute-start(f16[64,104,128]{2,1,0:T(8,128)(2,1)S(1)} %all_to_all.51), channel_id=1, source_target_pairs={{0,1},{1,0},{2,3},{3,2},{4,5},{5,4},{6,7},{7,6},{8,9},{9,8},{10,11... | collective-permute-start | bytes 5111816 | tf_op jit(solution)/shard_map/ppermute | solution.py:497
  155.7 0.2 convert_element_type.19.blocks_ref
  155.9 2.4 %place_gradients.2 = (f32[2048,256]{1,0:T(8,128)}, f32[1024,256]{1,0:T(8,128)}, f32[256,1024]{1,0:T(8,128)}, f32[256,2048]{1,0:T(8,128)}) custom-call(s32[1]{0:T(128)} %bitcast.core_ref.half_ref, f32[64,104,128]{2,1,0:T(8,128)S(1)} %convert_element_type.19.blocks_ref), custom_call_target="tpu_custom_call" | custom-call | flops 851968 | bytes 6815744 | tf_op jit(solution)/shard_map/place_gradients/pallas_call | solution.py:614
  158.4 0.6 collective-permute-done.6
  158.9 0.2 convert_element_type.18.blocks_ref
  159.2 2.4 %place_gradients.3 = (f32[2048,256]{1,0:T(8,128)}, f32[1024,256]{1,0:T(8,128)}, f32[256,1024]{1,0:T(8,128)}, f32[256,2048]{1,0:T(8,128)}) custom-call(s32[1]{0:T(128)S(6)} %sub.3.half_ref, f32[64,104,128]{2,1,0:T(8,128)S(1)} %convert_element_type.18.blocks_ref, ...), custom_call_target="tpu_custom_call", output_to_operand_aliasing={{0}: (2, {}), {1}: (3, {}), {2}: (4, {}), {3}: (5, {})} | custom-call | flops 851968 | bytes 6815744 | tf_op jit(solution)/shard_map/place_gradients/pallas_call | solution.py:614
  (16 shorter events, 0.3 us)
Async XLA Ops:
  0.6 45.2 %copy-start = (bf16[2048,256]{1,0:T(8,128)(2,1)S(1)}, bf16[2048,256]{1,0:T(8,128)(2,1)}, u32[]{:S(2)}) copy-start(bf16[2048,256]{1,0:T(8,128)(2,1)} %w_ref.1) | copy-start | bytes 3145732
  0.6 45.2 %copy-start.4 = (s32[16]{0:T(128)S(1)}, s32[16]{0:T(128)}, u32[]{:S(2)}) copy-start(s32[16]{0:T(128)} %perm_ref.5) | copy-start | bytes 196
  5.6 2.4 %collective-permute-start = (f32[72,128]{1,0:T(8,128)S(1)}, f32[72,128]{1,0:T(8,128)S(1)}, u32[]{:S(2)}, u32[]{:S(2)}) collective-permute-start(f32[72,128]{1,0:T(8,128)S(1)} %get-tuple-element.25), channel_id=1, source_target_pairs={{0,1},{1,0},{2,3},{3,2},{4,5},{5,4},{6,7},{7,6},{8,9},{9,8},{10,11... | collective-permute-start | bytes 110600 | tf_op jit(solution)/shard_map/ppermute | solution.py:497
  42.1 3.8 %collective-permute-start.1 = (f32[128,128]{1,0:T(8,128)S(1)}, f32[128,128]{1,0:T(8,128)S(1)}, u32[]{:S(2)}, u32[]{:S(2)}) collective-permute-start(f32[128,128]{1,0:T(8,128)S(1)} %bitcast.10), channel_id=1, source_target_pairs={{0,1},{1,0},{2,3},{3,2},{4,5},{5,4},{6,7},{7,6},{8,9},{9,8},{10,11... | collective-permute-start | bytes 196616 | tf_op jit(solution)/shard_map/ppermute | solution.py:497
  45.9 15.9 %copy-start.1 = (bf16[256,2048]{1,0:T(8,128)(2,1)S(1)}, bf16[256,2048]{1,0:T(8,128)(2,1)}, u32[]{:S(2)}) copy-start(bf16[256,2048]{1,0:T(8,128)(2,1)} %c_ref.1) | copy-start | bytes 3145732
  45.9 15.9 %copy-start.2 = (bf16[1024,256]{1,0:T(8,128)(2,1)S(1)}, bf16[1024,256]{1,0:T(8,128)(2,1)}, u32[]{:S(2)}) copy-start(bf16[1024,256]{1,0:T(8,128)(2,1)} %v_ref.1) | copy-start | bytes 1572868
  45.9 15.9 %copy-start.3 = (bf16[256,1024]{1,0:T(8,128)(2,1)S(1)}, bf16[256,1024]{1,0:T(8,128)(2,1)}, u32[]{:S(2)}) copy-start(bf16[256,1024]{1,0:T(8,128)(2,1)} %b_ref.1) | copy-start | bytes 1572868
  49.3 1.3 collective-permute-start.2
  74.6 2.1 %collective-permute-start.3 = (f32[16,512]{1,0:T(8,128)S(1)}, f32[16,512]{1,0:T(8,128)S(1)}, u32[]{:S(2)}, u32[]{:S(2)}) collective-permute-start(f32[16,512]{1,0:T(8,128)S(1)} %get-tuple-element.30.mine_ref), channel_id=1, source_target_pairs={{0,1},{1,0},{2,3},{3,2},{4,5},{5,4},{6,7},{7,6},{8,9},{9,8},{10,11... | collective-permute-start | bytes 98312 | tf_op jit(solution)/shard_map/ppermute | solution.py:497
  76.8 18.3 %collective-permute-start.4 = (f32[2048,256]{1,0:T(8,128)S(1)}, f32[2048,256]{1,0:T(8,128)S(1)}, u32[]{:S(2)}, u32[]{:S(2)}) collective-permute-start(f32[2048,256]{1,0:T(8,128)S(1)} %get-tuple-element.32), channel_id=1, source_target_pairs={{0,1},{1,0},{2,3},{3,2},{4,5},{5,4},{6,7},{7,6},{8,9},{9,8},{10,11... | collective-permute-start | bytes 6291464 | tf_op jit(solution)/shard_map/ppermute | solution.py:497
  91.7 3.2 %collective-permute-start.5 = (f32[1024,256]{1,0:T(8,128)S(1)}, f32[1024,256]{1,0:T(8,128)S(1)}, u32[]{:S(2)}, u32[]{:S(2)}) collective-permute-start(f32[1024,256]{1,0:T(8,128)S(1)} %get-tuple-element.37), channel_id=1, source_target_pairs={{0,1},{1,0},{2,3},{3,2},{4,5},{5,4},{6,7},{7,6},{8,9},{9,8},{10,11... | collective-permute-start | bytes 3145736 | tf_op jit(solution)/shard_map/ppermute | solution.py:497
  153.1 5.9 %collective-permute-start.6 = (f16[64,104,128]{2,1,0:T(8,128)(2,1)S(1)}, f16[64,104,128]{2,1,0:T(8,128)(2,1)S(1)}, u32[]{:S(2)}, u32[]{:S(2)}) collective-permute-start(f16[64,104,128]{2,1,0:T(8,128)(2,1)S(1)} %all_to_all.51), channel_id=1, source_target_pairs={{0,1},{1,0},{2,3},{3,2},{4,5},{5,4},{6,7},{7,6},{8,9},{9,8},{10,11... | collective-permute-start | bytes 5111816 | tf_op jit(solution)/shard_map/ppermute | solution.py:497

commit v9 on v7

--- a/solution.py
+++ b/solution.py
@@ -394,69 +394,73 @@
     )(permutation, core, on_chip(normed), on_chip(pre), on_chip(stat), on_chip(w_enc2), on_chip(w_dec1), on_chip(w_dec2))
 
 
-def grad_kernel(perm_ref, core_ref, normed_ref, pre_ref, back_ref, moment_ref, sums_ref, own_ref, send_ref, grads, scale, *, quarter, cols):
-    step = pl.program_id(0)
+def tap_grads(normed_ref, delta_ref, out_ref, taps):
+    pairs = (((3, 2), (1, 1)), ((0, 0), (2, 1)), ((1, 0), (3, 1)), ((2, 0), (0, 3)))
     bins = normed_ref.shape[2]
+    for n, k in enumerate(taps):
+        (f0, d0), (f1, d1) = pairs[k]
+        out_ref[n * bins:(n + 1) * bins, :] = dot_tn(normed_ref[f0], delta_ref[d0]) + dot_tn(normed_ref[f1], delta_ref[d1])
+
+
+def send_grad_kernel(perm_ref, core_ref, normed_ref, pre_ref, back_ref, moment_ref, sums_ref, send_ref, delta_ref, scale, *, quarter, cols):
     ch = pre_ref.shape[2]
-    windows = STEP_WINDOWS
-    rows = windows * quarter
-    normed_ref = step_rows(normed_ref, rows)
-    pre_ref, back_ref = step_rows(pre_ref, rows), step_rows(back_ref, rows)
-    all_windows = windows * pl.num_programs(0)
-
-    @pl.when(step == 0)
-    def _():
-        scale[...] = jnp.sum(sums_ref[...], axis=0) / (2.0 * quarter * cols)
-        grads[...] = jnp.zeros_like(grads)
-
-    pick = functools.partial(window_rows, perm_ref, step=step, windows=windows, quarter=quarter, all_windows=all_windows, cols=cols)
+    windows = pre_ref.shape[1] // quarter
+    scale[...] = jnp.sum(sums_ref[...], axis=0) / (2.0 * quarter * cols)
+    pick = functools.partial(window_rows, perm_ref, step=0, windows=windows, quarter=quarter, all_windows=windows, cols=cols)
     mean = pick(table=moment_ref, first=0, last=ch)
     inverse = pick(table=moment_ref, first=ch, last=2 * ch)
     first = pick(table=scale, first=0, last=ch)
     second = pick(table=scale, first=ch, last=2 * ch)
     hat_e = (pre_ref[0] - mean) * inverse
     hat_o = (pre_ref[1] - mean) * inverse
-    de32 = (back_ref[0] - first - hat_e * second) * inverse
-    do32 = (back_ref[1] - first - hat_o * second) * inverse
-    de = de32.astype(BF16)
-    do = do32.astype(BF16)
-    de_up = shift_up(de32, quarter).astype(BF16)
-    do_down = shift_down(do32, quarter).astype(BF16)
-    f0, f1, f2, f3 = (normed_ref[i] for i in range(4))
-    grads[0:bins, :] += dot_tn(f3, de_up) + dot_tn(f1, do)
-    grads[bins:2 * bins, :] += dot_tn(f0, de) + dot_tn(f2, do)
-    grads[2 * bins:3 * bins, :] += dot_tn(f1, de) + dot_tn(f3, do)
-    grads[3 * bins:4 * bins, :] += dot_tn(f2, de) + dot_tn(f0, do_down)
-
-    @pl.when(step == pl.num_programs(0) - 1)
-    def _():
-        write_halves(core_ref, grads, own_ref, send_ref, (0, 4 * bins))
-
-
-def grad_call(permutation, core, normed, pre, back, moment, sums, quarter, cols):
-    bins = normed.shape[2]
+    even = (back_ref[0] - first - hat_e * second) * inverse
+    odd = (back_ref[1] - first - hat_o * second) * inverse
+    delta_ref[0] = even.astype(BF16)
+    delta_ref[1] = odd.astype(BF16)
+    delta_ref[2] = shift_up(even, quarter).astype(BF16)
+    delta_ref[3] = shift_down(odd, quarter).astype(BF16)
+    core_taps(core_ref, normed_ref, delta_ref, send_ref, ((2, 3), (0, 1)))
+
+
+def own_grad_kernel(core_ref, normed_ref, delta_ref, own_ref):
+    core_taps(core_ref, normed_ref, delta_ref, own_ref, ((0, 1), (2, 3)))
+
+
+def core_taps(core_ref, normed_ref, delta_ref, out_ref, taps):
+    for core in range(2):
+        @pl.when(core_ref[0] == core)
+        def _():
+            tap_grads(normed_ref, delta_ref, out_ref, taps[core])
+
+
+def grad_calls(permutation, core, normed, pre, back, moment, sums, quarter, cols):
+    _, rows, bins = normed.shape
     channels = pre.shape[2]
-    windows = normed.shape[1] // quarter
-    grid_spec = pltpu.PrefetchScalarGridSpec(
-        num_scalar_prefetch=2,
-        grid=(windows // STEP_WINDOWS,),
-        in_specs=[
-            ON_CHIP,
-            ON_CHIP,
-            ON_CHIP,
-            pl.BlockSpec(moment.shape, lambda i, p, c: (0, 0)),
-            ON_CHIP,
-        ],
-        out_specs=[ON_CHIP] * 2,
-        scratch_shapes=[pltpu.VMEM((4 * bins, channels), F32), pltpu.VMEM((windows, 2 * channels), F32)],
-    )
-    return pl.pallas_call(
-        functools.partial(grad_kernel, quarter=quarter, cols=cols),
-        grid_spec=grid_spec,
-        out_shape=[pltpu.VMEM((2 * bins, channels), F32)] * 2,
+    windows = rows // quarter
+    half = jax.ShapeDtypeStruct((2 * bins, channels), F32)
+    send, deltas = pl.pallas_call(
+        functools.partial(send_grad_kernel, quarter=quarter, cols=cols),
+        grid_spec=pltpu.PrefetchScalarGridSpec(
+            num_scalar_prefetch=2,
+            grid=(1,),
+            in_specs=[ON_CHIP] * 5,
+            out_specs=[ON_CHIP] * 2,
+            scratch_shapes=[pltpu.VMEM((windows, 2 * channels), F32)],
+        ),
+        out_shape=[pltpu.VMEM(half.shape, F32), pltpu.VMEM((4, rows, channels), BF16)],
         compiler_params=pltpu.CompilerParams(vmem_limit_bytes=16 * MIB),
-        name="grad_enc1",
-    )(permutation, core, on_chip(normed), on_chip(pre), on_chip(back), moment, on_chip(sums))
+        name="send_grad_enc1",
+    )(permutation, core, on_chip(normed), on_chip(pre), on_chip(back), on_chip(moment), on_chip(sums))
+    own = pl.pallas_call(
+        own_grad_kernel,
+        grid_spec=pltpu.PrefetchScalarGridSpec(
+            num_scalar_prefetch=1, grid=(1,), in_specs=[ON_CHIP] * 2, out_specs=ON_CHIP),
+        out_shape=pltpu.VMEM(half.shape, F32),
+        compiler_params=pltpu.CompilerParams(vmem_limit_bytes=12 * MIB),
+        cost_estimate=pl.CostEstimate(flops=8 * rows * bins * channels, bytes_accessed=8 * rows * bins, transcendentals=0),
+        name="own_grad_enc1",
+    )(core, on_chip(normed), on_chip(deltas))
+    return own, send
 
 
 def swap_cores(values):
@@ -531,9 +535,9 @@
     return exchange(copies.reshape(-1, width), axes).reshape(chips, rows, width)
 
 
-def place_kernel(half_ref, blocks_ref, *refs, rows, cut):
+def place_kernel(half_ref, blocks_ref, *refs, rows, cut, start, stop):
     grad_w_ref, grad_v_ref, grad_b_ref, grad_c_ref = refs[-4:]
-    step = pl.program_id(0)
+    step = start + pl.program_id(0)
     channels = grad_w_ref.shape[1]
     late = rows - cut
     group = channels // cut
@@ -545,40 +549,44 @@
             grad_w_ref[i * late:(i + 1) * late, k * LANES:(k + 1) * LANES] = block[cut:rows]
             out_ref[row:row + cut, column + k * LANES:column + (k + 1) * LANES] = block[0:cut]
 
-    @pl.when(step < 2)
-    def _():
-        for i in range(2 * group):
-            copy(grad_c_ref, i, i % group * cut, i // group * channels)
-
-    @pl.when(step == 2)
-    def _():
-        for i in range(2 * group):
-            copy(grad_b_ref, i, i % group * cut, i // group * channels)
-
-    @pl.when(step == 3)
-    def _():
-        for i in range(2 * group):
-            copy(grad_v_ref, i, i * cut, 0)
-
-
-def place_call(half, blocks, rows, cut, channels, bins, earlier=()):
+    if start < 2:
+        @pl.when(step < 2)
+        def _():
+            for i in range(2 * group):
+                copy(grad_c_ref, i, i % group * cut, i // group * channels)
+
+    if stop > 2:
+        @pl.when(step == 2)
+        def _():
+            for i in range(2 * group):
+                copy(grad_b_ref, i, i % group * cut, i // group * channels)
+
+        @pl.when(step == 3)
+        def _():
+            for i in range(2 * group):
+                copy(grad_v_ref, i, i * cut, 0)
+
+
+def place_call(half, blocks, rows, cut, channels, bins, start=0, earlier=()):
     chips, total, _ = blocks.shape
     group = channels // cut
+    stop = start + chips // (2 * group)
+    untouched = pl.BlockSpec(memory_space=pl.ANY)
     late = rows - cut
     grid_spec = pltpu.PrefetchScalarGridSpec(
         num_scalar_prefetch=1,
-        grid=(4,),
+        grid=(stop - start,),
         in_specs=[pl.BlockSpec((2 * group, total, LANES), lambda i, h: (i, 0, 0))]
         + [pl.BlockSpec(memory_space=pl.ANY)] * len(earlier),
         out_specs=[
-            pl.BlockSpec((2 * group * late, channels), lambda i, h: (h[0] * 4 + i, 0)),
-            pl.BlockSpec((2 * channels, channels), lambda i, h: (h[0], 0)),
-            pl.BlockSpec((channels, 2 * channels), lambda i, h: (0, h[0])),
-            pl.BlockSpec((channels, 2 * channels), lambda i, h: (0, h[0] * 2 + jnp.minimum(i, 1))),
+            pl.BlockSpec((2 * group * late, channels), lambda i, h: (h[0] * 4 + start + i, 0)),
+            pl.BlockSpec((2 * channels, channels), lambda i, h: (h[0], 0)) if stop > 2 else untouched,
+            pl.BlockSpec((channels, 2 * channels), lambda i, h: (0, h[0])) if stop > 2 else untouched,
+            pl.BlockSpec((channels, 2 * channels), lambda i, h: (0, h[0] * 2 + jnp.minimum(start + i, 1))) if start < 2 else untouched,
         ],
     )
     return pl.pallas_call(
-        functools.partial(place_kernel, rows=rows, cut=cut),
+        functools.partial(place_kernel, rows=rows, cut=cut, start=start, stop=stop),
         grid_spec=grid_spec,
         out_shape=[
             jax.ShapeDtypeStruct((4 * bins, channels), F32),
@@ -617,13 +625,15 @@
         permutation, core, normed, pre, stat, w_enc2, w_dec1, w_dec2, quarter, cols, total_windows)
     moments, send = lax.optimization_barrier((join_cores(moments, cols // 2, False), send))
     moments = exchange_copies(moments)
-    late = grad_call(permutation, core, normed, pre, back, moment, moments, quarter, cols)
+    late = grad_calls(permutation, core, normed, pre, back, moment, moments, quarter, cols)
     piece = owner_call(chip_sums([(own, send), late], chip_axes, chips))
     mine = gather_rows(piece, chip_axes, chips)
-    other = swap_cores(mine)
     rows, cut = own.shape[0] // chips + late[0].shape[0] // chips, own.shape[0] // chips
+    others = [swap_cores(mine[0:chips // 2]), swap_cores(mine[chips // 2:])]
     placed = place_call(core, mine.astype(F32), rows, cut, channels, bins)
-    return tuple(place_call(1 - core, other.astype(F32), rows, cut, channels, bins, placed))
+    for n, other in enumerate(others):
+        placed = place_call(1 - core, other.astype(F32), rows, cut, channels, bins, 2 * n, placed)
+    return tuple(placed)
 
 
 def solution(mesh):

time: 158 us -> 159 us (level)
  waiting for transfers between devices: 4.57 us -> 2.72 us
    ppermute x5 -> x6, waiting for transfers between devices: 4.57 us -> 2.72 us  [swap_cores(): return lax.ppermute(values, 'core', [(0, 1), (1, 0)])]
    pallas_call x3 -> x5, Pallas kernels: 8.09 us -> 9.62 us  [the longest x3 4.97 us: place_call(): pl.pallas_call(functools.partial(place_kernel, rows=rows, cut=cut, start=...]
    ppermute x5 -> x6, starting transfers between devices: 5.92 us -> 6.1 us  [swap_cores(): return lax.ppermute(values, 'core', [(0, 1), (1, 0)])]
  transfers between devices with their start and end apart: 5 -> 6, of which waited for: 4 -> 3; matrix products, arithmetic and copies ran while one was open for 0% -> 0% of each run, Pallas kernels for 4% -> 5%
where the time goes in v9:
time: 159 us; the launch traced here: 158 us
  blocking collectives  115 us (72%)
  Pallas kernels  32.2 us (20%)
  starting transfers between devices  6.1 us (4%)
  waiting for transfers between devices  2.72 us (2%)
    all_to_all x6, blocking collectives, exchange(): return lax.all_to_all(values, axes, split_axis=0, concat_axis=0, tiled=True)  115 us
    pallas_call x1, Pallas kernels, middle_call(): pl.pallas_call(functools.partial(middle_kernel, quarter=quarter, cols=col...  12.8 us
    ppermute x6, starting transfers between devices, swap_cores(): return lax.ppermute(values, 'core', [(0, 1), (1, 0)])  6.1 us
    pallas_call x3, Pallas kernels, place_call(): pl.pallas_call(functools.partial(place_kernel, rows=rows, cut=cut, start=...  4.97 us
    pallas_call x1, Pallas kernels, sums_call(): pl.pallas_call(functools.partial(sums_kernel, chunks=chunks, count=window...  4.93 us
    pallas_call x1, Pallas kernels, enc1_call(): pl.pallas_call(functools.partial(enc1_kernel, cols=cols), grid_spec=grid_...  3.41 us
    pallas_call x1, Pallas kernels, grad_calls(): pl.pallas_call(functools.partial(send_grad_kernel, quarter=quarter, cols=...  3.35 us
  transfers between devices with their start and end apart: 6, of which 3 were waited for; matrix products, arithmetic and copies ran while one was open for 0% of the time, Pallas kernels for 5%

profile of v9, /device:TPU:1, one launch (start us, length us, event | category | flops | bytes accessed | tf_op | source)
XLA Modules:
  0.0 158.2 jit_solution(18147577739916002971)
XLA Ops:
  0.7 4.9 %log_and_sum.1 = (f32[16,4,256,128]{3,2,1,0:T(8,128)S(1)}, f32[256,128]{1,0:T(8,128)S(1)}) custom-call(s32[16]{0:T(128)} %bitcast.16, bf16[16,256,512]{2,1,0:T(8,128)(2,1)} %spec_ref.1), custom_call_target="tpu_custom_call" | custom-call | tf_op jit(solution)/shard_map/log_and_sum/pallas_call | solution.py:120
  5.6 21.6 %all_to_all.46 = f32[128,2,128]{2,1,0:T(2,128)S(1)} all-to-all(f32[128,2,128]{2,1,0:T(2,128)S(1)} %bitcast.13), channel_id=1, replica_groups=mesh['row'=8,'pair'=8,'core'=2] {'row','pair','core'}, dimensions={0} | all-to-all | bytes 262144 | tf_op jit(solution)/shard_map/all_to_all | solution.py:471
  27.2 1.1 sensor_stats.1
  28.2 13.6 %all_to_all.47 = f32[128,1,128]{2,1,0:T(1,128)S(1)} all-to-all(f32[128,1,128]{2,1,0:T(1,128)S(1)} %bitcast.12), channel_id=1, replica_groups=mesh['row'=8,'pair'=8,'core'=2] {'row','pair','core'}, dimensions={0} | all-to-all | bytes 131072 | tf_op jit(solution)/shard_map/all_to_all | solution.py:471
  41.9 3.4 %normalize_enc1.1 = (bf16[4,1024,512]{2,1,0:T(8,128)(2,1)S(1)}, f32[2,1024,256]{2,1,0:T(8,128)S(1)}, f32[16,512]{1,0:T(8,128)S(1)}) custom-call(s32[16]{0:T(128)S(1)} %copy-done.4, f32[16,4,256,128]{3,2,1,0:T(8,128)S(1)} %get-tuple-element.30.log_ref, f32[128,128]{1,0:T(8,128)S(1)} %bitcast.11, bf16[2048,256]{1,0:T(8,128)(2,1)S(1)} %copy-done), custom_call_target="tpu_custom_call" | custom-call | tf_op jit(solution)/shard_map/normalize_enc1/pallas_call | solution.py:214
  45.3 0.7 collective-permute-start
  46.0 0.9 collective-permute-done.other_ref
  46.9 11.2 %all_to_all.48.stat_ref = f32[8,16,512]{2,1,0:T(8,128)S(1)} all-to-all(f32[8,16,512]{2,1,0:T(8,128)S(1)} %join_cores.2), channel_id=1, replica_groups=mesh['row'=8,'pair'=8,'core'=2] {'pair'}, dimensions={0} | all-to-all | bytes 524288 | tf_op jit(solution)/shard_map/all_to_all | solution.py:471
  58.1 12.8 %middle.1 = (f32[2048,256]{1,0:T(8,128)S(1)}, f32[2048,256]{1,0:T(8,128)S(1)}, f32[2,1024,256]{2,1,0:T(8,128)S(1)}, f32[16,512]{1,0:T(8,128)S(1)}, f32[16,512]{1,0:T(8,128)S(1)}) custom-call(s32[16]{0:T(128)S(1)} %copy-done.4, s32[1]{0:T(128)} %bitcast.1.core_ref.half_ref, bf16[4,1024,512]{2,1,0:T(8,128)(2,1)S(1)} %get-tuple-element.32.normed_ref, ...), custom_call_target="tpu_custom_call" | custom-call | tf_op jit(solution)/shard_map/middle/pallas_call | solution.py:382
  70.9 1.3 collective-permute-start.1
  72.2 0.9 collective-permute-done.1.other_ref
  73.1 0.4 collective-permute-start.2
  73.5 11.3 %all_to_all.49.sums_ref = f32[8,16,512]{2,1,0:T(8,128)S(1)} all-to-all(f32[8,16,512]{2,1,0:T(8,128)S(1)} %join_cores.3), channel_id=1, replica_groups=mesh['row'=8,'pair'=8,'core'=2] {'pair'}, dimensions={0} | all-to-all | bytes 524288 | tf_op jit(solution)/shard_map/all_to_all | solution.py:471
  84.8 3.4 %send_grad_enc1.1 = (f32[1024,256]{1,0:T(8,128)S(1)}, bf16[4,1024,256]{2,1,0:T(8,128)(2,1)S(1)}) custom-call(s32[16]{0:T(128)S(1)} %copy-done.4, s32[1]{0:T(128)} %bitcast.1.core_ref.half_ref, bf16[4,1024,512]{2,1,0:T(8,128)(2,1)S(1)} %get-tuple-element.32.normed_ref, f32[2,1024,256]{2,1,0:T(8,128)S(1)} %get-tuple-element.33.pre_ref, ...), custom_call_target="tpu_custom_call" | custom-call | tf_op jit(solution)/shard_map/send_grad_enc1/pallas_call | solution.py:441
  88.2 0.9 collective-permute-start.3
  89.1 1.3 own_grad_enc1.1
  90.4 1.0 collective-permute-done.3
  91.3 0.2 add_convert_fusion.1
  91.5 0.4 add_convert_fusion
  91.9 0.1 pad_maximum_fusion
  92.0 27.1 %all_to_all.50.in_ref = bf16[64,48,256]{2,1,0:T(8,128)(2,1)S(1)} all-to-all(bf16[64,48,256]{2,1,0:T(8,128)(2,1)S(1)} %pad_maximum_fusion), channel_id=1, replica_groups=mesh['row'=8,'pair'=8,'core'=2] {'row','pair'}, dimensions={0} | all-to-all | bytes 3145728 | tf_op jit(solution)/shard_map/all_to_all | solution.py:471
  119.2 0.4 owner_sum.1
  119.6 0.2 broadcast_in_dim.2
  119.8 29.9 %all_to_all.51 = f16[64,104,128]{2,1,0:T(8,128)(2,1)S(1)} all-to-all(f16[64,104,128]{2,1,0:T(8,128)(2,1)S(1)} %broadcast_in_dim.2), channel_id=1, replica_groups=mesh['row'=8,'pair'=8,'core'=2] {'row','pair'}, dimensions={0} | all-to-all | bytes 3407872 | tf_op jit(solution)/shard_map/all_to_all | solution.py:471
  149.6 0.3 fusion
  150.0 2.7 %collective-permute-start.5 = (f16[32,104,128]{2,1,0:T(8,128)(2,1)S(1)}, f16[32,104,128]{2,1,0:T(8,128)(2,1)S(1)}, u32[]{:S(2)}, u32[]{:S(2)}) collective-permute-start(f16[32,104,128]{2,1,0:T(8,128)(2,1)S(1)} %get-tuple-element.52), channel_id=1, source_target_pairs={{0,1},{1,0},{2,3},{3,2},{4,5},{5,4},{6,7},{7,6},{8,9},{9,8},{10,11... | collective-permute-start | bytes 2555912 | tf_op jit(solution)/shard_map/ppermute | solution.py:467
  152.8 0.2 convert_element_type.23.blocks_ref
  153.0 2.4 %place_gradients.3 = (f32[2048,256]{1,0:T(8,128)}, f32[1024,256]{1,0:T(8,128)}, f32[256,1024]{1,0:T(8,128)}, f32[256,2048]{1,0:T(8,128)}) custom-call(s32[1]{0:T(128)} %bitcast.1.core_ref.half_ref, f32[64,104,128]{2,1,0:T(8,128)S(1)} %convert_element_type.23.blocks_ref), custom_call_target="tpu_custom_call" | custom-call | flops 851968 | bytes 6815744 | tf_op jit(solution)/shard_map/place_gradients/pallas_call | solution.py:588
  155.4 0.1 convert_element_type.22.blocks_ref
  155.6 1.3 place_gradients.4
  156.8 0.1 convert_element_type.21.blocks_ref
  156.9 1.3 place_gradients.5
  (17 shorter events, 0.2 us)
Async XLA Ops:
  0.6 41.3 %copy-start = (bf16[2048,256]{1,0:T(8,128)(2,1)S(1)}, bf16[2048,256]{1,0:T(8,128)(2,1)}, u32[]{:S(2)}) copy-start(bf16[2048,256]{1,0:T(8,128)(2,1)} %w_ref.1) | copy-start | bytes 3145732
  0.6 41.2 %copy-start.4 = (s32[16]{0:T(128)S(1)}, s32[16]{0:T(128)}, u32[]{:S(2)}) copy-start(s32[16]{0:T(128)} %perm_ref.5) | copy-start | bytes 196
  41.9 16.2 %copy-start.1 = (bf16[256,2048]{1,0:T(8,128)(2,1)S(1)}, bf16[256,2048]{1,0:T(8,128)(2,1)}, u32[]{:S(2)}) copy-start(bf16[256,2048]{1,0:T(8,128)(2,1)} %c_ref.1) | copy-start | bytes 3145732
  41.9 16.2 %copy-start.2 = (bf16[1024,256]{1,0:T(8,128)(2,1)S(1)}, bf16[1024,256]{1,0:T(8,128)(2,1)}, u32[]{:S(2)}) copy-start(bf16[1024,256]{1,0:T(8,128)(2,1)} %v_ref.1) | copy-start | bytes 1572868
  41.9 16.2 %copy-start.3 = (bf16[256,1024]{1,0:T(8,128)(2,1)S(1)}, bf16[256,1024]{1,0:T(8,128)(2,1)}, u32[]{:S(2)}) copy-start(bf16[256,1024]{1,0:T(8,128)(2,1)} %b_ref.1) | copy-start | bytes 1572868
  45.3 1.6 collective-permute-start
  70.9 2.1 %collective-permute-start.1 = (f32[16,512]{1,0:T(8,128)S(1)}, f32[16,512]{1,0:T(8,128)S(1)}, u32[]{:S(2)}, u32[]{:S(2)}) collective-permute-start(f32[16,512]{1,0:T(8,128)S(1)} %get-tuple-element.36.mine_ref), channel_id=1, source_target_pairs={{0,1},{1,0},{2,3},{3,2},{4,5},{5,4},{6,7},{7,6},{8,9},{9,8},{10,11... | collective-permute-start | bytes 98312 | tf_op jit(solution)/shard_map/ppermute | solution.py:467
  73.1 18.5 %collective-permute-start.2 = (f32[2048,256]{1,0:T(8,128)S(1)}, f32[2048,256]{1,0:T(8,128)S(1)}, u32[]{:S(2)}, u32[]{:S(2)}) collective-permute-start(f32[2048,256]{1,0:T(8,128)S(1)} %get-tuple-element.38), channel_id=1, source_target_pairs={{0,1},{1,0},{2,3},{3,2},{4,5},{5,4},{6,7},{7,6},{8,9},{9,8},{10,11... | collective-permute-start | bytes 6291464 | tf_op jit(solution)/shard_map/ppermute | solution.py:467
  88.2 3.2 %collective-permute-start.3 = (f32[1024,256]{1,0:T(8,128)S(1)}, f32[1024,256]{1,0:T(8,128)S(1)}, u32[]{:S(2)}, u32[]{:S(2)}) collective-permute-start(f32[1024,256]{1,0:T(8,128)S(1)} %get-tuple-element.43), channel_id=1, source_target_pairs={{0,1},{1,0},{2,3},{3,2},{4,5},{5,4},{6,7},{7,6},{8,9},{9,8},{10,11... | collective-permute-start | bytes 3145736 | tf_op jit(solution)/shard_map/ppermute | solution.py:467
  150.0 5.5 %collective-permute-start.5 = (f16[32,104,128]{2,1,0:T(8,128)(2,1)S(1)}, f16[32,104,128]{2,1,0:T(8,128)(2,1)S(1)}, u32[]{:S(2)}, u32[]{:S(2)}) collective-permute-start(f16[32,104,128]{2,1,0:T(8,128)(2,1)S(1)} %get-tuple-element.52), channel_id=1, source_target_pairs={{0,1},{1,0},{2,3},{3,2},{4,5},{5,4},{6,7},{7,6},{8,9},{9,8},{10,11... | collective-permute-start | bytes 2555912 | tf_op jit(solution)/shard_map/ppermute | solution.py:467
  152.7 4.1 %collective-permute-start.4 = (f16[32,104,128]{2,1,0:T(8,128)(2,1)S(1)}, f16[32,104,128]{2,1,0:T(8,128)(2,1)S(1)}, u32[]{:S(2)}, u32[]{:S(2)}) collective-permute-start(f16[32,104,128]{2,1,0:T(8,128)(2,1)S(1)} %get-tuple-element.53), channel_id=1, source_target_pairs={{0,1},{1,0},{2,3},{3,2},{4,5},{5,4},{6,7},{7,6},{8,9},{9,8},{10,11... | collective-permute-start | bytes 2555912 | tf_op jit(solution)/shard_map/ppermute | solution.py:467

commit v10 on v7

--- a/solution.py
+++ b/solution.py
@@ -54,7 +54,7 @@
 
 
 def sigmoid(values):
-    return 1.0 / (1.0 + jnp.exp(-values))
+    return 0.5 + 0.5 * jnp.tanh(0.5 * values)
 
 
 def shift_down(values, period):
@@ -90,7 +90,7 @@
             return (total + value[0:8] + value[8:16], square + value_sq[0:8] + value_sq[8:16])
 
         zero = jnp.zeros((8, bins), F32)
-        total, square = lax.fori_loop(0, frames // rows, body, (zero, zero), unroll=4)
+        total, square = lax.fori_loop(0, frames // rows, body, (zero, zero), unroll=8)
         total = jnp.sum(total, axis=0, keepdims=True)
         square = jnp.sum(square, axis=0, keepdims=True)
         pieces = [total[:, k * LANES:(k + 1) * LANES] for k in range(chunks)]

time: 158 us -> 158 us (level)
  no operation moved by 1% of the time
where the time goes in v10:
time: 158 us
  blocking collectives  115 us (73%)
  Pallas kernels  30.4 us (19%)
  starting transfers between devices  5.92 us (4%)
  waiting for transfers between devices  4.57 us (3%)
    all_to_all x6, blocking collectives, exchange(): return lax.all_to_all(values, axes, split_axis=0, concat_axis=0, tiled=True)  115 us
    pallas_call x1, Pallas kernels, middle_call(): pl.pallas_call(functools.partial(middle_kernel, quarter=quarter, cols=col...  12.6 us
    ppermute x5, starting transfers between devices, swap_cores(): return lax.ppermute(values, 'core', [(0, 1), (1, 0)])  5.92 us
    pallas_call x2, Pallas kernels, place_call(): pl.pallas_call(functools.partial(place_kernel, rows=rows, cut=cut), grid_...  4.88 us
    pallas_call x1, Pallas kernels, sums_call(): pl.pallas_call(functools.partial(sums_kernel, chunks=chunks, count=window...  4.79 us
    ppermute x5, waiting for transfers between devices, swap_cores(): return lax.ppermute(values, 'core', [(0, 1), (1, 0)])  4.57 us
    pallas_call x1, Pallas kernels, enc1_call(): pl.pallas_call(functools.partial(enc1_kernel, cols=cols), grid_spec=grid_...  3.41 us
    pallas_call x1, Pallas kernels, grad_call(): pl.pallas_call(functools.partial(grad_kernel, quarter=quarter, cols=cols)...  3.22 us
  transfers between devices with their start and end apart: 5, of which 4 were waited for; matrix products, arithmetic and copies ran while one was open for 0% of the time, Pallas kernels for 4%

profile of v10, /device:TPU:1, one launch (start us, length us, event | category | flops | bytes accessed | tf_op | source)
XLA Modules:
  0.0 157.7 jit_solution(7059243626967101820)
XLA Ops:
  0.7 4.8 %log_and_sum.1 = (f32[16,4,256,128]{3,2,1,0:T(8,128)S(1)}, f32[256,128]{1,0:T(8,128)S(1)}) custom-call(s32[16]{0:T(128)} %bitcast.16, bf16[16,256,512]{2,1,0:T(8,128)(2,1)} %spec_ref.1), custom_call_target="tpu_custom_call" | custom-call | tf_op jit(solution)/shard_map/log_and_sum/pallas_call | solution.py:120
  5.5 21.6 %all_to_all.46 = f32[128,2,128]{2,1,0:T(2,128)S(1)} all-to-all(f32[128,2,128]{2,1,0:T(2,128)S(1)} %bitcast.13), channel_id=1, replica_groups=mesh['row'=8,'pair'=8,'core'=2] {'row','pair','core'}, dimensions={0} | all-to-all | bytes 262144 | tf_op jit(solution)/shard_map/all_to_all | solution.py:467
  27.0 1.1 sensor_stats.1
  28.1 13.6 %all_to_all.47 = f32[128,1,128]{2,1,0:T(1,128)S(1)} all-to-all(f32[128,1,128]{2,1,0:T(1,128)S(1)} %bitcast.12), channel_id=1, replica_groups=mesh['row'=8,'pair'=8,'core'=2] {'row','pair','core'}, dimensions={0} | all-to-all | bytes 131072 | tf_op jit(solution)/shard_map/all_to_all | solution.py:467
  41.8 0.0 copy-start.3
  41.8 3.4 %normalize_enc1.1 = (bf16[4,1024,512]{2,1,0:T(8,128)(2,1)S(1)}, f32[2,1024,256]{2,1,0:T(8,128)S(1)}, f32[16,512]{1,0:T(8,128)S(1)}) custom-call(s32[16]{0:T(128)S(1)} %copy-done.4, f32[16,4,256,128]{3,2,1,0:T(8,128)S(1)} %get-tuple-element.26.log_ref, f32[128,128]{1,0:T(8,128)S(1)} %bitcast.11, bf16[2048,256]{1,0:T(8,128)(2,1)S(1)} %copy-done), custom_call_target="tpu_custom_call" | custom-call | tf_op jit(solution)/shard_map/normalize_enc1/pallas_call | solution.py:214
  45.2 0.7 collective-permute-start
  45.9 0.9 collective-permute-done.other_ref
  46.8 11.2 %all_to_all.48.stat_ref = f32[8,16,512]{2,1,0:T(8,128)S(1)} all-to-all(f32[8,16,512]{2,1,0:T(8,128)S(1)} %join_cores.2), channel_id=1, replica_groups=mesh['row'=8,'pair'=8,'core'=2] {'pair'}, dimensions={0} | all-to-all | bytes 524288 | tf_op jit(solution)/shard_map/all_to_all | solution.py:467
  57.9 0.0 copy-done.1
  57.9 12.6 %middle.1 = (f32[2048,256]{1,0:T(8,128)S(1)}, f32[2048,256]{1,0:T(8,128)S(1)}, f32[2,1024,256]{2,1,0:T(8,128)S(1)}, f32[16,512]{1,0:T(8,128)S(1)}, f32[16,512]{1,0:T(8,128)S(1)}) custom-call(s32[16]{0:T(128)S(1)} %copy-done.4, s32[1]{0:T(128)} %bitcast.1.core_ref.half_ref, bf16[4,1024,512]{2,1,0:T(8,128)(2,1)S(1)} %get-tuple-element.28.normed_ref, ...), custom_call_target="tpu_custom_call" | custom-call | tf_op jit(solution)/shard_map/middle/pallas_call | solution.py:382
  70.6 1.3 collective-permute-start.1
  71.8 0.9 collective-permute-done.1.other_ref
  72.7 0.4 collective-permute-start.2
  73.2 11.3 %all_to_all.49.sums_ref = f32[8,16,512]{2,1,0:T(8,128)S(1)} all-to-all(f32[8,16,512]{2,1,0:T(8,128)S(1)} %join_cores.3), channel_id=1, replica_groups=mesh['row'=8,'pair'=8,'core'=2] {'pair'}, dimensions={0} | all-to-all | bytes 524288 | tf_op jit(solution)/shard_map/all_to_all | solution.py:467
  84.5 3.2 %grad_enc1.1 = (f32[1024,256]{1,0:T(8,128)S(1)}, f32[1024,256]{1,0:T(8,128)S(1)}) custom-call(s32[16]{0:T(128)S(1)} %copy-done.4, s32[1]{0:T(128)} %bitcast.1.core_ref.half_ref, bf16[4,1024,512]{2,1,0:T(8,128)(2,1)S(1)} %get-tuple-element.28.normed_ref, f32[2,1024,256]{2,1,0:T(8,128)S(1)} %get-tuple-element.29.pre_ref, ...), custom_call_target="tpu_custom_call" | custom-call | tf_op jit(solution)/shard_map/grad_enc1/pallas_call | solution.py:453
  87.7 0.9 collective-permute-start.3
  88.6 2.3 %collective-permute-done.3 = f32[1024,256]{1,0:T(8,128)S(1)} collective-permute-done((f32[1024,256]{1,0:T(8,128)S(1)}, f32[1024,256]{1,0:T(8,128)S(1)}, u32[]{:S(2)}, u32[]{:S(2)}) %collective-permute-start.3) | collective-permute-done | bytes 1048608 | tf_op jit(solution)/shard_map/ppermute | solution.py:463
  90.9 0.2 add_convert_fusion.1
  91.1 0.0 collective-permute-done.2
  91.1 0.4 add_convert_fusion
  91.5 0.1 pad_maximum_fusion
  91.6 27.1 %all_to_all.50.in_ref = bf16[64,48,256]{2,1,0:T(8,128)(2,1)S(1)} all-to-all(bf16[64,48,256]{2,1,0:T(8,128)(2,1)S(1)} %pad_maximum_fusion), channel_id=1, replica_groups=mesh['row'=8,'pair'=8,'core'=2] {'row','pair'}, dimensions={0} | all-to-all | bytes 3145728 | tf_op jit(solution)/shard_map/all_to_all | solution.py:467
  118.7 0.4 owner_sum.1
  119.1 0.2 broadcast_in_dim.2
  119.3 29.9 %all_to_all.51 = f16[64,104,128]{2,1,0:T(8,128)(2,1)S(1)} all-to-all(f16[64,104,128]{2,1,0:T(8,128)(2,1)S(1)} %broadcast_in_dim.2), channel_id=1, replica_groups=mesh['row'=8,'pair'=8,'core'=2] {'row','pair'}, dimensions={0} | all-to-all | bytes 3407872 | tf_op jit(solution)/shard_map/all_to_all | solution.py:467
  149.2 2.6 %collective-permute-start.4 = (f16[64,104,128]{2,1,0:T(8,128)(2,1)S(1)}, f16[64,104,128]{2,1,0:T(8,128)(2,1)S(1)}, u32[]{:S(2)}, u32[]{:S(2)}) collective-permute-start(f16[64,104,128]{2,1,0:T(8,128)(2,1)S(1)} %all_to_all.51), channel_id=1, source_target_pairs={{0,1},{1,0},{2,3},{3,2},{4,5},{5,4},{6,7},{7,6},{8,9},{9,8},{10,11... | collective-permute-start | bytes 5111816 | tf_op jit(solution)/shard_map/ppermute | solution.py:463
  151.8 0.2 convert_element_type.19.blocks_ref
  152.0 2.4 %place_gradients.2 = (f32[2048,256]{1,0:T(8,128)}, f32[1024,256]{1,0:T(8,128)}, f32[256,1024]{1,0:T(8,128)}, f32[256,2048]{1,0:T(8,128)}) custom-call(s32[1]{0:T(128)} %bitcast.1.core_ref.half_ref, f32[64,104,128]{2,1,0:T(8,128)S(1)} %convert_element_type.19.blocks_ref), custom_call_target="tpu_custom_call" | custom-call | flops 851968 | bytes 6815744 | tf_op jit(solution)/shard_map/place_gradients/pallas_call | solution.py:580
  154.5 0.6 collective-permute-done.4
  155.0 0.2 convert_element_type.18.blocks_ref
  155.3 2.4 %place_gradients.3 = (f32[2048,256]{1,0:T(8,128)}, f32[1024,256]{1,0:T(8,128)}, f32[256,1024]{1,0:T(8,128)}, f32[256,2048]{1,0:T(8,128)}) custom-call(s32[1]{0:T(128)S(6)} %sub.3.half_ref, f32[64,104,128]{2,1,0:T(8,128)S(1)} %convert_element_type.18.blocks_ref, ...), custom_call_target="tpu_custom_call", output_to_operand_aliasing={{0}: (2, {}), {1}: (3, {}), {2}: (4, {}), {3}: (5, {})} | custom-call | flops 851968 | bytes 6815744 | tf_op jit(solution)/shard_map/place_gradients/pallas_call | solution.py:580
  (11 shorter events, 0.1 us)
Async XLA Ops:
  0.6 41.1 %copy-start = (bf16[2048,256]{1,0:T(8,128)(2,1)S(1)}, bf16[2048,256]{1,0:T(8,128)(2,1)}, u32[]{:S(2)}) copy-start(bf16[2048,256]{1,0:T(8,128)(2,1)} %w_ref.1) | copy-start | bytes 3145732
  0.6 41.1 %copy-start.4 = (s32[16]{0:T(128)S(1)}, s32[16]{0:T(128)}, u32[]{:S(2)}) copy-start(s32[16]{0:T(128)} %perm_ref.5) | copy-start | bytes 196
  41.8 16.2 %copy-start.1 = (bf16[256,2048]{1,0:T(8,128)(2,1)S(1)}, bf16[256,2048]{1,0:T(8,128)(2,1)}, u32[]{:S(2)}) copy-start(bf16[256,2048]{1,0:T(8,128)(2,1)} %c_ref.1) | copy-start | bytes 3145732
  41.8 16.2 %copy-start.2 = (bf16[1024,256]{1,0:T(8,128)(2,1)S(1)}, bf16[1024,256]{1,0:T(8,128)(2,1)}, u32[]{:S(2)}) copy-start(bf16[1024,256]{1,0:T(8,128)(2,1)} %v_ref.1) | copy-start | bytes 1572868
  41.8 16.2 %copy-start.3 = (bf16[256,1024]{1,0:T(8,128)(2,1)S(1)}, bf16[256,1024]{1,0:T(8,128)(2,1)}, u32[]{:S(2)}) copy-start(bf16[256,1024]{1,0:T(8,128)(2,1)} %b_ref.1) | copy-start | bytes 1572868
  45.2 1.6 collective-permute-start
  70.6 2.1 %collective-permute-start.1 = (f32[16,512]{1,0:T(8,128)S(1)}, f32[16,512]{1,0:T(8,128)S(1)}, u32[]{:S(2)}, u32[]{:S(2)}) collective-permute-start(f32[16,512]{1,0:T(8,128)S(1)} %get-tuple-element.32.mine_ref), channel_id=1, source_target_pairs={{0,1},{1,0},{2,3},{3,2},{4,5},{5,4},{6,7},{7,6},{8,9},{9,8},{10,11... | collective-permute-start | bytes 98312 | tf_op jit(solution)/shard_map/ppermute | solution.py:463
  72.7 18.3 %collective-permute-start.2 = (f32[2048,256]{1,0:T(8,128)S(1)}, f32[2048,256]{1,0:T(8,128)S(1)}, u32[]{:S(2)}, u32[]{:S(2)}) collective-permute-start(f32[2048,256]{1,0:T(8,128)S(1)} %get-tuple-element.34), channel_id=1, source_target_pairs={{0,1},{1,0},{2,3},{3,2},{4,5},{5,4},{6,7},{7,6},{8,9},{9,8},{10,11... | collective-permute-start | bytes 6291464 | tf_op jit(solution)/shard_map/ppermute | solution.py:463
  87.7 3.2 %collective-permute-start.3 = (f32[1024,256]{1,0:T(8,128)S(1)}, f32[1024,256]{1,0:T(8,128)S(1)}, u32[]{:S(2)}, u32[]{:S(2)}) collective-permute-start(f32[1024,256]{1,0:T(8,128)S(1)} %get-tuple-element.39), channel_id=1, source_target_pairs={{0,1},{1,0},{2,3},{3,2},{4,5},{5,4},{6,7},{7,6},{8,9},{9,8},{10,11... | collective-permute-start | bytes 3145736 | tf_op jit(solution)/shard_map/ppermute | solution.py:463
  149.2 5.9 %collective-permute-start.4 = (f16[64,104,128]{2,1,0:T(8,128)(2,1)S(1)}, f16[64,104,128]{2,1,0:T(8,128)(2,1)S(1)}, u32[]{:S(2)}, u32[]{:S(2)}) collective-permute-start(f16[64,104,128]{2,1,0:T(8,128)(2,1)S(1)} %all_to_all.51), channel_id=1, source_target_pairs={{0,1},{1,0},{2,3},{3,2},{4,5},{5,4},{6,7},{7,6},{8,9},{9,8},{10,11... | collective-permute-start | bytes 5111816 | tf_op jit(solution)/shard_map/ppermute | solution.py:463

commit v11 on v10

--- a/solution.py
+++ b/solution.py
@@ -54,7 +54,7 @@
 
 
 def sigmoid(values):
-    return 0.5 + 0.5 * jnp.tanh(0.5 * values)
+    return 1.0 / (1.0 + jnp.exp(-values))
 
 
 def shift_down(values, period):

time: 158 us -> 158 us (level)
  no operation moved by 1% of the time
where the time goes in v11:
time: 158 us
  blocking collectives  115 us (73%)
  Pallas kernels  30.5 us (19%)
  starting transfers between devices  5.93 us (4%)
  waiting for transfers between devices  4.57 us (3%)
    all_to_all x6, blocking collectives, exchange(): return lax.all_to_all(values, axes, split_axis=0, concat_axis=0, tiled=True)  115 us
    pallas_call x1, Pallas kernels, middle_call(): pl.pallas_call(functools.partial(middle_kernel, quarter=quarter, cols=col...  12.8 us
    ppermute x5, starting transfers between devices, swap_cores(): return lax.ppermute(values, 'core', [(0, 1), (1, 0)])  5.93 us
    pallas_call x2, Pallas kernels, place_call(): pl.pallas_call(functools.partial(place_kernel, rows=rows, cut=cut), grid_...  4.88 us
    pallas_call x1, Pallas kernels, sums_call(): pl.pallas_call(functools.partial(sums_kernel, chunks=chunks, count=window...  4.79 us
    ppermute x5, waiting for transfers between devices, swap_cores(): return lax.ppermute(values, 'core', [(0, 1), (1, 0)])  4.57 us
    pallas_call x1, Pallas kernels, enc1_call(): pl.pallas_call(functools.partial(enc1_kernel, cols=cols), grid_spec=grid_...  3.41 us
    pallas_call x1, Pallas kernels, grad_call(): pl.pallas_call(functools.partial(grad_kernel, quarter=quarter, cols=cols)...  3.21 us
  transfers between devices with their start and end apart: 5, of which 4 were waited for; matrix products, arithmetic and copies ran while one was open for 0% of the time, Pallas kernels for 4%

profile of v11, /device:TPU:1, one launch (start us, length us, event | category | flops | bytes accessed | tf_op | source)
XLA Modules:
  0.0 157.9 jit_solution(15345475143075143541)
XLA Ops:
  0.7 4.8 %log_and_sum.1 = (f32[16,4,256,128]{3,2,1,0:T(8,128)S(1)}, f32[256,128]{1,0:T(8,128)S(1)}) custom-call(s32[16]{0:T(128)} %bitcast.16, bf16[16,256,512]{2,1,0:T(8,128)(2,1)} %spec_ref.1), custom_call_target="tpu_custom_call" | custom-call | tf_op jit(solution)/shard_map/log_and_sum/pallas_call | solution.py:120
  5.5 21.6 %all_to_all.46 = f32[128,2,128]{2,1,0:T(2,128)S(1)} all-to-all(f32[128,2,128]{2,1,0:T(2,128)S(1)} %bitcast.13), channel_id=1, replica_groups=mesh['row'=8,'pair'=8,'core'=2] {'row','pair','core'}, dimensions={0} | all-to-all | bytes 262144 | tf_op jit(solution)/shard_map/all_to_all | solution.py:467
  27.0 1.1 sensor_stats.1
  28.1 13.6 %all_to_all.47 = f32[128,1,128]{2,1,0:T(1,128)S(1)} all-to-all(f32[128,1,128]{2,1,0:T(1,128)S(1)} %bitcast.12), channel_id=1, replica_groups=mesh['row'=8,'pair'=8,'core'=2] {'row','pair','core'}, dimensions={0} | all-to-all | bytes 131072 | tf_op jit(solution)/shard_map/all_to_all | solution.py:467
  41.8 0.0 copy-start.3
  41.8 3.4 %normalize_enc1.1 = (bf16[4,1024,512]{2,1,0:T(8,128)(2,1)S(1)}, f32[2,1024,256]{2,1,0:T(8,128)S(1)}, f32[16,512]{1,0:T(8,128)S(1)}) custom-call(s32[16]{0:T(128)S(1)} %copy-done.4, f32[16,4,256,128]{3,2,1,0:T(8,128)S(1)} %get-tuple-element.26.log_ref, f32[128,128]{1,0:T(8,128)S(1)} %bitcast.11, bf16[2048,256]{1,0:T(8,128)(2,1)S(1)} %copy-done), custom_call_target="tpu_custom_call" | custom-call | tf_op jit(solution)/shard_map/normalize_enc1/pallas_call | solution.py:214
  45.2 0.7 collective-permute-start
  45.9 0.9 collective-permute-done.other_ref
  46.8 11.2 %all_to_all.48.stat_ref = f32[8,16,512]{2,1,0:T(8,128)S(1)} all-to-all(f32[8,16,512]{2,1,0:T(8,128)S(1)} %join_cores.2), channel_id=1, replica_groups=mesh['row'=8,'pair'=8,'core'=2] {'pair'}, dimensions={0} | all-to-all | bytes 524288 | tf_op jit(solution)/shard_map/all_to_all | solution.py:467
  57.9 0.0 copy-done.1
  57.9 12.8 %middle.1 = (f32[2048,256]{1,0:T(8,128)S(1)}, f32[2048,256]{1,0:T(8,128)S(1)}, f32[2,1024,256]{2,1,0:T(8,128)S(1)}, f32[16,512]{1,0:T(8,128)S(1)}, f32[16,512]{1,0:T(8,128)S(1)}) custom-call(s32[16]{0:T(128)S(1)} %copy-done.4, s32[1]{0:T(128)} %bitcast.1.core_ref.half_ref, bf16[4,1024,512]{2,1,0:T(8,128)(2,1)S(1)} %get-tuple-element.28.normed_ref, ...), custom_call_target="tpu_custom_call" | custom-call | tf_op jit(solution)/shard_map/middle/pallas_call | solution.py:382
  70.8 1.3 collective-permute-start.1
  72.0 0.9 collective-permute-done.1.other_ref
  72.9 0.4 collective-permute-start.2
  73.3 11.3 %all_to_all.49.sums_ref = f32[8,16,512]{2,1,0:T(8,128)S(1)} all-to-all(f32[8,16,512]{2,1,0:T(8,128)S(1)} %join_cores.3), channel_id=1, replica_groups=mesh['row'=8,'pair'=8,'core'=2] {'pair'}, dimensions={0} | all-to-all | bytes 524288 | tf_op jit(solution)/shard_map/all_to_all | solution.py:467
  84.7 3.2 %grad_enc1.1 = (f32[1024,256]{1,0:T(8,128)S(1)}, f32[1024,256]{1,0:T(8,128)S(1)}) custom-call(s32[16]{0:T(128)S(1)} %copy-done.4, s32[1]{0:T(128)} %bitcast.1.core_ref.half_ref, bf16[4,1024,512]{2,1,0:T(8,128)(2,1)S(1)} %get-tuple-element.28.normed_ref, f32[2,1024,256]{2,1,0:T(8,128)S(1)} %get-tuple-element.29.pre_ref, ...), custom_call_target="tpu_custom_call" | custom-call | tf_op jit(solution)/shard_map/grad_enc1/pallas_call | solution.py:453
  87.9 0.9 collective-permute-start.3
  88.8 2.3 %collective-permute-done.3 = f32[1024,256]{1,0:T(8,128)S(1)} collective-permute-done((f32[1024,256]{1,0:T(8,128)S(1)}, f32[1024,256]{1,0:T(8,128)S(1)}, u32[]{:S(2)}, u32[]{:S(2)}) %collective-permute-start.3) | collective-permute-done | bytes 1048608 | tf_op jit(solution)/shard_map/ppermute | solution.py:463
  91.1 0.2 add_convert_fusion.1
  91.3 0.0 collective-permute-done.2
  91.3 0.4 add_convert_fusion
  91.7 0.1 pad_maximum_fusion
  91.8 27.1 %all_to_all.50.in_ref = bf16[64,48,256]{2,1,0:T(8,128)(2,1)S(1)} all-to-all(bf16[64,48,256]{2,1,0:T(8,128)(2,1)S(1)} %pad_maximum_fusion), channel_id=1, replica_groups=mesh['row'=8,'pair'=8,'core'=2] {'row','pair'}, dimensions={0} | all-to-all | bytes 3145728 | tf_op jit(solution)/shard_map/all_to_all | solution.py:467
  118.9 0.4 owner_sum.1
  119.3 0.2 broadcast_in_dim.2
  119.5 29.9 %all_to_all.51 = f16[64,104,128]{2,1,0:T(8,128)(2,1)S(1)} all-to-all(f16[64,104,128]{2,1,0:T(8,128)(2,1)S(1)} %broadcast_in_dim.2), channel_id=1, replica_groups=mesh['row'=8,'pair'=8,'core'=2] {'row','pair'}, dimensions={0} | all-to-all | bytes 3407872 | tf_op jit(solution)/shard_map/all_to_all | solution.py:467
  149.4 2.6 %collective-permute-start.4 = (f16[64,104,128]{2,1,0:T(8,128)(2,1)S(1)}, f16[64,104,128]{2,1,0:T(8,128)(2,1)S(1)}, u32[]{:S(2)}, u32[]{:S(2)}) collective-permute-start(f16[64,104,128]{2,1,0:T(8,128)(2,1)S(1)} %all_to_all.51), channel_id=1, source_target_pairs={{0,1},{1,0},{2,3},{3,2},{4,5},{5,4},{6,7},{7,6},{8,9},{9,8},{10,11... | collective-permute-start | bytes 5111816 | tf_op jit(solution)/shard_map/ppermute | solution.py:463
  152.0 0.2 convert_element_type.19.blocks_ref
  152.2 2.4 %place_gradients.2 = (f32[2048,256]{1,0:T(8,128)}, f32[1024,256]{1,0:T(8,128)}, f32[256,1024]{1,0:T(8,128)}, f32[256,2048]{1,0:T(8,128)}) custom-call(s32[1]{0:T(128)} %bitcast.1.core_ref.half_ref, f32[64,104,128]{2,1,0:T(8,128)S(1)} %convert_element_type.19.blocks_ref), custom_call_target="tpu_custom_call" | custom-call | flops 851968 | bytes 6815744 | tf_op jit(solution)/shard_map/place_gradients/pallas_call | solution.py:580
  154.7 0.6 collective-permute-done.4
  155.2 0.2 convert_element_type.18.blocks_ref
  155.5 2.4 %place_gradients.3 = (f32[2048,256]{1,0:T(8,128)}, f32[1024,256]{1,0:T(8,128)}, f32[256,1024]{1,0:T(8,128)}, f32[256,2048]{1,0:T(8,128)}) custom-call(s32[1]{0:T(128)S(6)} %sub.3.half_ref, f32[64,104,128]{2,1,0:T(8,128)S(1)} %convert_element_type.18.blocks_ref, ...), custom_call_target="tpu_custom_call", output_to_operand_aliasing={{0}: (2, {}), {1}: (3, {}), {2}: (4, {}), {3}: (5, {})} | custom-call | flops 851968 | bytes 6815744 | tf_op jit(solution)/shard_map/place_gradients/pallas_call | solution.py:580
  (11 shorter events, 0.1 us)
Async XLA Ops:
  0.6 41.1 %copy-start = (bf16[2048,256]{1,0:T(8,128)(2,1)S(1)}, bf16[2048,256]{1,0:T(8,128)(2,1)}, u32[]{:S(2)}) copy-start(bf16[2048,256]{1,0:T(8,128)(2,1)} %w_ref.1) | copy-start | bytes 3145732
  0.6 41.1 %copy-start.4 = (s32[16]{0:T(128)S(1)}, s32[16]{0:T(128)}, u32[]{:S(2)}) copy-start(s32[16]{0:T(128)} %perm_ref.5) | copy-start | bytes 196
  41.8 16.2 %copy-start.1 = (bf16[256,2048]{1,0:T(8,128)(2,1)S(1)}, bf16[256,2048]{1,0:T(8,128)(2,1)}, u32[]{:S(2)}) copy-start(bf16[256,2048]{1,0:T(8,128)(2,1)} %c_ref.1) | copy-start | bytes 3145732
  41.8 16.2 %copy-start.2 = (bf16[1024,256]{1,0:T(8,128)(2,1)S(1)}, bf16[1024,256]{1,0:T(8,128)(2,1)}, u32[]{:S(2)}) copy-start(bf16[1024,256]{1,0:T(8,128)(2,1)} %v_ref.1) | copy-start | bytes 1572868
  41.8 16.2 %copy-start.3 = (bf16[256,1024]{1,0:T(8,128)(2,1)S(1)}, bf16[256,1024]{1,0:T(8,128)(2,1)}, u32[]{:S(2)}) copy-start(bf16[256,1024]{1,0:T(8,128)(2,1)} %b_ref.1) | copy-start | bytes 1572868
  45.2 1.6 collective-permute-start
  70.8 2.1 %collective-permute-start.1 = (f32[16,512]{1,0:T(8,128)S(1)}, f32[16,512]{1,0:T(8,128)S(1)}, u32[]{:S(2)}, u32[]{:S(2)}) collective-permute-start(f32[16,512]{1,0:T(8,128)S(1)} %get-tuple-element.32.mine_ref), channel_id=1, source_target_pairs={{0,1},{1,0},{2,3},{3,2},{4,5},{5,4},{6,7},{7,6},{8,9},{9,8},{10,11... | collective-permute-start | bytes 98312 | tf_op jit(solution)/shard_map/ppermute | solution.py:463
  72.9 18.3 %collective-permute-start.2 = (f32[2048,256]{1,0:T(8,128)S(1)}, f32[2048,256]{1,0:T(8,128)S(1)}, u32[]{:S(2)}, u32[]{:S(2)}) collective-permute-start(f32[2048,256]{1,0:T(8,128)S(1)} %get-tuple-element.34), channel_id=1, source_target_pairs={{0,1},{1,0},{2,3},{3,2},{4,5},{5,4},{6,7},{7,6},{8,9},{9,8},{10,11... | collective-permute-start | bytes 6291464 | tf_op jit(solution)/shard_map/ppermute | solution.py:463
  87.9 3.2 %collective-permute-start.3 = (f32[1024,256]{1,0:T(8,128)S(1)}, f32[1024,256]{1,0:T(8,128)S(1)}, u32[]{:S(2)}, u32[]{:S(2)}) collective-permute-start(f32[1024,256]{1,0:T(8,128)S(1)} %get-tuple-element.39), channel_id=1, source_target_pairs={{0,1},{1,0},{2,3},{3,2},{4,5},{5,4},{6,7},{7,6},{8,9},{9,8},{10,11... | collective-permute-start | bytes 3145736 | tf_op jit(solution)/shard_map/ppermute | solution.py:463
  149.4 5.9 %collective-permute-start.4 = (f16[64,104,128]{2,1,0:T(8,128)(2,1)S(1)}, f16[64,104,128]{2,1,0:T(8,128)(2,1)S(1)}, u32[]{:S(2)}, u32[]{:S(2)}) collective-permute-start(f16[64,104,128]{2,1,0:T(8,128)(2,1)S(1)} %all_to_all.51), channel_id=1, source_target_pairs={{0,1},{1,0},{2,3},{3,2},{4,5},{5,4},{6,7},{7,6},{8,9},{9,8},{10,11... | collective-permute-start | bytes 5111816 | tf_op jit(solution)/shard_map/ppermute | solution.py:463
